TPU v7x, 32 devices: a whole 2x2x4 slice. The times are simulated.
32 devices in a mesh: prow: 4 (over y, x), pcol: 8 (over z, core).
Axes of the slice: x: 2, y: 2, z: 4, core: 2. Of those that a mesh axis runs over, the one named last changes fastest.
Arguments:
- rhs: bfloat16 [3, 8, 512, 128], P(None, 'pcol', 'prow'), may hold values from -6 to 6
- inverse_diagonal_blocks: bfloat16 [3, 8, 512, 512], P(None, 'pcol'), may hold values from -1 to 2, as said below
- offdiagonal_blocks: bfloat16 [2, 8, 4, 512, 512], P(None, 'pcol', 'prow'), may hold values from -0.09375 to 0.09375
- targets: int32 [2, 8, 4], P(None, 'pcol'), may hold values from 0 to 15, as said below
Outputs:
- solution: bfloat16 [3, 8, 512, 128], P(None, 'pcol', 'prow')
Inputs may be any that keep to these rules, and one draw needn't show every extreme that they name: For a supernode of level l the 4 entries of targets[l] are distinct and lie between l * 8 and (2) * 8 - 1, so they name supernodes of later levels only. Each block of inverse_diagonal_blocks is lower triangular.
All inputs are finite; a program needn't handle non-finite values.
Results may differ from a plain program's by a relative error of at most 0.014.
Values may be sent and summed in bfloat16 or wider, within the bound.
No kernel may reach another device: no remote copies, remote signals or barrier semaphores. Data moves between devices by JAX's collectives and lax.ppermute only.
A program may use at most 64 MiB of HBM per device.

v0:
```python
import functools

import jax
import jax.numpy as jnp
from jax import lax
from jax.experimental import pallas as pl
from jax.experimental.pallas import tpu as pltpu
from jax.sharding import PartitionSpec as P


F32 = jnp.float32
BF16 = jnp.bfloat16
NT = (((1,), (1,)), ((), ()))
GRANT = 24 << 20


def pairs(size, step):
    return [(i, i ^ step) for i in range(size)]


def call(kernel, out_shapes, operands, scalars=0, placed=0, scratch=(), flops=0):
    vmem = pl.BlockSpec(memory_space=pltpu.VMEM)
    smem = pl.BlockSpec(memory_space=pltpu.SMEM)
    moved = sum(x.size * x.dtype.itemsize for x in operands)
    return pl.pallas_call(
        kernel,
        out_shape=out_shapes,
        in_specs=[smem] * scalars + [vmem] * (len(operands) - scalars - placed) + [pl.BlockSpec(memory_space=pl.ANY)] * placed,
        out_specs=[vmem] * len(out_shapes),
        scratch_shapes=list(scratch),
        compiler_params=pltpu.CompilerParams(vmem_limit_bytes=GRANT),
        cost_estimate=pl.CostEstimate(flops=flops, bytes_accessed=moved, transcendentals=0),
    )(*operands)


def first_kernel(rows, later, *refs):
    shares = refs[:rows]
    inverse, rhs, off, kept = refs[rows : rows + 4]
    messages = refs[rows + 4 : 2 * rows + 4]
    whole, turned, turned_rest, rest, block, arrived = refs[2 * rows + 4 :]
    block_copy = pltpu.make_async_copy(off.at[0, 0, 0], block, arrived.at[0])
    rest_copy = pltpu.make_async_copy(rhs.at[pl.ds(1, later), 0], rest, arrived.at[1])
    block_copy.start()
    rest_copy.start()
    part, vectors = shares[0].shape
    size = inverse.shape[-1]
    each = vectors // rows
    me = lax.axis_index("prow")
    for step in range(rows):
        whole[pl.ds(pl.multiple_of((me ^ step) * part, part), part), :] = shares[step][...]
    solved = jnp.dot(inverse[...], whole[...], preferred_element_type=F32).astype(BF16)
    whole[...] = solved
    kept[...] = whole[pl.ds(pl.multiple_of(me * part, part), part), :]
    block_copy.wait()
    product = jnp.dot(block[...], solved, preferred_element_type=F32)
    turned[...] = product.T
    rest_copy.wait()
    for level in range(later):
        turned_rest[level] = rest[level].astype(F32).T
    for step in range(rows):
        at = pl.ds(pl.multiple_of((me ^ step) * each, each), each)
        messages[step][:, :size] = turned[at, :].astype(BF16)
        for level in range(later):
            low = size + level * part
            messages[step][:, low : low + part] = turned_rest[level, at, :].astype(BF16)


def slots_kernel(half, level, sources, own_targets, far_targets, *refs):
    own = refs[: len(sources)]
    far = refs[len(sources) : 2 * len(sources)]
    outs = refs[2 * len(sources) :]
    each, size = outs[0].shape
    me_row = lax.axis_index("prow")
    me_col = lax.axis_index("pcol")
    for step in range(half):
        column = (me_col ^ (2 * step)) + level * 2 * half
        total = jnp.zeros((each, size), F32)
        for targets, group in ((own_targets, own), (far_targets, far)):
            for (source, at), ref in zip(sources, group):
                value = ref[at] if ref.ndim == 3 else ref[:, :size]
                hit = targets[source[0], 0, me_row ^ source[1]] == column
                total = total + jnp.where(hit, value.astype(F32), 0.0)
        outs[step][...] = total.astype(outs[step].dtype)


def residual(rows, level, messages, arrived, out):
    each, size = out.shape
    part = size // rows
    me = lax.axis_index("prow")
    total = arrived[0][...].astype(F32)
    for ref in arrived[1:]:
        total = total + ref[...].astype(F32)
    low = size + level * part
    if part % 128 == 0:
        for step in range(rows):
            at = pl.ds(pl.multiple_of((me ^ step) * part, part), part)
            out[:, at] = messages[step][:, low : low + part].astype(F32)
        return out[...] - total
    given = jnp.zeros((each, size), F32)
    for step in range(rows):
        place = lax.broadcasted_iota(jnp.int32, (part, size), 1) - (me ^ step) * part
        chosen = (place == lax.broadcasted_iota(jnp.int32, (part, size), 0)).astype(F32).astype(BF16)
        given = given + jnp.dot(messages[step][:, low : low + part], chosen, preferred_element_type=F32)
    return given - total


def solve(inverse, level, given):
    high = given.astype(BF16)
    low = (given - high.astype(F32)).astype(BF16)
    both = jnp.concatenate([high, low], axis=0)
    wide = lax.dot_general(both, inverse[level, 0], NT, preferred_element_type=F32)
    each = given.shape[0]
    return (wide[:each] + wide[each:]).astype(BF16)


def middle_kernel(rows, half, level, *refs):
    messages = refs[:rows]
    arrived = refs[rows : rows + half]
    inverse = refs[rows + half]
    blocks = refs[rows + half + 1 : 3 * rows + half + 1]
    solved, products, scratch = refs[3 * rows + half + 1 :]
    given = residual(rows, level - 1, messages, arrived, scratch)
    value = solve(inverse, level, given)
    solved[...] = value
    for step in range(rows):
        low = 0
        for piece in blocks[2 * step : 2 * step + 2]:
            high = low + piece.shape[0]
            products[step, :, low:high] = lax.dot_general(value, piece[...], NT, preferred_element_type=F32).astype(BF16)
            low = high


def last_kernel(rows, half, level, before, *refs):
    messages = refs[:rows]
    arrived = refs[rows : rows + half]
    inverse = refs[rows + half]
    earlier = refs[rows + half + 1 : rows + half + 1 + before]
    outs = refs[rows + half + 1 + before : 2 * rows + half + 1 + before]
    scratch = refs[-1]
    _, size = scratch.shape
    part = size // rows
    me = lax.axis_index("prow")
    given = residual(rows, level - 1, messages, arrived, scratch)
    values = [ref[...] for ref in earlier] + [solve(inverse, level, given)]
    for index, value in enumerate(values):
        if part % 128 == 0:
            scratch[...] = value.astype(F32)
            for step in range(rows):
                at = pl.ds(pl.multiple_of((me ^ step) * part, part), part)
                outs[step][index] = scratch[:, at].astype(BF16)
        else:
            for step in range(rows):
                place = lax.broadcasted_iota(jnp.int32, (part, size), 1) - (me ^ step) * part
                chosen = (place == lax.broadcasted_iota(jnp.int32, (part, size), 0)).astype(F32).astype(BF16)
                outs[step][index] = lax.dot_general(value, chosen, NT, preferred_element_type=F32).astype(BF16)


def output_kernel(rows, later, *refs):
    kept = refs[0]
    pieces = refs[1 : rows + 1]
    out, scratch = refs[rows + 1 :]
    _, each, _ = pieces[0].shape
    me = lax.axis_index("prow")
    out[0, 0] = kept[...]
    for level in range(later):
        for step in range(rows):
            at = pl.ds(pl.multiple_of((me ^ step) * each, each), each)
            scratch[at, :] = pieces[step][level].astype(F32)
        out[level + 1, 0] = scratch[...].T.astype(BF16)


def local(rhs, inverse, off, targets):
    levels, _, part, vectors = rhs.shape
    size = inverse.shape[-1]
    rows, columns = lax.axis_size("prow"), lax.axis_size("pcol")
    half = columns // 2
    later = levels - 1
    each = vectors // rows
    shape = jax.ShapeDtypeStruct

    def over_rows(x, step):
        return lax.ppermute(x, "prow", pairs(rows, step)) if step else x

    def over_pairs(x, step):
        return lax.ppermute(x, "pcol", pairs(columns, 2 * step)) if step else x

    def flip(x):
        return lax.ppermute(x, "pcol", pairs(columns, 1))

    far_targets = flip(targets)
    first = rhs[0, 0]
    shares = [over_rows(first, step) for step in range(rows)]
    width = size + later * part
    kept, *sent = call(
        functools.partial(first_kernel, rows, later),
        [shape((part, vectors), BF16)] + [shape((each, width), BF16)] * rows,
        [*shares, inverse[0, 0], rhs, off],
        placed=2,
        scratch=[
            pltpu.VMEM((size, vectors), BF16),
            pltpu.VMEM((vectors, size), F32),
            pltpu.VMEM((later, vectors, part), F32),
            pltpu.VMEM((later, part, vectors), BF16),
            pltpu.VMEM((size, size), BF16),
            pltpu.SemaphoreType.DMA((2,)),
        ],
        flops=4 * size * size * vectors,
    )
    messages = [over_rows(x, step) for step, x in enumerate(sent)]
    far_messages = [flip(x) for x in messages]
    blocks = {}
    for level in range(1, later):
        cut = size // 2
        upper, lower = off[level, 0, 0, :cut], off[level, 0, 0, cut:]
        late_upper, late_lower, _ = lax.optimization_barrier((upper, lower, sent[0]))
        bits = [1 << b for b in range(rows.bit_length() - 1)]
        blocks[level] = [None] * (2 * rows)
        for side, (early, late, order) in enumerate(((upper, late_upper, bits), (lower, late_lower, bits[::-1]))):
            have = {0: early}
            for number, bit in enumerate(order):
                for step in sorted(have):
                    source = have[step]
                    if number:
                        source = late if step == 0 else lax.optimization_barrier((source, sent[0]))[0]
                    blocks[level][2 * (step ^ bit) + side] = over_rows(source, bit)
                have = {step: blocks[level][2 * step + side] if step else early for step in [*have, *(x ^ bit for x in have)]}
            blocks[level][side] = early

    own, far = list(messages), list(far_messages)
    sources = [((0, step), None) for step in range(rows)]
    solved = []
    for level in range(1, levels):
        out = call(
            functools.partial(slots_kernel, half, level - 1, tuple(sources)),
            [shape((each, size), BF16)] * half,
            [targets, far_targets, *own, *far],
            scalars=2,
        )
        arrived = [over_pairs(x, step) for step, x in enumerate(out)]
        if level < later:
            value, products = call(
                functools.partial(middle_kernel, rows, half, level),
                [shape((each, size), BF16), shape((rows, each, size), BF16)],
                [*messages, *arrived, inverse, *blocks[level]],
                scratch=[pltpu.VMEM((each, size), F32)],
                flops=2 * each * size * size * (rows + 1),
            )
            solved.append(value)
            far_products = flip(products)
            own += [products] * rows
            far += [far_products] * rows
            sources += [((level, step), step) for step in range(rows)]
    pieces = call(
        functools.partial(last_kernel, rows, half, later, len(solved)),
        [shape((later, each, part), BF16)] * rows,
        [*messages, *arrived, inverse, *solved],
        scratch=[pltpu.VMEM((each, size), F32)],
        flops=2 * each * size * size,
    )
    pieces = [over_rows(x, step) for step, x in enumerate(pieces)]
    (out,) = call(
        functools.partial(output_kernel, rows, later),
        [shape((levels, 1, part, vectors), BF16)],
        [kept, *pieces],
        scratch=[pltpu.VMEM((vectors, part), F32)],
    )
    return out


def solution(mesh):
    in_specs = (
        P(None, "pcol", "prow", None),
        P(None, "pcol", None, None),
        P(None, "pcol", "prow", None, None),
        P(None, "pcol", None),
    )
    out_specs = P(None, "pcol", "prow", None)

    return jax.shard_map(local, mesh=mesh, in_specs=in_specs, out_specs=out_specs, check_vma=False)
```

profile of v0, /device:TPU:0, one launch (start us, length us, event | category | flops | bytes accessed | tf_op | source)
XLA Modules:
  0.0 62.0 jit_solution(413724671774948469)
XLA Ops:
  0.0 0.9 %slice_bitcast_fusion.3.refs_0_ = bf16[128,128]{1,0:T(8,128)(2,1)S(1)} fusion(bf16[3,1,128,128]{3,2,1,0:T(8,128)(2,1)} %refs_5_.1), kind=kLoop, calls=%fused_computation.3 | loop fusion | bytes 65536 | tf_op jit(solution)/shard_map/squeeze | solution.py:191
  0.9 3.9 %collective-permute-start.2 = (bf16[128,128]{1,0:T(8,128)(2,1)S(1)}, bf16[128,128]{1,0:T(8,128)(2,1)S(1)}, u32[]{:S(2)}, u32[]{:S(2)}) collective-permute-start(bf16[128,128]{1,0:T(8,128)(2,1)S(1)} %slice_bitcast_fusion.3.refs_0_), channel_id=1, source_target_pairs={{0,24},{8,16},{16,8},{24,0},{1,25},{9,17},{17,9},{25,1},{2,26},{10... | collective-permute-start | bytes 98312 | tf_op jit(solution)/shard_map/ppermute | solution.py:182
  4.8 0.5 collective-permute-start.1
  5.3 0.1 collective-permute-start
  5.4 1.1 %slice_bitcast_fusion.1 = (bf16[256,512]{1,0:T(8,128)(2,1)S(1)}, bf16[256,512]{1,0:T(8,128)(2,1)S(1)}) fusion(bf16[2,1,1,512,512]{4,3,2,1,0:T(8,128)(2,1)} %refs_6_.1), kind=kLoop, calls=%fused_computation.1 | loop fusion | bytes 1048576 | tf_op jit(solution)/shard_map/squeeze | solution.py:214
  6.4 0.0 copy-start.3
  6.4 2.1 %collective-permute-start.17 = (bf16[256,512]{1,0:T(8,128)(2,1)S(1)}, bf16[256,512]{1,0:T(8,128)(2,1)S(1)}, u32[]{:S(2)}, u32[]{:S(2)}) collective-permute-start(bf16[256,512]{1,0:T(8,128)(2,1)S(1)} %get-tuple-element.37.refs_10_), channel_id=1, source_target_pairs={{0,16},{8,24},{16,0},{24,8},{1,17},{9,25},{17,1},{25,9},{2,18},{10... | collective-permute-start | bytes 786440 | tf_op jit(solution)/shard_map/ppermute | solution.py:182
  8.5 1.5 %collective-permute-start.14 = (bf16[256,512]{1,0:T(8,128)(2,1)S(1)}, bf16[256,512]{1,0:T(8,128)(2,1)S(1)}, u32[]{:S(2)}, u32[]{:S(2)}) collective-permute-start(bf16[256,512]{1,0:T(8,128)(2,1)S(1)} %get-tuple-element.38.refs_9_), channel_id=1, source_target_pairs={{0,8},{8,0},{16,24},{24,16},{1,9},{9,1},{17,25},{25,17},{2,10},{10... | collective-permute-start | bytes 786440 | tf_op jit(solution)/shard_map/ppermute | solution.py:182
  10.0 1.1 %slice_bitcast_fusion.refs_4_ = bf16[512,512]{1,0:T(8,128)(2,1)S(1)} fusion(bf16[3,1,512,512]{3,2,1,0:T(8,128)(2,1)} %refs_8_.3), kind=kLoop, calls=%fused_computation | loop fusion | bytes 1048576 | tf_op jit(solution)/shard_map/squeeze | solution.py:197
  11.1 0.0 collective-permute-done.2.refs_3_
  11.1 0.0 collective-permute-done.1.refs_2_
  11.1 0.0 collective-permute-done.refs_1_
  11.1 1.2 %shard_map.46 = (bf16[128,128]{1,0:T(8,128)(2,1)S(1)}, bf16[32,768]{1,0:T(8,128)(2,1)S(1)}, bf16[32,768]{1,0:T(8,128)(2,1)S(1)}, bf16[32,768]{1,0:T(8,128)(2,1)S(1)}, bf16[32,768]{1,0:T(8,128)(2,1)S(1)}) custom-call(bf16[128,128]{1,0:T(8,128)(2,1)S(1)} %slice_bitcast_fusion.3.refs_0_, bf16[128,128]{1,0:T(8,128)(2,1)S(1)} %collective-permute-done.refs_1_, ...), custom_call_target="tpu_custom_call" | custom-call | flops 134217728 | bytes 1802240 | tf_op jit(solution)/shard_map/pallas_call | solution.py:25
  12.3 0.6 collective-permute-start.3
  12.9 0.2 collective-permute-start.4
  13.1 2.7 %collective-permute-start.5 = (bf16[32,768]{1,0:T(8,128)(2,1)S(1)}, bf16[32,768]{1,0:T(8,128)(2,1)S(1)}, u32[]{:S(2)}, u32[]{:S(2)}) collective-permute-start(bf16[32,768]{1,0:T(8,128)(2,1)S(1)} %get-tuple-element.32), channel_id=1, source_target_pairs={{0,24},{8,16},{16,8},{24,0},{1,25},{9,17},{17,9},{25,1},{2,26},{10... | collective-permute-start | bytes 147464 | tf_op jit(solution)/shard_map/ppermute | solution.py:182
  15.9 0.0 collective-permute-done.17.refs_14_
  15.9 0.0 collective-permute-start.7
  15.9 0.6 collective-permute-done.14.refs_11_
  16.5 0.0 collective-permute-start.6
  16.5 1.2 %collective-permute-done.6.far_targets = s32[2,1,4]{2,1,0:T(1,128)S(1)} collective-permute-done((s32[2,1,4]{2,1,0:T(1,128)S(1)}, s32[2,1,4]{2,1,0:T(1,128)S(1)}, u32[]{:S(2)}, u32[]{:S(2)}) %collective-permute-start.6) | collective-permute-done | bytes 64 | tf_op jit(solution)/shard_map/ppermute | solution.py:188
  17.6 1.5 %collective-permute-start.15 = (bf16[256,512]{1,0:T(8,128)(2,1)S(1)}, bf16[256,512]{1,0:T(8,128)(2,1)S(1)}, u32[]{:S(2)}, u32[]{:S(2)}) collective-permute-start(bf16[256,512]{1,0:T(8,128)(2,1)S(1)} %get-tuple-element.37.refs_10_), channel_id=1, source_target_pairs={{0,8},{8,0},{16,24},{24,16},{1,9},{9,1},{17,25},{25,17},{2,10},{10... | collective-permute-start | bytes 786440 | tf_op jit(solution)/shard_map/ppermute | solution.py:182
  19.1 0.0 collective-permute-done.3.refs_1_
  19.1 0.5 collective-permute-start.16
  19.6 0.0 collective-permute-done.4.refs_2_
  19.6 0.7 %collective-permute-start.19 = (bf16[256,512]{1,0:T(8,128)(2,1)S(1)}, bf16[256,512]{1,0:T(8,128)(2,1)S(1)}, u32[]{:S(2)}, u32[]{:S(2)}) collective-permute-start(bf16[256,512]{1,0:T(8,128)(2,1)S(1)} %collective-permute-done.17.refs_14_), channel_id=1, source_target_pairs={{0,8},{8,0},{16,24},{24,16},{1,9},{9,1},{17,25},{25,17},{2,10},{10... | collective-permute-start | bytes 786440 | tf_op jit(solution)/shard_map/ppermute | solution.py:182
  20.4 0.0 collective-permute-done.5.refs_3_
  20.4 1.3 %collective-permute-start.18 = (bf16[256,512]{1,0:T(8,128)(2,1)S(1)}, bf16[256,512]{1,0:T(8,128)(2,1)S(1)}, u32[]{:S(2)}, u32[]{:S(2)}) collective-permute-start(bf16[256,512]{1,0:T(8,128)(2,1)S(1)} %collective-permute-done.14.refs_11_), channel_id=1, source_target_pairs={{0,16},{8,24},{16,0},{24,8},{1,17},{9,25},{17,1},{25,9},{2,18},{10... | collective-permute-start | bytes 786440 | tf_op jit(solution)/shard_map/ppermute | solution.py:182
  21.7 0.0 collective-permute-done.7.refs_4_.refs_8_
  21.7 0.0 collective-permute-start.8
  21.7 1.2 %collective-permute-done.8.refs_5_.refs_9_ = bf16[32,768]{1,0:T(8,128)(2,1)S(1)} collective-permute-done((bf16[32,768]{1,0:T(8,128)(2,1)S(1)}, bf16[32,768]{1,0:T(8,128)(2,1)S(1)}, u32[]{:S(2)}, u32[]{:S(2)}) %collective-permute-start.8) | collective-permute-done | bytes 49184 | tf_op jit(solution)/shard_map/ppermute | solution.py:188
  22.9 0.2 collective-permute-start.9
  23.1 1.1 %collective-permute-done.9.refs_6_.refs_10_ = bf16[32,768]{1,0:T(8,128)(2,1)S(1)} collective-permute-done((bf16[32,768]{1,0:T(8,128)(2,1)S(1)}, bf16[32,768]{1,0:T(8,128)(2,1)S(1)}, u32[]{:S(2)}, u32[]{:S(2)}) %collective-permute-start.9) | collective-permute-done | bytes 49184 | tf_op jit(solution)/shard_map/ppermute | solution.py:188
  24.2 0.2 collective-permute-start.10
  24.3 1.1 %collective-permute-done.10.refs_7_.refs_11_ = bf16[32,768]{1,0:T(8,128)(2,1)S(1)} collective-permute-done((bf16[32,768]{1,0:T(8,128)(2,1)S(1)}, bf16[32,768]{1,0:T(8,128)(2,1)S(1)}, u32[]{:S(2)}, u32[]{:S(2)}) %collective-permute-start.10) | collective-permute-done | bytes 49184 | tf_op jit(solution)/shard_map/ppermute | solution.py:188
  25.4 0.8 %shard_map.47 = (bf16[32,512]{1,0:T(8,128)(2,1)S(1)}, bf16[32,512]{1,0:T(8,128)(2,1)S(1)}, bf16[32,512]{1,0:T(8,128)(2,1)S(1)}, bf16[32,512]{1,0:T(8,128)(2,1)S(1)}) custom-call(s32[2,1,4]{2,1,0:T(1,128)S(1)} %copy-done.3, s32[2,1,4]{2,1,0:T(1,128)S(1)} %collective-permute-done.6.far_targets, bf16[32,768]{1,0:T(8,128)(2,1)S(1)} %get-tuple-element.29.refs_0_, ...), custom_call_target="tpu_custom_call" | custom-call | bytes 393280 | tf_op jit(solution)/shard_map/pallas_call | solution.py:25
  26.2 1.6 %collective-permute-start.11 = (bf16[32,512]{1,0:T(8,128)(2,1)S(1)}, bf16[32,512]{1,0:T(8,128)(2,1)S(1)}, u32[]{:S(2)}, u32[]{:S(2)}) collective-permute-start(bf16[32,512]{1,0:T(8,128)(2,1)S(1)} %get-tuple-element.34), channel_id=1, source_target_pairs={{0,2},{1,3},{2,0},{3,1},{4,6},{5,7},{6,4},{7,5},{8,10},{9,11},{10,... | collective-permute-start | bytes 98312 | tf_op jit(solution)/shard_map/ppermute | solution.py:185
  27.8 2.3 %collective-permute-done.11.refs_5_ = bf16[32,512]{1,0:T(8,128)(2,1)S(1)} collective-permute-done((bf16[32,512]{1,0:T(8,128)(2,1)S(1)}, bf16[32,512]{1,0:T(8,128)(2,1)S(1)}, u32[]{:S(2)}, u32[]{:S(2)}) %collective-permute-start.11) | collective-permute-done | bytes 32800 | tf_op jit(solution)/shard_map/ppermute | solution.py:185
  30.2 2.6 %collective-permute-start.12 = (bf16[32,512]{1,0:T(8,128)(2,1)S(1)}, bf16[32,512]{1,0:T(8,128)(2,1)S(1)}, u32[]{:S(2)}, u32[]{:S(2)}) collective-permute-start(bf16[32,512]{1,0:T(8,128)(2,1)S(1)} %get-tuple-element.35), channel_id=1, source_target_pairs={{0,4},{1,5},{2,6},{3,7},{4,0},{5,1},{6,2},{7,3},{8,12},{9,13},{10,... | collective-permute-start | bytes 98312 | tf_op jit(solution)/shard_map/ppermute | solution.py:185
  32.8 2.2 %collective-permute-done.12.refs_6_ = bf16[32,512]{1,0:T(8,128)(2,1)S(1)} collective-permute-done((bf16[32,512]{1,0:T(8,128)(2,1)S(1)}, bf16[32,512]{1,0:T(8,128)(2,1)S(1)}, u32[]{:S(2)}, u32[]{:S(2)}) %collective-permute-start.12) | collective-permute-done | bytes 32800 | tf_op jit(solution)/shard_map/ppermute | solution.py:185
  35.0 3.8 %collective-permute-start.13 = (bf16[32,512]{1,0:T(8,128)(2,1)S(1)}, bf16[32,512]{1,0:T(8,128)(2,1)S(1)}, u32[]{:S(2)}, u32[]{:S(2)}) collective-permute-start(bf16[32,512]{1,0:T(8,128)(2,1)S(1)} %get-tuple-element.36), channel_id=1, source_target_pairs={{0,6},{1,7},{2,4},{3,5},{4,2},{5,3},{6,0},{7,1},{8,14},{9,15},{10,... | collective-permute-start | bytes 98312 | tf_op jit(solution)/shard_map/ppermute | solution.py:185
  38.8 1.9 %collective-permute-done.13.refs_7_ = bf16[32,512]{1,0:T(8,128)(2,1)S(1)} collective-permute-done((bf16[32,512]{1,0:T(8,128)(2,1)S(1)}, bf16[32,512]{1,0:T(8,128)(2,1)S(1)}, u32[]{:S(2)}, u32[]{:S(2)}) %collective-permute-start.13) | collective-permute-done | bytes 32800 | tf_op jit(solution)/shard_map/ppermute | solution.py:185
  40.7 0.0 collective-permute-done.15.refs_12_
  40.7 0.0 collective-permute-done.16.refs_13_
  40.7 0.0 collective-permute-done.19.refs_16_
  40.7 0.0 collective-permute-done.18.refs_15_
  40.8 0.9 %shard_map.48 = (bf16[32,512]{1,0:T(8,128)(2,1)S(1)}, bf16[4,32,512]{2,1,0:T(8,128)(2,1)S(1)}) custom-call(bf16[32,768]{1,0:T(8,128)(2,1)S(1)} %get-tuple-element.29.refs_0_, bf16[32,768]{1,0:T(8,128)(2,1)S(1)} %collective-permute-done.3.refs_1_, bf16[32,768]{1,0:T(8,128)(2,1)S(1)} %collective-permute-done.4.refs_2_, ...), custom_call_target="tpu_custom_call" | custom-call | flops 83886080 | bytes 3997696 | tf_op jit(solution)/shard_map/pallas_call | solution.py:25
  41.7 0.0 collective-permute-start.20
  41.7 1.3 %collective-permute-done.20.refs_12_.refs_13_.refs_14_.refs_15_ = bf16[4,32,512]{2,1,0:T(8,128)(2,1)S(1)} collective-permute-done((bf16[4,32,512]{2,1,0:T(8,128)(2,1)S(1)}, bf16[4,32,512]{2,1,0:T(8,128)(2,1)S(1)}, u32[]{:S(2)}, u32[]{:S(2)}) %collective-permute-start.20) | collective-permute-done | bytes 131104 | tf_op jit(solution)/shard_map/ppermute | solution.py:188
  43.0 1.0 %shard_map.49 = (bf16[32,512]{1,0:T(8,128)(2,1)S(1)}, bf16[32,512]{1,0:T(8,128)(2,1)S(1)}, bf16[32,512]{1,0:T(8,128)(2,1)S(1)}, bf16[32,512]{1,0:T(8,128)(2,1)S(1)}) custom-call(s32[2,1,4]{2,1,0:T(1,128)S(1)} %copy-done.3, s32[2,1,4]{2,1,0:T(1,128)S(1)} %collective-permute-done.6.far_targets, bf16[32,768]{1,0:T(8,128)(2,1)S(1)} %get-tuple-element.29.refs_0_, ...), custom_call_target="tpu_custom_call" | custom-call | bytes 1441856 | tf_op jit(solution)/shard_map/pallas_call | solution.py:25
  44.1 0.1 collective-permute-start.21
  44.1 4.4 %collective-permute-start.22 = (bf16[32,512]{1,0:T(8,128)(2,1)S(1)}, bf16[32,512]{1,0:T(8,128)(2,1)S(1)}, u32[]{:S(2)}, u32[]{:S(2)}) collective-permute-start(bf16[32,512]{1,0:T(8,128)(2,1)S(1)} %get-tuple-element.44), channel_id=1, source_target_pairs={{0,4},{1,5},{2,6},{3,7},{4,0},{5,1},{6,2},{7,3},{8,12},{9,13},{10,... | collective-permute-start | bytes 98312 | tf_op jit(solution)/shard_map/ppermute | solution.py:185
  48.5 0.0 collective-permute-start.23
  48.5 0.0 collective-permute-done.21.refs_5_
  48.5 2.5 %collective-permute-done.22.refs_6_ = bf16[32,512]{1,0:T(8,128)(2,1)S(1)} collective-permute-done((bf16[32,512]{1,0:T(8,128)(2,1)S(1)}, bf16[32,512]{1,0:T(8,128)(2,1)S(1)}, u32[]{:S(2)}, u32[]{:S(2)}) %collective-permute-start.22) | collective-permute-done | bytes 32800 | tf_op jit(solution)/shard_map/ppermute | solution.py:185
  51.0 3.2 %collective-permute-done.23.refs_7_ = bf16[32,512]{1,0:T(8,128)(2,1)S(1)} collective-permute-done((bf16[32,512]{1,0:T(8,128)(2,1)S(1)}, bf16[32,512]{1,0:T(8,128)(2,1)S(1)}, u32[]{:S(2)}, u32[]{:S(2)}) %collective-permute-start.23) | collective-permute-done | bytes 32800 | tf_op jit(solution)/shard_map/ppermute | solution.py:185
  54.2 0.3 shard_map.50
  54.5 1.6 %collective-permute-start.24 = (bf16[2,32,128]{2,1,0:T(8,128)(2,1)S(1)}, bf16[2,32,128]{2,1,0:T(8,128)(2,1)S(1)}, u32[]{:S(2)}, u32[]{:S(2)}) collective-permute-start(bf16[2,32,128]{2,1,0:T(8,128)(2,1)S(1)} %get-tuple-element.48), channel_id=1, source_target_pairs={{0,8},{8,0},{16,24},{24,16},{1,9},{9,1},{17,25},{25,17},{2,10},{10... | collective-permute-start | bytes 49160 | tf_op jit(solution)/shard_map/ppermute | solution.py:182
  56.1 0.5 collective-permute-start.25
  56.6 1.5 %collective-permute-start.26 = (bf16[2,32,128]{2,1,0:T(8,128)(2,1)S(1)}, bf16[2,32,128]{2,1,0:T(8,128)(2,1)S(1)}, u32[]{:S(2)}, u32[]{:S(2)}) collective-permute-start(bf16[2,32,128]{2,1,0:T(8,128)(2,1)S(1)} %get-tuple-element.50), channel_id=1, source_target_pairs={{0,24},{8,16},{16,8},{24,0},{1,25},{9,17},{17,9},{25,1},{2,26},{10... | collective-permute-start | bytes 49160 | tf_op jit(solution)/shard_map/ppermute | solution.py:182
  58.1 0.3 collective-permute-done.24.refs_2_
  58.4 1.5 %collective-permute-done.25.refs_3_ = bf16[2,32,128]{2,1,0:T(8,128)(2,1)S(1)} collective-permute-done((bf16[2,32,128]{2,1,0:T(8,128)(2,1)S(1)}, bf16[2,32,128]{2,1,0:T(8,128)(2,1)S(1)}, u32[]{:S(2)}, u32[]{:S(2)}) %collective-permute-start.25) | collective-permute-done | bytes 16416 | tf_op jit(solution)/shard_map/ppermute | solution.py:182
  59.8 1.4 %collective-permute-done.26.refs_4_ = bf16[2,32,128]{2,1,0:T(8,128)(2,1)S(1)} collective-permute-done((bf16[2,32,128]{2,1,0:T(8,128)(2,1)S(1)}, bf16[2,32,128]{2,1,0:T(8,128)(2,1)S(1)}, u32[]{:S(2)}, u32[]{:S(2)}) %collective-permute-start.26) | collective-permute-done | bytes 16416 | tf_op jit(solution)/shard_map/ppermute | solution.py:182
  61.2 0.8 %shard_map.51 = bf16[3,1,128,128]{3,2,1,0:T(8,128)(2,1)} custom-call(bf16[128,128]{1,0:T(8,128)(2,1)S(1)} %get-tuple-element.28.refs_0_, bf16[2,32,128]{2,1,0:T(8,128)(2,1)S(1)} %get-tuple-element.47.refs_1_, bf16[2,32,128]{2,1,0:T(8,128)(2,1)S(1)} %collective-permute-done.24.refs_2_, bf16[2,32,128]{2,1,0:T(8,128)(2,1)S(1)} %collective-permute-done.25.refs_3_, ...), custom_call_target="tpu_custom_call" | custom-call | bytes 98304 | tf_op jit(solution)/shard_map/pallas_call | solution.py:25
  (7 shorter events, 0.0 us)
Async XLA Ops:
  0.0 11.1 %copy-start.2 = (bf16[3,1,128,128]{3,2,1,0:T(8,128)(2,1)S(1)}, bf16[3,1,128,128]{3,2,1,0:T(8,128)(2,1)}, u32[]{:S(2)}) copy-start(bf16[3,1,128,128]{3,2,1,0:T(8,128)(2,1)} %refs_5_.1) | copy-start | bytes 294916
  0.0 11.1 %copy-start.1 = (bf16[2,1,1,512,512]{4,3,2,1,0:T(8,128)(2,1)S(1)}, bf16[2,1,1,512,512]{4,3,2,1,0:T(8,128)(2,1)}, u32[]{:S(2)}) copy-start(bf16[2,1,1,512,512]{4,3,2,1,0:T(8,128)(2,1)} %refs_6_.1) | copy-start | bytes 3145732
  0.9 10.2 %collective-permute-start.2 = (bf16[128,128]{1,0:T(8,128)(2,1)S(1)}, bf16[128,128]{1,0:T(8,128)(2,1)S(1)}, u32[]{:S(2)}, u32[]{:S(2)}) collective-permute-start(bf16[128,128]{1,0:T(8,128)(2,1)S(1)} %slice_bitcast_fusion.3.refs_0_), channel_id=1, source_target_pairs={{0,24},{8,16},{16,8},{24,0},{1,25},{9,17},{17,9},{25,1},{2,26},{10... | collective-permute-start | bytes 98312 | tf_op jit(solution)/shard_map/ppermute | solution.py:182
  4.8 6.3 %collective-permute-start.1 = (bf16[128,128]{1,0:T(8,128)(2,1)S(1)}, bf16[128,128]{1,0:T(8,128)(2,1)S(1)}, u32[]{:S(2)}, u32[]{:S(2)}) collective-permute-start(bf16[128,128]{1,0:T(8,128)(2,1)S(1)} %slice_bitcast_fusion.3.refs_0_), channel_id=1, source_target_pairs={{0,16},{8,24},{16,0},{24,8},{1,17},{9,25},{17,1},{25,9},{2,18},{10... | collective-permute-start | bytes 98312 | tf_op jit(solution)/shard_map/ppermute | solution.py:182
  5.3 5.8 %collective-permute-start = (bf16[128,128]{1,0:T(8,128)(2,1)S(1)}, bf16[128,128]{1,0:T(8,128)(2,1)S(1)}, u32[]{:S(2)}, u32[]{:S(2)}) collective-permute-start(bf16[128,128]{1,0:T(8,128)(2,1)S(1)} %slice_bitcast_fusion.3.refs_0_), channel_id=1, source_target_pairs={{0,8},{8,0},{16,24},{24,16},{1,9},{9,1},{17,25},{25,17},{2,10},{10... | collective-permute-start | bytes 98312 | tf_op jit(solution)/shard_map/ppermute | solution.py:182
  6.4 10.1 %copy-start.3 = (s32[2,1,4]{2,1,0:T(1,128)S(1)}, s32[2,1,4]{2,1,0:T(1,128)}, u32[]{:S(2)}) copy-start(s32[2,1,4]{2,1,0:T(1,128)} %own_targets.3) | copy-start | bytes 100
  6.4 9.4 %collective-permute-start.17 = (bf16[256,512]{1,0:T(8,128)(2,1)S(1)}, bf16[256,512]{1,0:T(8,128)(2,1)S(1)}, u32[]{:S(2)}, u32[]{:S(2)}) collective-permute-start(bf16[256,512]{1,0:T(8,128)(2,1)S(1)} %get-tuple-element.37.refs_10_), channel_id=1, source_target_pairs={{0,16},{8,24},{16,0},{24,8},{1,17},{9,25},{17,1},{25,9},{2,18},{10... | collective-permute-start | bytes 786440 | tf_op jit(solution)/shard_map/ppermute | solution.py:182
  8.5 32.3 %copy-start = (bf16[3,1,512,512]{3,2,1,0:T(8,128)(2,1)S(1)}, bf16[3,1,512,512]{3,2,1,0:T(8,128)(2,1)}, u32[]{:S(2)}) copy-start(bf16[3,1,512,512]{3,2,1,0:T(8,128)(2,1)} %refs_8_.3) | copy-start | bytes 4718596
  8.5 8.0 %collective-permute-start.14 = (bf16[256,512]{1,0:T(8,128)(2,1)S(1)}, bf16[256,512]{1,0:T(8,128)(2,1)S(1)}, u32[]{:S(2)}, u32[]{:S(2)}) collective-permute-start(bf16[256,512]{1,0:T(8,128)(2,1)S(1)} %get-tuple-element.38.refs_9_), channel_id=1, source_target_pairs={{0,8},{8,0},{16,24},{24,16},{1,9},{9,1},{17,25},{25,17},{2,10},{10... | collective-permute-start | bytes 786440 | tf_op jit(solution)/shard_map/ppermute | solution.py:182
  12.3 6.8 %collective-permute-start.3 = (bf16[32,768]{1,0:T(8,128)(2,1)S(1)}, bf16[32,768]{1,0:T(8,128)(2,1)S(1)}, u32[]{:S(2)}, u32[]{:S(2)}) collective-permute-start(bf16[32,768]{1,0:T(8,128)(2,1)S(1)} %get-tuple-element.30), channel_id=1, source_target_pairs={{0,8},{8,0},{16,24},{24,16},{1,9},{9,1},{17,25},{25,17},{2,10},{10... | collective-permute-start | bytes 147464 | tf_op jit(solution)/shard_map/ppermute | solution.py:182
  12.9 6.7 %collective-permute-start.4 = (bf16[32,768]{1,0:T(8,128)(2,1)S(1)}, bf16[32,768]{1,0:T(8,128)(2,1)S(1)}, u32[]{:S(2)}, u32[]{:S(2)}) collective-permute-start(bf16[32,768]{1,0:T(8,128)(2,1)S(1)} %get-tuple-element.31), channel_id=1, source_target_pairs={{0,16},{8,24},{16,0},{24,8},{1,17},{9,25},{17,1},{25,9},{2,18},{10... | collective-permute-start | bytes 147464 | tf_op jit(solution)/shard_map/ppermute | solution.py:182
  13.1 7.3 %collective-permute-start.5 = (bf16[32,768]{1,0:T(8,128)(2,1)S(1)}, bf16[32,768]{1,0:T(8,128)(2,1)S(1)}, u32[]{:S(2)}, u32[]{:S(2)}) collective-permute-start(bf16[32,768]{1,0:T(8,128)(2,1)S(1)} %get-tuple-element.32), channel_id=1, source_target_pairs={{0,24},{8,16},{16,8},{24,0},{1,25},{9,17},{17,9},{25,1},{2,26},{10... | collective-permute-start | bytes 147464 | tf_op jit(solution)/shard_map/ppermute | solution.py:182
  15.9 5.8 %collective-permute-start.7 = (bf16[32,768]{1,0:T(8,128)(2,1)S(1)}, bf16[32,768]{1,0:T(8,128)(2,1)S(1)}, u32[]{:S(2)}, u32[]{:S(2)}) collective-permute-start(bf16[32,768]{1,0:T(8,128)(2,1)S(1)} %get-tuple-element.29.refs_0_), channel_id=1, source_target_pairs={{0,1},{1,0},{2,3},{3,2},{4,5},{5,4},{6,7},{7,6},{8,9},{9,8},{10,11... | collective-permute-start | bytes 147464 | tf_op jit(solution)/shard_map/ppermute | solution.py:188
  16.5 1.2 %collective-permute-start.6 = (s32[2,1,4]{2,1,0:T(1,128)S(1)}, s32[2,1,4]{2,1,0:T(1,128)S(1)}, u32[]{:S(2)}, u32[]{:S(2)}) collective-permute-start(s32[2,1,4]{2,1,0:T(1,128)S(1)} %copy-done.3), channel_id=1, source_target_pairs={{0,1},{1,0},{2,3},{3,2},{4,5},{5,4},{6,7},{7,6},{8,9},{9,8},{10,11... | collective-permute-start | bytes 104 | tf_op jit(solution)/shard_map/ppermute | solution.py:188
  17.6 23.1 %collective-permute-start.15 = (bf16[256,512]{1,0:T(8,128)(2,1)S(1)}, bf16[256,512]{1,0:T(8,128)(2,1)S(1)}, u32[]{:S(2)}, u32[]{:S(2)}) collective-permute-start(bf16[256,512]{1,0:T(8,128)(2,1)S(1)} %get-tuple-element.37.refs_10_), channel_id=1, source_target_pairs={{0,8},{8,0},{16,24},{24,16},{1,9},{9,1},{17,25},{25,17},{2,10},{10... | collective-permute-start | bytes 786440 | tf_op jit(solution)/shard_map/ppermute | solution.py:182
  19.1 21.6 %collective-permute-start.16 = (bf16[256,512]{1,0:T(8,128)(2,1)S(1)}, bf16[256,512]{1,0:T(8,128)(2,1)S(1)}, u32[]{:S(2)}, u32[]{:S(2)}) collective-permute-start(bf16[256,512]{1,0:T(8,128)(2,1)S(1)} %get-tuple-element.38.refs_9_), channel_id=1, source_target_pairs={{0,16},{8,24},{16,0},{24,8},{1,17},{9,25},{17,1},{25,9},{2,18},{10... | collective-permute-start | bytes 786440 | tf_op jit(solution)/shard_map/ppermute | solution.py:182
  19.6 21.1 %collective-permute-start.19 = (bf16[256,512]{1,0:T(8,128)(2,1)S(1)}, bf16[256,512]{1,0:T(8,128)(2,1)S(1)}, u32[]{:S(2)}, u32[]{:S(2)}) collective-permute-start(bf16[256,512]{1,0:T(8,128)(2,1)S(1)} %collective-permute-done.17.refs_14_), channel_id=1, source_target_pairs={{0,8},{8,0},{16,24},{24,16},{1,9},{9,1},{17,25},{25,17},{2,10},{10... | collective-permute-start | bytes 786440 | tf_op jit(solution)/shard_map/ppermute | solution.py:182
  20.4 20.3 %collective-permute-start.18 = (bf16[256,512]{1,0:T(8,128)(2,1)S(1)}, bf16[256,512]{1,0:T(8,128)(2,1)S(1)}, u32[]{:S(2)}, u32[]{:S(2)}) collective-permute-start(bf16[256,512]{1,0:T(8,128)(2,1)S(1)} %collective-permute-done.14.refs_11_), channel_id=1, source_target_pairs={{0,16},{8,24},{16,0},{24,8},{1,17},{9,25},{17,1},{25,9},{2,18},{10... | collective-permute-start | bytes 786440 | tf_op jit(solution)/shard_map/ppermute | solution.py:182
  21.7 1.2 %collective-permute-start.8 = (bf16[32,768]{1,0:T(8,128)(2,1)S(1)}, bf16[32,768]{1,0:T(8,128)(2,1)S(1)}, u32[]{:S(2)}, u32[]{:S(2)}) collective-permute-start(bf16[32,768]{1,0:T(8,128)(2,1)S(1)} %collective-permute-done.3.refs_1_), channel_id=1, source_target_pairs={{0,1},{1,0},{2,3},{3,2},{4,5},{5,4},{6,7},{7,6},{8,9},{9,8},{10,11... | collective-permute-start | bytes 147464 | tf_op jit(solution)/shard_map/ppermute | solution.py:188
  22.9 1.2 %collective-permute-start.9 = (bf16[32,768]{1,0:T(8,128)(2,1)S(1)}, bf16[32,768]{1,0:T(8,128)(2,1)S(1)}, u32[]{:S(2)}, u32[]{:S(2)}) collective-permute-start(bf16[32,768]{1,0:T(8,128)(2,1)S(1)} %collective-permute-done.4.refs_2_), channel_id=1, source_target_pairs={{0,1},{1,0},{2,3},{3,2},{4,5},{5,4},{6,7},{7,6},{8,9},{9,8},{10,11... | collective-permute-start | bytes 147464 | tf_op jit(solution)/shard_map/ppermute | solution.py:188
  24.2 1.2 %collective-permute-start.10 = (bf16[32,768]{1,0:T(8,128)(2,1)S(1)}, bf16[32,768]{1,0:T(8,128)(2,1)S(1)}, u32[]{:S(2)}, u32[]{:S(2)}) collective-permute-start(bf16[32,768]{1,0:T(8,128)(2,1)S(1)} %collective-permute-done.5.refs_3_), channel_id=1, source_target_pairs={{0,1},{1,0},{2,3},{3,2},{4,5},{5,4},{6,7},{7,6},{8,9},{9,8},{10,11... | collective-permute-start | bytes 147464 | tf_op jit(solution)/shard_map/ppermute | solution.py:188
  26.2 4.0 %collective-permute-start.11 = (bf16[32,512]{1,0:T(8,128)(2,1)S(1)}, bf16[32,512]{1,0:T(8,128)(2,1)S(1)}, u32[]{:S(2)}, u32[]{:S(2)}) collective-permute-start(bf16[32,512]{1,0:T(8,128)(2,1)S(1)} %get-tuple-element.34), channel_id=1, source_target_pairs={{0,2},{1,3},{2,0},{3,1},{4,6},{5,7},{6,4},{7,5},{8,10},{9,11},{10,... | collective-permute-start | bytes 98312 | tf_op jit(solution)/shard_map/ppermute | solution.py:185
  30.2 4.8 %collective-permute-start.12 = (bf16[32,512]{1,0:T(8,128)(2,1)S(1)}, bf16[32,512]{1,0:T(8,128)(2,1)S(1)}, u32[]{:S(2)}, u32[]{:S(2)}) collective-permute-start(bf16[32,512]{1,0:T(8,128)(2,1)S(1)} %get-tuple-element.35), channel_id=1, source_target_pairs={{0,4},{1,5},{2,6},{3,7},{4,0},{5,1},{6,2},{7,3},{8,12},{9,13},{10,... | collective-permute-start | bytes 98312 | tf_op jit(solution)/shard_map/ppermute | solution.py:185
  35.0 5.7 %collective-permute-start.13 = (bf16[32,512]{1,0:T(8,128)(2,1)S(1)}, bf16[32,512]{1,0:T(8,128)(2,1)S(1)}, u32[]{:S(2)}, u32[]{:S(2)}) collective-permute-start(bf16[32,512]{1,0:T(8,128)(2,1)S(1)} %get-tuple-element.36), channel_id=1, source_target_pairs={{0,6},{1,7},{2,4},{3,5},{4,2},{5,3},{6,0},{7,1},{8,14},{9,15},{10,... | collective-permute-start | bytes 98312 | tf_op jit(solution)/shard_map/ppermute | solution.py:185
  41.7 1.4 %collective-permute-start.20 = (bf16[4,32,512]{2,1,0:T(8,128)(2,1)S(1)}, bf16[4,32,512]{2,1,0:T(8,128)(2,1)S(1)}, u32[]{:S(2)}, u32[]{:S(2)}) collective-permute-start(bf16[4,32,512]{2,1,0:T(8,128)(2,1)S(1)} %get-tuple-element.41.refs_4_.refs_5_.refs_6_.refs_7_), channel_id=1, source_target_pairs={{0,1},{1,0},{2,3},{3,2},{4,5},{5,4},{6,7},{7,6},{8,9},{9,8},{10,11... | collective-permute-start | bytes 393224 | tf_op jit(solution)/shard_map/ppermute | solution.py:188
  44.1 4.5 %collective-permute-start.21 = (bf16[32,512]{1,0:T(8,128)(2,1)S(1)}, bf16[32,512]{1,0:T(8,128)(2,1)S(1)}, u32[]{:S(2)}, u32[]{:S(2)}) collective-permute-start(bf16[32,512]{1,0:T(8,128)(2,1)S(1)} %get-tuple-element.43), channel_id=1, source_target_pairs={{0,2},{1,3},{2,0},{3,1},{4,6},{5,7},{6,4},{7,5},{8,10},{9,11},{10,... | collective-permute-start | bytes 98312 | tf_op jit(solution)/shard_map/ppermute | solution.py:185
  44.1 6.9 %collective-permute-start.22 = (bf16[32,512]{1,0:T(8,128)(2,1)S(1)}, bf16[32,512]{1,0:T(8,128)(2,1)S(1)}, u32[]{:S(2)}, u32[]{:S(2)}) collective-permute-start(bf16[32,512]{1,0:T(8,128)(2,1)S(1)} %get-tuple-element.44), channel_id=1, source_target_pairs={{0,4},{1,5},{2,6},{3,7},{4,0},{5,1},{6,2},{7,3},{8,12},{9,13},{10,... | collective-permute-start | bytes 98312 | tf_op jit(solution)/shard_map/ppermute | solution.py:185
  48.5 5.7 %collective-permute-start.23 = (bf16[32,512]{1,0:T(8,128)(2,1)S(1)}, bf16[32,512]{1,0:T(8,128)(2,1)S(1)}, u32[]{:S(2)}, u32[]{:S(2)}) collective-permute-start(bf16[32,512]{1,0:T(8,128)(2,1)S(1)} %get-tuple-element.45), channel_id=1, source_target_pairs={{0,6},{1,7},{2,4},{3,5},{4,2},{5,3},{6,0},{7,1},{8,14},{9,15},{10,... | collective-permute-start | bytes 98312 | tf_op jit(solution)/shard_map/ppermute | solution.py:185
  54.5 3.8 %collective-permute-start.24 = (bf16[2,32,128]{2,1,0:T(8,128)(2,1)S(1)}, bf16[2,32,128]{2,1,0:T(8,128)(2,1)S(1)}, u32[]{:S(2)}, u32[]{:S(2)}) collective-permute-start(bf16[2,32,128]{2,1,0:T(8,128)(2,1)S(1)} %get-tuple-element.48), channel_id=1, source_target_pairs={{0,8},{8,0},{16,24},{24,16},{1,9},{9,1},{17,25},{25,17},{2,10},{10... | collective-permute-start | bytes 49160 | tf_op jit(solution)/shard_map/ppermute | solution.py:182
  56.1 3.7 %collective-permute-start.25 = (bf16[2,32,128]{2,1,0:T(8,128)(2,1)S(1)}, bf16[2,32,128]{2,1,0:T(8,128)(2,1)S(1)}, u32[]{:S(2)}, u32[]{:S(2)}) collective-permute-start(bf16[2,32,128]{2,1,0:T(8,128)(2,1)S(1)} %get-tuple-element.49), channel_id=1, source_target_pairs={{0,16},{8,24},{16,0},{24,8},{1,17},{9,25},{17,1},{25,9},{2,18},{10... | collective-permute-start | bytes 49160 | tf_op jit(solution)/shard_map/ppermute | solution.py:182
  56.6 4.6 %collective-permute-start.26 = (bf16[2,32,128]{2,1,0:T(8,128)(2,1)S(1)}, bf16[2,32,128]{2,1,0:T(8,128)(2,1)S(1)}, u32[]{:S(2)}, u32[]{:S(2)}) collective-permute-start(bf16[2,32,128]{2,1,0:T(8,128)(2,1)S(1)} %get-tuple-element.50), channel_id=1, source_target_pairs={{0,24},{8,16},{16,8},{24,0},{1,25},{9,17},{17,9},{25,1},{2,26},{10... | collective-permute-start | bytes 49160 | tf_op jit(solution)/shard_map/ppermute | solution.py:182
where the time goes:
time: 62.2 us; the launch traced here: 62 us
  starting transfers between devices  32.1 us (52%)
  waiting for transfers between devices  21.8 us (35%)
  Pallas kernels  4.98 us (8%)
  local copies, waits for them, and re-layouts  3.01 us (5%)
    ppermute x15, starting transfers between devices, over_rows(): return lax.ppermute(x, 'prow', pairs(rows, step)) if step else x  19.2 us
    ppermute x6, starting transfers between devices, over_pairs(): return lax.ppermute(x, 'pcol', pairs(columns, 2 * step)) if step else x  12.5 us
    ppermute x6, waiting for transfers between devices, over_pairs(): return lax.ppermute(x, 'pcol', pairs(columns, 2 * step)) if step else x  12.2 us
    ppermute x6, waiting for transfers between devices, flip(): return lax.ppermute(x, 'pcol', pairs(columns, 1))  5.87 us
    pallas_call x6, Pallas kernels, call(): pl.pallas_call(kernel, out_shape=out_shapes, in_specs=[smem] * scalars +...  4.98 us
    ppermute x15, waiting for transfers between devices, over_rows(): return lax.ppermute(x, 'prow', pairs(rows, step)) if step else x  3.77 us
  transfers between devices with their start and end apart: 27, of which 14 were waited for; matrix products, arithmetic and copies ran while one was open for 3% of the time, Pallas kernels for 3%

commit v1 on v0

--- a/solution.py
+++ b/solution.py
@@ -25,12 +25,23 @@
     return pl.pallas_call(
         kernel,
         out_shape=out_shapes,
-        in_specs=[smem] * scalars + [vmem] * (len(operands) - scalars - placed) + [pl.BlockSpec(memory_space=pl.ANY)] * placed,
+        in_specs=[smem] * scalars + [vmem] * (len(operands) - scalars - placed) + [pl.BlockSpec(memory_space=pltpu.HBM if placed == len(operands) else pl.ANY)] * placed,
         out_specs=[vmem] * len(out_shapes),
         scratch_shapes=list(scratch),
         compiler_params=pltpu.CompilerParams(vmem_limit_bytes=GRANT),
         cost_estimate=pl.CostEstimate(flops=flops, bytes_accessed=moved, transcendentals=0),
     )(*operands)
+
+
+def load_kernel(later, rhs, inverse, off, first, *refs):
+    blocks, top, done = refs[: later - 1], refs[later - 1], refs[later]
+    copies = [(rhs.at[0, 0], first), (inverse.at[0, 0], top)]
+    copies += [(off.at[level + 1, 0, 0], block) for level, block in enumerate(blocks)]
+    copies = [pltpu.make_async_copy(*ends, done.at[at]) for at, ends in enumerate(copies)]
+    for copy in copies:
+        copy.start()
+    for copy in copies:
+        copy.wait()
 
 
 def first_kernel(rows, later, *refs):
@@ -75,10 +86,11 @@
     for step in range(half):
         column = (me_col ^ (2 * step)) + level * 2 * half
         total = jnp.zeros((each, size), F32)
-        for targets, group in ((own_targets, own), (far_targets, far)):
-            for (source, at), ref in zip(sources, group):
-                value = ref[at] if ref.ndim == 3 else ref[:, :size]
-                hit = targets[source[0], 0, me_row ^ source[1]] == column
+        for targets, group, odd in ((own_targets, own, me_col % 2), (far_targets, far, 1 - me_col % 2)):
+            for (source, turns, at), ref in zip(sources, group):
+                value = ref[:, :size] if at is None else ref[at]
+                turn = turns[0] if turns[0] == turns[1] else jnp.where(odd == 1, turns[1], turns[0])
+                hit = targets[source, 0, me_row ^ turn] == column
                 total = total + jnp.where(hit, value.astype(F32), 0.0)
         outs[step][...] = total.astype(outs[step].dtype)
 
@@ -117,17 +129,13 @@
     messages = refs[:rows]
     arrived = refs[rows : rows + half]
     inverse = refs[rows + half]
-    blocks = refs[rows + half + 1 : 3 * rows + half + 1]
-    solved, products, scratch = refs[3 * rows + half + 1 :]
+    blocks = refs[rows + half + 1 : 2 * rows + half + 1]
+    solved, products, scratch = refs[2 * rows + half + 1 :]
     given = residual(rows, level - 1, messages, arrived, scratch)
     value = solve(inverse, level, given)
     solved[...] = value
-    for step in range(rows):
-        low = 0
-        for piece in blocks[2 * step : 2 * step + 2]:
-            high = low + piece.shape[0]
-            products[step, :, low:high] = lax.dot_general(value, piece[...], NT, preferred_element_type=F32).astype(BF16)
-            low = high
+    for at, block in enumerate(blocks):
+        products[at] = lax.dot_general(value, block[...], NT, preferred_element_type=F32).astype(BF16)
 
 
 def last_kernel(rows, half, level, before, *refs):
@@ -181,6 +189,10 @@
     def over_rows(x, step):
         return lax.ppermute(x, "prow", pairs(rows, step)) if step else x
 
+    def over_turns(x, turn):
+        links = [(r * columns + c, (r ^ turn[c % 2]) * columns + c) for r in range(rows) for c in range(columns)]
+        return lax.ppermute(x, ("prow", "pcol"), links)
+
     def over_pairs(x, step):
         return lax.ppermute(x, "pcol", pairs(columns, 2 * step)) if step else x
 
@@ -188,13 +200,19 @@
         return lax.ppermute(x, "pcol", pairs(columns, 1))
 
     far_targets = flip(targets)
-    first = rhs[0, 0]
+    first, *owned, top = call(
+        functools.partial(load_kernel, later),
+        [shape((part, vectors), BF16)] + [shape((size, size), BF16)] * later,
+        [pltpu.with_memory_space_constraint(x, pltpu.HBM) for x in (rhs, inverse, off)],
+        placed=3,
+        scratch=[pltpu.SemaphoreType.DMA((later + 1,))],
+    )
     shares = [over_rows(first, step) for step in range(rows)]
     width = size + later * part
     kept, *sent = call(
         functools.partial(first_kernel, rows, later),
         [shape((part, vectors), BF16)] + [shape((each, width), BF16)] * rows,
-        [*shares, inverse[0, 0], rhs, off],
+        [*shares, top, rhs, off],
         placed=2,
         scratch=[
             pltpu.VMEM((size, vectors), BF16),
@@ -208,26 +226,18 @@
     )
     messages = [over_rows(x, step) for step, x in enumerate(sent)]
     far_messages = [flip(x) for x in messages]
-    blocks = {}
+    bits = [1 << b for b in range(rows.bit_length() - 1)]
+    blocks, steps = {}, [(0, 0)]
     for level in range(1, later):
-        cut = size // 2
-        upper, lower = off[level, 0, 0, :cut], off[level, 0, 0, cut:]
-        late_upper, late_lower, _ = lax.optimization_barrier((upper, lower, sent[0]))
-        bits = [1 << b for b in range(rows.bit_length() - 1)]
-        blocks[level] = [None] * (2 * rows)
-        for side, (early, late, order) in enumerate(((upper, late_upper, bits), (lower, late_lower, bits[::-1]))):
-            have = {0: early}
-            for number, bit in enumerate(order):
-                for step in sorted(have):
-                    source = have[step]
-                    if number:
-                        source = late if step == 0 else lax.optimization_barrier((source, sent[0]))[0]
-                    blocks[level][2 * (step ^ bit) + side] = over_rows(source, bit)
-                have = {step: blocks[level][2 * step + side] if step else early for step in [*have, *(x ^ bit for x in have)]}
-            blocks[level][side] = early
+        have = [owned[level - 1]]
+        for turn in zip(bits, bits[::-1]):
+            have += [over_turns(x, turn) for x in have]
+        blocks[level] = have
+    for turn in zip(bits, bits[::-1]):
+        steps += [(even ^ turn[0], odd ^ turn[1]) for even, odd in steps]
 
     own, far = list(messages), list(far_messages)
-    sources = [((0, step), None) for step in range(rows)]
+    sources = [(0, (step, step), None) for step in range(rows)]
     solved = []
     for level in range(1, levels):
         out = call(
@@ -249,7 +259,7 @@
             far_products = flip(products)
             own += [products] * rows
             far += [far_products] * rows
-            sources += [((level, step), step) for step in range(rows)]
+            sources += [(level, turns, at) for at, turns in enumerate(steps)]
     pieces = call(
         functools.partial(last_kernel, rows, half, later, len(solved)),
         [shape((later, each, part), BF16)] * rows,

time: 62.2 us -> 66.3 us (1.066)
  waiting for transfers between devices: 21.8 us -> 33.3 us
  starting transfers between devices: 32.1 us -> 26.4 us
  local copies, waits for them, and re-layouts: 3.01 us -> 0.02 us
  Pallas kernels: 4.98 us -> 6.3 us
    ppermute x0 -> x3, waiting for transfers between devices: none -> 10.7 us  [over_turns(): return lax.ppermute(x, ('prow', 'pcol'), links)]
    ppermute x15 -> x9, waiting for transfers between devices: 3.77 us -> 12.2 us  [over_rows(): return lax.ppermute(x, 'prow', pairs(rows, step)) if step else x]
    ppermute x15 -> x9, starting transfers between devices: 19.2 us -> 10.9 us  [over_rows(): return lax.ppermute(x, 'prow', pairs(rows, step)) if step else x]
    ppermute x0 -> x3, starting transfers between devices: none -> 6.11 us  [over_turns(): return lax.ppermute(x, ('prow', 'pcol'), links)]
    ppermute x6, waiting for transfers between devices: 12.2 us -> 7.78 us  [over_pairs(): return lax.ppermute(x, 'pcol', pairs(columns, 2 * step)) if step else x]
    ppermute x6, starting transfers between devices: 12.5 us -> 8.9 us  [over_pairs(): return lax.ppermute(x, 'pcol', pairs(columns, 2 * step)) if step else x]
    ppermute x6, waiting for transfers between devices: 5.87 us -> 2.64 us  [flip(): return lax.ppermute(x, 'pcol', pairs(columns, 1))]
    squeeze x3 -> x0, local copies, waits for them, and re-layouts: 2.99 us -> none  [the longest x1 1.08 us: local(): inverse[0, 0]]
  transfers between devices with their start and end apart: 27 -> 24, of which waited for: 14 -> 17; matrix products, arithmetic and copies ran while one was open for 3% -> 0% of each run, Pallas kernels for 3% -> 3%
where the time goes in v1:
time: 66.3 us; the launch traced here: 66.1 us
  waiting for transfers between devices  33.3 us (50%)
  starting transfers between devices  26.4 us (40%)
  Pallas kernels  6.3 us (10%)
    ppermute x9, waiting for transfers between devices, over_rows(): return lax.ppermute(x, 'prow', pairs(rows, step)) if step else x  12.2 us
    ppermute x9, starting transfers between devices, over_rows(): return lax.ppermute(x, 'prow', pairs(rows, step)) if step else x  10.9 us
    ppermute x3, waiting for transfers between devices, over_turns(): return lax.ppermute(x, ('prow', 'pcol'), links)  10.7 us
    ppermute x6, starting transfers between devices, over_pairs(): return lax.ppermute(x, 'pcol', pairs(columns, 2 * step)) if step else x  8.9 us
    ppermute x6, waiting for transfers between devices, over_pairs(): return lax.ppermute(x, 'pcol', pairs(columns, 2 * step)) if step else x  7.78 us
    pallas_call x7, Pallas kernels, call(): pl.pallas_call(kernel, out_shape=out_shapes, in_specs=[smem] * scalars +...  6.3 us
    ppermute x3, starting transfers between devices, over_turns(): return lax.ppermute(x, ('prow', 'pcol'), links)  6.11 us
    ppermute x6, waiting for transfers between devices, flip(): return lax.ppermute(x, 'pcol', pairs(columns, 1))  2.64 us
  transfers between devices with their start and end apart: 24, of which 17 were waited for; matrix products, arithmetic and copies ran while one was open for 0% of the time, Pallas kernels for 3%

profile of v1, /device:TPU:0, one launch (start us, length us, event | category | flops | bytes accessed | tf_op | source)
XLA Modules:
  0.0 66.1 jit_solution(15885785205640587960)
XLA Ops:
  0.0 0.0 copy-start.1
  0.0 0.0 copy-start.2
  0.0 1.3 %shard_map.46 = (bf16[128,128]{1,0:T(8,128)(2,1)S(1)}, bf16[512,512]{1,0:T(8,128)(2,1)S(1)}, bf16[512,512]{1,0:T(8,128)(2,1)S(1)}) custom-call(bf16[3,1,128,128]{3,2,1,0:T(8,128)(2,1)} %refs_5_.1, bf16[3,1,512,512]{3,2,1,0:T(8,128)(2,1)} %refs_8_.3, bf16[2,1,1,512,512]{4,3,2,1,0:T(8,128)(2,1)} %refs_6_.1), custom_call_target="tpu_custom_call" | custom-call | bytes 2719744 | tf_op jit(solution)/shard_map/pallas_call | solution.py:25
  1.4 0.0 copy-start.3
  1.4 0.0 copy-start
  1.4 3.0 %collective-permute-start.14 = (bf16[512,512]{1,0:T(8,128)(2,1)S(1)}, bf16[512,512]{1,0:T(8,128)(2,1)S(1)}, u32[]{:S(2)}, u32[]{:S(2)}) collective-permute-start(bf16[512,512]{1,0:T(8,128)(2,1)S(1)} %get-tuple-element.38.refs_9_), channel_id=1, source_target_pairs={{0,8},{1,17},{2,10},{3,19},{4,12},{5,21},{6,14},{7,23},{8,0},{9,25... | collective-permute-start | bytes 1572872 | tf_op jit(solution)/shard_map/ppermute | solution.py:194
  4.4 1.5 %collective-permute-start.15 = (bf16[512,512]{1,0:T(8,128)(2,1)S(1)}, bf16[512,512]{1,0:T(8,128)(2,1)S(1)}, u32[]{:S(2)}, u32[]{:S(2)}) collective-permute-start(bf16[512,512]{1,0:T(8,128)(2,1)S(1)} %get-tuple-element.38.refs_9_), channel_id=1, source_target_pairs={{0,16},{1,9},{2,18},{3,11},{4,20},{5,13},{6,22},{7,15},{8,24},{9,1... | collective-permute-start | bytes 1572872 | tf_op jit(solution)/shard_map/ppermute | solution.py:194
  5.9 10.7 %collective-permute-done.14.refs_10_ = bf16[512,512]{1,0:T(8,128)(2,1)S(1)} collective-permute-done((bf16[512,512]{1,0:T(8,128)(2,1)S(1)}, bf16[512,512]{1,0:T(8,128)(2,1)S(1)}, u32[]{:S(2)}, u32[]{:S(2)}) %collective-permute-start.14) | collective-permute-done | bytes 524320 | tf_op jit(solution)/shard_map/ppermute | solution.py:194
  16.6 1.6 %collective-permute-start.16 = (bf16[512,512]{1,0:T(8,128)(2,1)S(1)}, bf16[512,512]{1,0:T(8,128)(2,1)S(1)}, u32[]{:S(2)}, u32[]{:S(2)}) collective-permute-start(bf16[512,512]{1,0:T(8,128)(2,1)S(1)} %collective-permute-done.14.refs_10_), channel_id=1, source_target_pairs={{0,16},{1,9},{2,18},{3,11},{4,20},{5,13},{6,22},{7,15},{8,24},{9,1... | collective-permute-start | bytes 1572872 | tf_op jit(solution)/shard_map/ppermute | solution.py:194
  18.2 2.4 %collective-permute-start.2 = (bf16[128,128]{1,0:T(8,128)(2,1)S(1)}, bf16[128,128]{1,0:T(8,128)(2,1)S(1)}, u32[]{:S(2)}, u32[]{:S(2)}) collective-permute-start(bf16[128,128]{1,0:T(8,128)(2,1)S(1)} %get-tuple-element.27.refs_0_), channel_id=1, source_target_pairs={{0,24},{8,16},{16,8},{24,0},{1,25},{9,17},{17,9},{25,1},{2,26},{10... | collective-permute-start | bytes 98312 | tf_op jit(solution)/shard_map/ppermute | solution.py:190
  20.6 0.7 %collective-permute-start.1 = (bf16[128,128]{1,0:T(8,128)(2,1)S(1)}, bf16[128,128]{1,0:T(8,128)(2,1)S(1)}, u32[]{:S(2)}, u32[]{:S(2)}) collective-permute-start(bf16[128,128]{1,0:T(8,128)(2,1)S(1)} %get-tuple-element.27.refs_0_), channel_id=1, source_target_pairs={{0,16},{8,24},{16,0},{24,8},{1,17},{9,25},{17,1},{25,9},{2,18},{10... | collective-permute-start | bytes 98312 | tf_op jit(solution)/shard_map/ppermute | solution.py:190
  21.3 0.4 collective-permute-start
  21.7 1.7 %collective-permute-done.2.refs_3_ = bf16[128,128]{1,0:T(8,128)(2,1)S(1)} collective-permute-done((bf16[128,128]{1,0:T(8,128)(2,1)S(1)}, bf16[128,128]{1,0:T(8,128)(2,1)S(1)}, u32[]{:S(2)}, u32[]{:S(2)}) %collective-permute-start.2) | collective-permute-done | bytes 32800 | tf_op jit(solution)/shard_map/ppermute | solution.py:190
  23.3 3.5 %collective-permute-done.1.refs_2_ = bf16[128,128]{1,0:T(8,128)(2,1)S(1)} collective-permute-done((bf16[128,128]{1,0:T(8,128)(2,1)S(1)}, bf16[128,128]{1,0:T(8,128)(2,1)S(1)}, u32[]{:S(2)}, u32[]{:S(2)}) %collective-permute-start.1) | collective-permute-done | bytes 32800 | tf_op jit(solution)/shard_map/ppermute | solution.py:190
  26.9 0.0 collective-permute-done.refs_1_
  26.9 0.0 copy-done.1
  26.9 0.0 copy-done.2
  26.9 1.2 %shard_map.47 = (bf16[128,128]{1,0:T(8,128)(2,1)S(1)}, bf16[32,768]{1,0:T(8,128)(2,1)S(1)}, bf16[32,768]{1,0:T(8,128)(2,1)S(1)}, bf16[32,768]{1,0:T(8,128)(2,1)S(1)}, bf16[32,768]{1,0:T(8,128)(2,1)S(1)}) custom-call(bf16[128,128]{1,0:T(8,128)(2,1)S(1)} %get-tuple-element.27.refs_0_, bf16[128,128]{1,0:T(8,128)(2,1)S(1)} %collective-permute-done.refs_1_, ...), custom_call_target="tpu_custom_call" | custom-call | flops 134217728 | bytes 1802240 | tf_op jit(solution)/shard_map/pallas_call | solution.py:25
  28.1 2.5 %collective-permute-start.3 = (bf16[32,768]{1,0:T(8,128)(2,1)S(1)}, bf16[32,768]{1,0:T(8,128)(2,1)S(1)}, u32[]{:S(2)}, u32[]{:S(2)}) collective-permute-start(bf16[32,768]{1,0:T(8,128)(2,1)S(1)} %get-tuple-element.31), channel_id=1, source_target_pairs={{0,8},{8,0},{16,24},{24,16},{1,9},{9,1},{17,25},{25,17},{2,10},{10... | collective-permute-start | bytes 147464 | tf_op jit(solution)/shard_map/ppermute | solution.py:190
  30.6 0.0 copy-done.3
  30.6 0.0 collective-permute-start.6
  30.6 0.7 %collective-permute-start.4 = (bf16[32,768]{1,0:T(8,128)(2,1)S(1)}, bf16[32,768]{1,0:T(8,128)(2,1)S(1)}, u32[]{:S(2)}, u32[]{:S(2)}) collective-permute-start(bf16[32,768]{1,0:T(8,128)(2,1)S(1)} %get-tuple-element.32), channel_id=1, source_target_pairs={{0,16},{8,24},{16,0},{24,8},{1,17},{9,25},{17,1},{25,9},{2,18},{10... | collective-permute-start | bytes 147464 | tf_op jit(solution)/shard_map/ppermute | solution.py:190
  31.4 0.4 collective-permute-done.6.far_targets
  31.8 0.5 collective-permute-start.5
  32.3 0.4 collective-permute-done.3.refs_1_
  32.7 0.0 collective-permute-start.7
  32.7 2.1 %collective-permute-done.4.refs_2_ = bf16[32,768]{1,0:T(8,128)(2,1)S(1)} collective-permute-done((bf16[32,768]{1,0:T(8,128)(2,1)S(1)}, bf16[32,768]{1,0:T(8,128)(2,1)S(1)}, u32[]{:S(2)}, u32[]{:S(2)}) %collective-permute-start.4) | collective-permute-done | bytes 49184 | tf_op jit(solution)/shard_map/ppermute | solution.py:190
  34.8 0.0 collective-permute-start.8
  34.8 2.0 %collective-permute-done.5.refs_3_ = bf16[32,768]{1,0:T(8,128)(2,1)S(1)} collective-permute-done((bf16[32,768]{1,0:T(8,128)(2,1)S(1)}, bf16[32,768]{1,0:T(8,128)(2,1)S(1)}, u32[]{:S(2)}, u32[]{:S(2)}) %collective-permute-start.5) | collective-permute-done | bytes 49184 | tf_op jit(solution)/shard_map/ppermute | solution.py:190
  36.8 0.0 collective-permute-start.9
  36.8 0.0 collective-permute-done.7.refs_4_.refs_8_
  36.8 0.5 collective-permute-start.10
  37.3 0.0 collective-permute-done.8.refs_5_.refs_9_
  37.3 0.7 %collective-permute-done.9.refs_6_.refs_10_ = bf16[32,768]{1,0:T(8,128)(2,1)S(1)} collective-permute-done((bf16[32,768]{1,0:T(8,128)(2,1)S(1)}, bf16[32,768]{1,0:T(8,128)(2,1)S(1)}, u32[]{:S(2)}, u32[]{:S(2)}) %collective-permute-start.9) | collective-permute-done | bytes 49184 | tf_op jit(solution)/shard_map/ppermute | solution.py:200
  38.0 0.2 collective-permute-done.10.refs_7_.refs_11_
  38.2 0.8 %shard_map.48 = (bf16[32,512]{1,0:T(8,128)(2,1)S(1)}, bf16[32,512]{1,0:T(8,128)(2,1)S(1)}, bf16[32,512]{1,0:T(8,128)(2,1)S(1)}, bf16[32,512]{1,0:T(8,128)(2,1)S(1)}) custom-call(s32[2,1,4]{2,1,0:T(1,128)S(1)} %copy-done.3, s32[2,1,4]{2,1,0:T(1,128)S(1)} %collective-permute-done.6.far_targets, bf16[32,768]{1,0:T(8,128)(2,1)S(1)} %get-tuple-element.30.refs_0_, ...), custom_call_target="tpu_custom_call" | custom-call | bytes 393280 | tf_op jit(solution)/shard_map/pallas_call | solution.py:25
  39.0 1.6 %collective-permute-start.11 = (bf16[32,512]{1,0:T(8,128)(2,1)S(1)}, bf16[32,512]{1,0:T(8,128)(2,1)S(1)}, u32[]{:S(2)}, u32[]{:S(2)}) collective-permute-start(bf16[32,512]{1,0:T(8,128)(2,1)S(1)} %get-tuple-element.35), channel_id=1, source_target_pairs={{0,2},{1,3},{2,0},{3,1},{4,6},{5,7},{6,4},{7,5},{8,10},{9,11},{10,... | collective-permute-start | bytes 98312 | tf_op jit(solution)/shard_map/ppermute | solution.py:197
  40.6 2.6 %collective-permute-start.12 = (bf16[32,512]{1,0:T(8,128)(2,1)S(1)}, bf16[32,512]{1,0:T(8,128)(2,1)S(1)}, u32[]{:S(2)}, u32[]{:S(2)}) collective-permute-start(bf16[32,512]{1,0:T(8,128)(2,1)S(1)} %get-tuple-element.36), channel_id=1, source_target_pairs={{0,4},{1,5},{2,6},{3,7},{4,0},{5,1},{6,2},{7,3},{8,12},{9,13},{10,... | collective-permute-start | bytes 98312 | tf_op jit(solution)/shard_map/ppermute | solution.py:197
  43.2 0.2 collective-permute-start.13
  43.4 0.0 collective-permute-done.11.refs_5_
  43.4 2.6 %collective-permute-done.12.refs_6_ = bf16[32,512]{1,0:T(8,128)(2,1)S(1)} collective-permute-done((bf16[32,512]{1,0:T(8,128)(2,1)S(1)}, bf16[32,512]{1,0:T(8,128)(2,1)S(1)}, u32[]{:S(2)}, u32[]{:S(2)}) %collective-permute-start.12) | collective-permute-done | bytes 32800 | tf_op jit(solution)/shard_map/ppermute | solution.py:197
  46.0 2.9 %collective-permute-done.13.refs_7_ = bf16[32,512]{1,0:T(8,128)(2,1)S(1)} collective-permute-done((bf16[32,512]{1,0:T(8,128)(2,1)S(1)}, bf16[32,512]{1,0:T(8,128)(2,1)S(1)}, u32[]{:S(2)}, u32[]{:S(2)}) %collective-permute-start.13) | collective-permute-done | bytes 32800 | tf_op jit(solution)/shard_map/ppermute | solution.py:197
  48.9 0.0 collective-permute-done.15.refs_11_
  48.9 0.0 collective-permute-done.16.refs_12_
  48.9 0.0 copy-done
  48.9 0.9 %shard_map.49 = (bf16[32,512]{1,0:T(8,128)(2,1)S(1)}, bf16[4,32,512]{2,1,0:T(8,128)(2,1)S(1)}) custom-call(bf16[32,768]{1,0:T(8,128)(2,1)S(1)} %get-tuple-element.30.refs_0_, bf16[32,768]{1,0:T(8,128)(2,1)S(1)} %collective-permute-done.3.refs_1_, bf16[32,768]{1,0:T(8,128)(2,1)S(1)} %collective-permute-done.4.refs_2_, ...), custom_call_target="tpu_custom_call" | custom-call | flops 83886080 | bytes 3997696 | tf_op jit(solution)/shard_map/pallas_call | solution.py:25
  49.8 0.0 collective-permute-start.17
  49.9 1.3 %collective-permute-done.17.refs_12_.refs_13_.refs_14_.refs_15_ = bf16[4,32,512]{2,1,0:T(8,128)(2,1)S(1)} collective-permute-done((bf16[4,32,512]{2,1,0:T(8,128)(2,1)S(1)}, bf16[4,32,512]{2,1,0:T(8,128)(2,1)S(1)}, u32[]{:S(2)}, u32[]{:S(2)}) %collective-permute-start.17) | collective-permute-done | bytes 131104 | tf_op jit(solution)/shard_map/ppermute | solution.py:200
  51.2 1.0 %shard_map.50 = (bf16[32,512]{1,0:T(8,128)(2,1)S(1)}, bf16[32,512]{1,0:T(8,128)(2,1)S(1)}, bf16[32,512]{1,0:T(8,128)(2,1)S(1)}, bf16[32,512]{1,0:T(8,128)(2,1)S(1)}) custom-call(s32[2,1,4]{2,1,0:T(1,128)S(1)} %copy-done.3, s32[2,1,4]{2,1,0:T(1,128)S(1)} %collective-permute-done.6.far_targets, bf16[32,768]{1,0:T(8,128)(2,1)S(1)} %get-tuple-element.30.refs_0_, ...), custom_call_target="tpu_custom_call" | custom-call | bytes 1441856 | tf_op jit(solution)/shard_map/pallas_call | solution.py:25
  52.2 0.1 collective-permute-start.18
  52.3 1.0 %collective-permute-start.19 = (bf16[32,512]{1,0:T(8,128)(2,1)S(1)}, bf16[32,512]{1,0:T(8,128)(2,1)S(1)}, u32[]{:S(2)}, u32[]{:S(2)}) collective-permute-start(bf16[32,512]{1,0:T(8,128)(2,1)S(1)} %get-tuple-element.42), channel_id=1, source_target_pairs={{0,4},{1,5},{2,6},{3,7},{4,0},{5,1},{6,2},{7,3},{8,12},{9,13},{10,... | collective-permute-start | bytes 98312 | tf_op jit(solution)/shard_map/ppermute | solution.py:197
  53.2 3.4 %collective-permute-start.20 = (bf16[32,512]{1,0:T(8,128)(2,1)S(1)}, bf16[32,512]{1,0:T(8,128)(2,1)S(1)}, u32[]{:S(2)}, u32[]{:S(2)}) collective-permute-start(bf16[32,512]{1,0:T(8,128)(2,1)S(1)} %get-tuple-element.43), channel_id=1, source_target_pairs={{0,6},{1,7},{2,4},{3,5},{4,2},{5,3},{6,0},{7,1},{8,14},{9,15},{10,... | collective-permute-start | bytes 98312 | tf_op jit(solution)/shard_map/ppermute | solution.py:197
  56.7 0.0 collective-permute-done.18.refs_5_
  56.7 0.5 collective-permute-done.19.refs_6_
  57.2 1.8 %collective-permute-done.20.refs_7_ = bf16[32,512]{1,0:T(8,128)(2,1)S(1)} collective-permute-done((bf16[32,512]{1,0:T(8,128)(2,1)S(1)}, bf16[32,512]{1,0:T(8,128)(2,1)S(1)}, u32[]{:S(2)}, u32[]{:S(2)}) %collective-permute-start.20) | collective-permute-done | bytes 32800 | tf_op jit(solution)/shard_map/ppermute | solution.py:197
  59.0 0.3 shard_map.51
  59.3 0.6 collective-permute-start.21
  59.9 0.9 %collective-permute-start.22 = (bf16[2,32,128]{2,1,0:T(8,128)(2,1)S(1)}, bf16[2,32,128]{2,1,0:T(8,128)(2,1)S(1)}, u32[]{:S(2)}, u32[]{:S(2)}) collective-permute-start(bf16[2,32,128]{2,1,0:T(8,128)(2,1)S(1)} %get-tuple-element.47), channel_id=1, source_target_pairs={{0,16},{8,24},{16,0},{24,8},{1,17},{9,25},{17,1},{25,9},{2,18},{10... | collective-permute-start | bytes 49160 | tf_op jit(solution)/shard_map/ppermute | solution.py:190
  60.7 2.1 %collective-permute-start.23 = (bf16[2,32,128]{2,1,0:T(8,128)(2,1)S(1)}, bf16[2,32,128]{2,1,0:T(8,128)(2,1)S(1)}, u32[]{:S(2)}, u32[]{:S(2)}) collective-permute-start(bf16[2,32,128]{2,1,0:T(8,128)(2,1)S(1)} %get-tuple-element.48), channel_id=1, source_target_pairs={{0,24},{8,16},{16,8},{24,0},{1,25},{9,17},{17,9},{25,1},{2,26},{10... | collective-permute-start | bytes 49160 | tf_op jit(solution)/shard_map/ppermute | solution.py:190
  62.8 0.2 collective-permute-done.21.refs_2_
  63.1 0.5 collective-permute-done.22.refs_3_
  63.6 1.8 %collective-permute-done.23.refs_4_ = bf16[2,32,128]{2,1,0:T(8,128)(2,1)S(1)} collective-permute-done((bf16[2,32,128]{2,1,0:T(8,128)(2,1)S(1)}, bf16[2,32,128]{2,1,0:T(8,128)(2,1)S(1)}, u32[]{:S(2)}, u32[]{:S(2)}) %collective-permute-start.23) | collective-permute-done | bytes 16416 | tf_op jit(solution)/shard_map/ppermute | solution.py:190
  65.4 0.8 %shard_map.52 = bf16[3,1,128,128]{3,2,1,0:T(8,128)(2,1)} custom-call(bf16[128,128]{1,0:T(8,128)(2,1)S(1)} %get-tuple-element.29.refs_0_, bf16[2,32,128]{2,1,0:T(8,128)(2,1)S(1)} %get-tuple-element.45.refs_1_, bf16[2,32,128]{2,1,0:T(8,128)(2,1)S(1)} %collective-permute-done.21.refs_2_, bf16[2,32,128]{2,1,0:T(8,128)(2,1)S(1)} %collective-permute-done.22.refs_3_, ...), custom_call_target="tpu_custom_call" | custom-call | bytes 98304 | tf_op jit(solution)/shard_map/pallas_call | solution.py:25
Async XLA Ops:
  0.0 26.9 %copy-start.1 = (bf16[2,1,1,512,512]{4,3,2,1,0:T(8,128)(2,1)S(1)}, bf16[2,1,1,512,512]{4,3,2,1,0:T(8,128)(2,1)}, u32[]{:S(2)}) copy-start(bf16[2,1,1,512,512]{4,3,2,1,0:T(8,128)(2,1)} %refs_6_.1) | copy-start | bytes 3145732
  0.0 26.9 %copy-start.2 = (bf16[3,1,128,128]{3,2,1,0:T(8,128)(2,1)S(1)}, bf16[3,1,128,128]{3,2,1,0:T(8,128)(2,1)}, u32[]{:S(2)}) copy-start(bf16[3,1,128,128]{3,2,1,0:T(8,128)(2,1)} %refs_5_.1) | copy-start | bytes 294916
  1.4 29.3 %copy-start.3 = (s32[2,1,4]{2,1,0:T(1,128)S(1)}, s32[2,1,4]{2,1,0:T(1,128)}, u32[]{:S(2)}) copy-start(s32[2,1,4]{2,1,0:T(1,128)} %own_targets.3) | copy-start | bytes 100
  1.4 47.5 %copy-start = (bf16[3,1,512,512]{3,2,1,0:T(8,128)(2,1)S(1)}, bf16[3,1,512,512]{3,2,1,0:T(8,128)(2,1)}, u32[]{:S(2)}) copy-start(bf16[3,1,512,512]{3,2,1,0:T(8,128)(2,1)} %refs_8_.3) | copy-start | bytes 4718596
  1.4 15.2 %collective-permute-start.14 = (bf16[512,512]{1,0:T(8,128)(2,1)S(1)}, bf16[512,512]{1,0:T(8,128)(2,1)S(1)}, u32[]{:S(2)}, u32[]{:S(2)}) collective-permute-start(bf16[512,512]{1,0:T(8,128)(2,1)S(1)} %get-tuple-element.38.refs_9_), channel_id=1, source_target_pairs={{0,8},{1,17},{2,10},{3,19},{4,12},{5,21},{6,14},{7,23},{8,0},{9,25... | collective-permute-start | bytes 1572872 | tf_op jit(solution)/shard_map/ppermute | solution.py:194
  4.4 44.5 %collective-permute-start.15 = (bf16[512,512]{1,0:T(8,128)(2,1)S(1)}, bf16[512,512]{1,0:T(8,128)(2,1)S(1)}, u32[]{:S(2)}, u32[]{:S(2)}) collective-permute-start(bf16[512,512]{1,0:T(8,128)(2,1)S(1)} %get-tuple-element.38.refs_9_), channel_id=1, source_target_pairs={{0,16},{1,9},{2,18},{3,11},{4,20},{5,13},{6,22},{7,15},{8,24},{9,1... | collective-permute-start | bytes 1572872 | tf_op jit(solution)/shard_map/ppermute | solution.py:194
  16.6 32.3 %collective-permute-start.16 = (bf16[512,512]{1,0:T(8,128)(2,1)S(1)}, bf16[512,512]{1,0:T(8,128)(2,1)S(1)}, u32[]{:S(2)}, u32[]{:S(2)}) collective-permute-start(bf16[512,512]{1,0:T(8,128)(2,1)S(1)} %collective-permute-done.14.refs_10_), channel_id=1, source_target_pairs={{0,16},{1,9},{2,18},{3,11},{4,20},{5,13},{6,22},{7,15},{8,24},{9,1... | collective-permute-start | bytes 1572872 | tf_op jit(solution)/shard_map/ppermute | solution.py:194
  18.2 5.2 %collective-permute-start.2 = (bf16[128,128]{1,0:T(8,128)(2,1)S(1)}, bf16[128,128]{1,0:T(8,128)(2,1)S(1)}, u32[]{:S(2)}, u32[]{:S(2)}) collective-permute-start(bf16[128,128]{1,0:T(8,128)(2,1)S(1)} %get-tuple-element.27.refs_0_), channel_id=1, source_target_pairs={{0,24},{8,16},{16,8},{24,0},{1,25},{9,17},{17,9},{25,1},{2,26},{10... | collective-permute-start | bytes 98312 | tf_op jit(solution)/shard_map/ppermute | solution.py:190
  20.6 6.3 %collective-permute-start.1 = (bf16[128,128]{1,0:T(8,128)(2,1)S(1)}, bf16[128,128]{1,0:T(8,128)(2,1)S(1)}, u32[]{:S(2)}, u32[]{:S(2)}) collective-permute-start(bf16[128,128]{1,0:T(8,128)(2,1)S(1)} %get-tuple-element.27.refs_0_), channel_id=1, source_target_pairs={{0,16},{8,24},{16,0},{24,8},{1,17},{9,25},{17,1},{25,9},{2,18},{10... | collective-permute-start | bytes 98312 | tf_op jit(solution)/shard_map/ppermute | solution.py:190
  21.3 5.6 %collective-permute-start = (bf16[128,128]{1,0:T(8,128)(2,1)S(1)}, bf16[128,128]{1,0:T(8,128)(2,1)S(1)}, u32[]{:S(2)}, u32[]{:S(2)}) collective-permute-start(bf16[128,128]{1,0:T(8,128)(2,1)S(1)} %get-tuple-element.27.refs_0_), channel_id=1, source_target_pairs={{0,8},{8,0},{16,24},{24,16},{1,9},{9,1},{17,25},{25,17},{2,10},{10... | collective-permute-start | bytes 98312 | tf_op jit(solution)/shard_map/ppermute | solution.py:190
  28.1 4.6 %collective-permute-start.3 = (bf16[32,768]{1,0:T(8,128)(2,1)S(1)}, bf16[32,768]{1,0:T(8,128)(2,1)S(1)}, u32[]{:S(2)}, u32[]{:S(2)}) collective-permute-start(bf16[32,768]{1,0:T(8,128)(2,1)S(1)} %get-tuple-element.31), channel_id=1, source_target_pairs={{0,8},{8,0},{16,24},{24,16},{1,9},{9,1},{17,25},{25,17},{2,10},{10... | collective-permute-start | bytes 147464 | tf_op jit(solution)/shard_map/ppermute | solution.py:190
  30.6 1.2 %collective-permute-start.6 = (s32[2,1,4]{2,1,0:T(1,128)S(1)}, s32[2,1,4]{2,1,0:T(1,128)S(1)}, u32[]{:S(2)}, u32[]{:S(2)}) collective-permute-start(s32[2,1,4]{2,1,0:T(1,128)S(1)} %copy-done.3), channel_id=1, source_target_pairs={{0,1},{1,0},{2,3},{3,2},{4,5},{5,4},{6,7},{7,6},{8,9},{9,8},{10,11... | collective-permute-start | bytes 104 | tf_op jit(solution)/shard_map/ppermute | solution.py:200
  30.6 4.2 %collective-permute-start.4 = (bf16[32,768]{1,0:T(8,128)(2,1)S(1)}, bf16[32,768]{1,0:T(8,128)(2,1)S(1)}, u32[]{:S(2)}, u32[]{:S(2)}) collective-permute-start(bf16[32,768]{1,0:T(8,128)(2,1)S(1)} %get-tuple-element.32), channel_id=1, source_target_pairs={{0,16},{8,24},{16,0},{24,8},{1,17},{9,25},{17,1},{25,9},{2,18},{10... | collective-permute-start | bytes 147464 | tf_op jit(solution)/shard_map/ppermute | solution.py:190
  31.8 5.0 %collective-permute-start.5 = (bf16[32,768]{1,0:T(8,128)(2,1)S(1)}, bf16[32,768]{1,0:T(8,128)(2,1)S(1)}, u32[]{:S(2)}, u32[]{:S(2)}) collective-permute-start(bf16[32,768]{1,0:T(8,128)(2,1)S(1)} %get-tuple-element.33), channel_id=1, source_target_pairs={{0,24},{8,16},{16,8},{24,0},{1,25},{9,17},{17,9},{25,1},{2,26},{10... | collective-permute-start | bytes 147464 | tf_op jit(solution)/shard_map/ppermute | solution.py:190
  32.7 4.1 %collective-permute-start.7 = (bf16[32,768]{1,0:T(8,128)(2,1)S(1)}, bf16[32,768]{1,0:T(8,128)(2,1)S(1)}, u32[]{:S(2)}, u32[]{:S(2)}) collective-permute-start(bf16[32,768]{1,0:T(8,128)(2,1)S(1)} %get-tuple-element.30.refs_0_), channel_id=1, source_target_pairs={{0,1},{1,0},{2,3},{3,2},{4,5},{5,4},{6,7},{7,6},{8,9},{9,8},{10,11... | collective-permute-start | bytes 147464 | tf_op jit(solution)/shard_map/ppermute | solution.py:200
  34.8 2.5 %collective-permute-start.8 = (bf16[32,768]{1,0:T(8,128)(2,1)S(1)}, bf16[32,768]{1,0:T(8,128)(2,1)S(1)}, u32[]{:S(2)}, u32[]{:S(2)}) collective-permute-start(bf16[32,768]{1,0:T(8,128)(2,1)S(1)} %collective-permute-done.3.refs_1_), channel_id=1, source_target_pairs={{0,1},{1,0},{2,3},{3,2},{4,5},{5,4},{6,7},{7,6},{8,9},{9,8},{10,11... | collective-permute-start | bytes 147464 | tf_op jit(solution)/shard_map/ppermute | solution.py:200
  36.8 1.2 %collective-permute-start.9 = (bf16[32,768]{1,0:T(8,128)(2,1)S(1)}, bf16[32,768]{1,0:T(8,128)(2,1)S(1)}, u32[]{:S(2)}, u32[]{:S(2)}) collective-permute-start(bf16[32,768]{1,0:T(8,128)(2,1)S(1)} %collective-permute-done.4.refs_2_), channel_id=1, source_target_pairs={{0,1},{1,0},{2,3},{3,2},{4,5},{5,4},{6,7},{7,6},{8,9},{9,8},{10,11... | collective-permute-start | bytes 147464 | tf_op jit(solution)/shard_map/ppermute | solution.py:200
  36.8 1.4 %collective-permute-start.10 = (bf16[32,768]{1,0:T(8,128)(2,1)S(1)}, bf16[32,768]{1,0:T(8,128)(2,1)S(1)}, u32[]{:S(2)}, u32[]{:S(2)}) collective-permute-start(bf16[32,768]{1,0:T(8,128)(2,1)S(1)} %collective-permute-done.5.refs_3_), channel_id=1, source_target_pairs={{0,1},{1,0},{2,3},{3,2},{4,5},{5,4},{6,7},{7,6},{8,9},{9,8},{10,11... | collective-permute-start | bytes 147464 | tf_op jit(solution)/shard_map/ppermute | solution.py:200
  39.0 4.5 %collective-permute-start.11 = (bf16[32,512]{1,0:T(8,128)(2,1)S(1)}, bf16[32,512]{1,0:T(8,128)(2,1)S(1)}, u32[]{:S(2)}, u32[]{:S(2)}) collective-permute-start(bf16[32,512]{1,0:T(8,128)(2,1)S(1)} %get-tuple-element.35), channel_id=1, source_target_pairs={{0,2},{1,3},{2,0},{3,1},{4,6},{5,7},{6,4},{7,5},{8,10},{9,11},{10,... | collective-permute-start | bytes 98312 | tf_op jit(solution)/shard_map/ppermute | solution.py:197
  40.6 5.4 %collective-permute-start.12 = (bf16[32,512]{1,0:T(8,128)(2,1)S(1)}, bf16[32,512]{1,0:T(8,128)(2,1)S(1)}, u32[]{:S(2)}, u32[]{:S(2)}) collective-permute-start(bf16[32,512]{1,0:T(8,128)(2,1)S(1)} %get-tuple-element.36), channel_id=1, source_target_pairs={{0,4},{1,5},{2,6},{3,7},{4,0},{5,1},{6,2},{7,3},{8,12},{9,13},{10,... | collective-permute-start | bytes 98312 | tf_op jit(solution)/shard_map/ppermute | solution.py:197
  43.2 5.7 %collective-permute-start.13 = (bf16[32,512]{1,0:T(8,128)(2,1)S(1)}, bf16[32,512]{1,0:T(8,128)(2,1)S(1)}, u32[]{:S(2)}, u32[]{:S(2)}) collective-permute-start(bf16[32,512]{1,0:T(8,128)(2,1)S(1)} %get-tuple-element.37), channel_id=1, source_target_pairs={{0,6},{1,7},{2,4},{3,5},{4,2},{5,3},{6,0},{7,1},{8,14},{9,15},{10,... | collective-permute-start | bytes 98312 | tf_op jit(solution)/shard_map/ppermute | solution.py:197
  49.8 1.4 %collective-permute-start.17 = (bf16[4,32,512]{2,1,0:T(8,128)(2,1)S(1)}, bf16[4,32,512]{2,1,0:T(8,128)(2,1)S(1)}, u32[]{:S(2)}, u32[]{:S(2)}) collective-permute-start(bf16[4,32,512]{2,1,0:T(8,128)(2,1)S(1)} %get-tuple-element.39.refs_4_.refs_5_.refs_6_.refs_7_), channel_id=1, source_target_pairs={{0,1},{1,0},{2,3},{3,2},{4,5},{5,4},{6,7},{7,6},{8,9},{9,8},{10,11... | collective-permute-start | bytes 393224 | tf_op jit(solution)/shard_map/ppermute | solution.py:200
  52.2 4.5 %collective-permute-start.18 = (bf16[32,512]{1,0:T(8,128)(2,1)S(1)}, bf16[32,512]{1,0:T(8,128)(2,1)S(1)}, u32[]{:S(2)}, u32[]{:S(2)}) collective-permute-start(bf16[32,512]{1,0:T(8,128)(2,1)S(1)} %get-tuple-element.41), channel_id=1, source_target_pairs={{0,2},{1,3},{2,0},{3,1},{4,6},{5,7},{6,4},{7,5},{8,10},{9,11},{10,... | collective-permute-start | bytes 98312 | tf_op jit(solution)/shard_map/ppermute | solution.py:197
  52.3 4.9 %collective-permute-start.19 = (bf16[32,512]{1,0:T(8,128)(2,1)S(1)}, bf16[32,512]{1,0:T(8,128)(2,1)S(1)}, u32[]{:S(2)}, u32[]{:S(2)}) collective-permute-start(bf16[32,512]{1,0:T(8,128)(2,1)S(1)} %get-tuple-element.42), channel_id=1, source_target_pairs={{0,4},{1,5},{2,6},{3,7},{4,0},{5,1},{6,2},{7,3},{8,12},{9,13},{10,... | collective-permute-start | bytes 98312 | tf_op jit(solution)/shard_map/ppermute | solution.py:197
  53.2 5.7 %collective-permute-start.20 = (bf16[32,512]{1,0:T(8,128)(2,1)S(1)}, bf16[32,512]{1,0:T(8,128)(2,1)S(1)}, u32[]{:S(2)}, u32[]{:S(2)}) collective-permute-start(bf16[32,512]{1,0:T(8,128)(2,1)S(1)} %get-tuple-element.43), channel_id=1, source_target_pairs={{0,6},{1,7},{2,4},{3,5},{4,2},{5,3},{6,0},{7,1},{8,14},{9,15},{10,... | collective-permute-start | bytes 98312 | tf_op jit(solution)/shard_map/ppermute | solution.py:197
  59.3 3.8 %collective-permute-start.21 = (bf16[2,32,128]{2,1,0:T(8,128)(2,1)S(1)}, bf16[2,32,128]{2,1,0:T(8,128)(2,1)S(1)}, u32[]{:S(2)}, u32[]{:S(2)}) collective-permute-start(bf16[2,32,128]{2,1,0:T(8,128)(2,1)S(1)} %get-tuple-element.46), channel_id=1, source_target_pairs={{0,8},{8,0},{16,24},{24,16},{1,9},{9,1},{17,25},{25,17},{2,10},{10... | collective-permute-start | bytes 49160 | tf_op jit(solution)/shard_map/ppermute | solution.py:190
  59.9 3.7 %collective-permute-start.22 = (bf16[2,32,128]{2,1,0:T(8,128)(2,1)S(1)}, bf16[2,32,128]{2,1,0:T(8,128)(2,1)S(1)}, u32[]{:S(2)}, u32[]{:S(2)}) collective-permute-start(bf16[2,32,128]{2,1,0:T(8,128)(2,1)S(1)} %get-tuple-element.47), channel_id=1, source_target_pairs={{0,16},{8,24},{16,0},{24,8},{1,17},{9,25},{17,1},{25,9},{2,18},{10... | collective-permute-start | bytes 49160 | tf_op jit(solution)/shard_map/ppermute | solution.py:190
  60.7 4.6 %collective-permute-start.23 = (bf16[2,32,128]{2,1,0:T(8,128)(2,1)S(1)}, bf16[2,32,128]{2,1,0:T(8,128)(2,1)S(1)}, u32[]{:S(2)}, u32[]{:S(2)}) collective-permute-start(bf16[2,32,128]{2,1,0:T(8,128)(2,1)S(1)} %get-tuple-element.48), channel_id=1, source_target_pairs={{0,24},{8,16},{16,8},{24,0},{1,25},{9,17},{17,9},{25,1},{2,26},{10... | collective-permute-start | bytes 49160 | tf_op jit(solution)/shard_map/ppermute | solution.py:190

commit v2 on v1

--- a/solution.py
+++ b/solution.py
@@ -18,7 +18,7 @@
     return [(i, i ^ step) for i in range(size)]
 
 
-def call(kernel, out_shapes, operands, scalars=0, placed=0, scratch=(), flops=0):
+def call(kernel, out_shapes, operands, scalars=0, placed=0, out_space=pltpu.VMEM, scratch=(), flops=0):
     vmem = pl.BlockSpec(memory_space=pltpu.VMEM)
     smem = pl.BlockSpec(memory_space=pltpu.SMEM)
     moved = sum(x.size * x.dtype.itemsize for x in operands)
@@ -26,18 +26,17 @@
         kernel,
         out_shape=out_shapes,
         in_specs=[smem] * scalars + [vmem] * (len(operands) - scalars - placed) + [pl.BlockSpec(memory_space=pltpu.HBM if placed == len(operands) else pl.ANY)] * placed,
-        out_specs=[vmem] * len(out_shapes),
+        out_specs=[pl.BlockSpec(memory_space=out_space)] * len(out_shapes),
         scratch_shapes=list(scratch),
         compiler_params=pltpu.CompilerParams(vmem_limit_bytes=GRANT),
         cost_estimate=pl.CostEstimate(flops=flops, bytes_accessed=moved, transcendentals=0),
     )(*operands)
 
 
-def load_kernel(later, rhs, inverse, off, first, *refs):
-    blocks, top, done = refs[: later - 1], refs[later - 1], refs[later]
-    copies = [(rhs.at[0, 0], first), (inverse.at[0, 0], top)]
-    copies += [(off.at[level + 1, 0, 0], block) for level, block in enumerate(blocks)]
-    copies = [pltpu.make_async_copy(*ends, done.at[at]) for at, ends in enumerate(copies)]
+def load_kernel(places, *refs):
+    done = refs[-1]
+    outs = refs[len(refs) - 1 - len(places) : -1]
+    copies = [pltpu.make_async_copy(refs[at].at[place], out, done.at[i]) for i, ((at, place), out) in enumerate(zip(places, outs))]
     for copy in copies:
         copy.start()
     for copy in copies:
@@ -48,11 +47,7 @@
     shares = refs[:rows]
     inverse, rhs, off, kept = refs[rows : rows + 4]
     messages = refs[rows + 4 : 2 * rows + 4]
-    whole, turned, turned_rest, rest, block, arrived = refs[2 * rows + 4 :]
-    block_copy = pltpu.make_async_copy(off.at[0, 0, 0], block, arrived.at[0])
-    rest_copy = pltpu.make_async_copy(rhs.at[pl.ds(1, later), 0], rest, arrived.at[1])
-    block_copy.start()
-    rest_copy.start()
+    whole, turned, turned_rest = refs[2 * rows + 4 :]
     part, vectors = shares[0].shape
     size = inverse.shape[-1]
     each = vectors // rows
@@ -62,12 +57,10 @@
     solved = jnp.dot(inverse[...], whole[...], preferred_element_type=F32).astype(BF16)
     whole[...] = solved
     kept[...] = whole[pl.ds(pl.multiple_of(me * part, part), part), :]
-    block_copy.wait()
-    product = jnp.dot(block[...], solved, preferred_element_type=F32)
+    product = jnp.dot(off[0, 0, 0], solved, preferred_element_type=F32)
     turned[...] = product.T
-    rest_copy.wait()
     for level in range(later):
-        turned_rest[level] = rest[level].astype(F32).T
+        turned_rest[level] = rhs[level + 1, 0].astype(F32).T
     for step in range(rows):
         at = pl.ds(pl.multiple_of((me ^ step) * each, each), each)
         messages[step][:, :size] = turned[at, :].astype(BF16)
@@ -76,23 +69,58 @@
             messages[step][:, low : low + part] = turned_rest[level, at, :].astype(BF16)
 
 
-def slots_kernel(half, level, sources, own_targets, far_targets, *refs):
+def slot_of(targets, source, turns, odd, half, level):
+    me_col = lax.axis_index("pcol")
+    turn = turns[0] if turns[0] == turns[1] else jnp.where(odd == 1, turns[1], turns[0])
+    column = targets[source, 0, lax.axis_index("prow") ^ turn] - level * 2 * half
+    wanted = (column >= 0) & (column < 2 * half) & ((column & 1) == (me_col & 1))
+    return wanted, (column >> 1) ^ (me_col >> 1)
+
+
+def weights_kernel(half, level, turns, own_targets, far_targets, out):
+    parity = lax.axis_index("pcol") & 1
+    for group, (targets, odd) in enumerate(((own_targets, parity), (far_targets, 1 - parity))):
+        for at, turn in enumerate(turns):
+            wanted, slot = slot_of(targets, level, turn, odd, half, level)
+            for step in range(half):
+                value = jnp.where(wanted & (slot == step), 1.0, 0.0).astype(F32)
+                out[group * len(turns) + at, step] = jnp.full(out.shape[2:], value, F32)
+
+
+def earlier_kernel(half, level, sources, own_targets, far_targets, *refs):
     own = refs[: len(sources)]
     far = refs[len(sources) : 2 * len(sources)]
-    outs = refs[2 * len(sources) :]
+    total = refs[-1]
+    size = total.shape[2]
+    parity = lax.axis_index("pcol") & 1
+    total[...] = jnp.zeros_like(total)
+
+    def add(wanted, slot, at, ref):
+        @pl.when(wanted)
+        def _():
+            value = ref[:, :size] if at is None else ref[at]
+            total[slot] += value.astype(F32)
+
+    for targets, group, odd in ((own_targets, own, parity), (far_targets, far, 1 - parity)):
+        for (source, turns, at), ref in zip(sources, group):
+            add(*slot_of(targets, source, turns, odd, half, level), at, ref)
+
+
+def slots_kernel(half, places, weights, *refs):
+    products = refs[: len(places)]
+    outs = refs[-half:]
+    before = refs[len(places) : -half]
     each, size = outs[0].shape
-    me_row = lax.axis_index("prow")
-    me_col = lax.axis_index("pcol")
-    for step in range(half):
-        column = (me_col ^ (2 * step)) + level * 2 * half
-        total = jnp.zeros((each, size), F32)
-        for targets, group, odd in ((own_targets, own, me_col % 2), (far_targets, far, 1 - me_col % 2)):
-            for (source, turns, at), ref in zip(sources, group):
-                value = ref[:, :size] if at is None else ref[at]
-                turn = turns[0] if turns[0] == turns[1] else jnp.where(odd == 1, turns[1], turns[0])
-                hit = targets[source, 0, me_row ^ turn] == column
-                total = total + jnp.where(hit, value.astype(F32), 0.0)
-        outs[step][...] = total.astype(outs[step].dtype)
+    chunk = min(16, each)
+    for low in range(0, each, chunk):
+        at_rows = pl.ds(low, chunk)
+        totals = [before[0][step, at_rows, :] if before else jnp.zeros((chunk, size), F32) for step in range(half)]
+        for number, (at, ref) in enumerate(zip(places, products)):
+            value = (ref[at_rows, :size] if at is None else ref[at, at_rows, :]).astype(F32)
+            for step in range(half):
+                totals[step] = totals[step] + value * jnp.tile(weights[number, step], (chunk // 8, size // 128))
+        for step in range(half):
+            outs[step][at_rows, :] = totals[step].astype(outs[step].dtype)
 
 
 def residual(rows, level, messages, arrived, out):
@@ -166,15 +194,20 @@
 def output_kernel(rows, later, *refs):
     kept = refs[0]
     pieces = refs[1 : rows + 1]
-    out, scratch = refs[rows + 1 :]
+    out, scratch, turned, done = refs[rows + 1 :]
     _, each, _ = pieces[0].shape
     me = lax.axis_index("prow")
-    out[0, 0] = kept[...]
+    copies = [pltpu.make_async_copy(kept, out.at[0, 0], done.at[0])]
+    copies[0].start()
     for level in range(later):
         for step in range(rows):
             at = pl.ds(pl.multiple_of((me ^ step) * each, each), each)
-            scratch[at, :] = pieces[step][level].astype(F32)
-        out[level + 1, 0] = scratch[...].T.astype(BF16)
+            scratch[level, at, :] = pieces[step][level].astype(F32)
+        turned[level] = scratch[level].T.astype(BF16)
+        copies.append(pltpu.make_async_copy(turned.at[level], out.at[level + 1, 0], done.at[level + 1]))
+        copies[-1].start()
+    for copy in copies:
+        copy.wait()
 
 
 def local(rhs, inverse, off, targets):
@@ -200,27 +233,32 @@
         return lax.ppermute(x, "pcol", pairs(columns, 1))
 
     far_targets = flip(targets)
-    first, *owned, top = call(
-        functools.partial(load_kernel, later),
-        [shape((part, vectors), BF16)] + [shape((size, size), BF16)] * later,
-        [pltpu.with_memory_space_constraint(x, pltpu.HBM) for x in (rhs, inverse, off)],
-        placed=3,
-        scratch=[pltpu.SemaphoreType.DMA((later + 1,))],
-    )
+
+    def load(places, out_shapes, operands):
+        return call(
+            functools.partial(load_kernel, places),
+            out_shapes,
+            [pltpu.with_memory_space_constraint(x, pltpu.HBM) for x in operands],
+            placed=len(operands),
+            scratch=[pltpu.SemaphoreType.DMA((len(places),))],
+        )
+
+    first, *owned = load(
+        [(0, (0, 0))] + [(1, (level, 0, 0)) for level in range(1, later)],
+        [shape((part, vectors), BF16)] + [shape((size, size), BF16)] * (later - 1),
+        [rhs, off],
+    )
+    (top,) = load([(0, (0, 0))], [shape((size, size), BF16)], [inverse])
     shares = [over_rows(first, step) for step in range(rows)]
     width = size + later * part
     kept, *sent = call(
         functools.partial(first_kernel, rows, later),
         [shape((part, vectors), BF16)] + [shape((each, width), BF16)] * rows,
         [*shares, top, rhs, off],
-        placed=2,
         scratch=[
             pltpu.VMEM((size, vectors), BF16),
             pltpu.VMEM((vectors, size), F32),
             pltpu.VMEM((later, vectors, part), F32),
-            pltpu.VMEM((later, part, vectors), BF16),
-            pltpu.VMEM((size, size), BF16),
-            pltpu.SemaphoreType.DMA((2,)),
         ],
         flops=4 * size * size * vectors,
     )
@@ -237,14 +275,29 @@
         steps += [(even ^ turn[0], odd ^ turn[1]) for even, odd in steps]
 
     own, far = list(messages), list(far_messages)
-    sources = [(0, (step, step), None) for step in range(rows)]
+    places = [None] * (2 * rows)
+    turns = [(step, step) for step in range(rows)]
+    past = []
     solved = []
     for level in range(1, levels):
+        (weights,) = call(
+            functools.partial(weights_kernel, half, level - 1, tuple(turns)),
+            [shape((2 * rows, half, 8, 128), F32)],
+            [targets, far_targets],
+            scalars=2,
+        )
+        before = []
+        if past:
+            before = call(
+                functools.partial(earlier_kernel, half, level - 1, tuple(x[0] for x in past)),
+                [shape((half, each, size), F32)],
+                [targets, far_targets, *(x[1] for x in past), *(x[2] for x in past)],
+                scalars=2,
+            )
         out = call(
-            functools.partial(slots_kernel, half, level - 1, tuple(sources)),
+            functools.partial(slots_kernel, half, tuple(places)),
             [shape((each, size), BF16)] * half,
-            [targets, far_targets, *own, *far],
-            scalars=2,
+            [weights, *own, *far, *before],
         )
         arrived = [over_pairs(x, step) for step, x in enumerate(out)]
         if level < later:
@@ -257,9 +310,8 @@
             )
             solved.append(value)
             far_products = flip(products)
-            own += [products] * rows
-            far += [far_products] * rows
-            sources += [(level, turns, at) for at, turns in enumerate(steps)]
+            past += list(zip([(level - 1, turn, at) for turn, at in zip(turns, places)], own, far))
+            own, far, turns, places = [products] * rows, [far_products] * rows, steps, [*range(rows)] * 2
     pieces = call(
         functools.partial(last_kernel, rows, half, later, len(solved)),
         [shape((later, each, part), BF16)] * rows,
@@ -272,7 +324,8 @@
         functools.partial(output_kernel, rows, later),
         [shape((levels, 1, part, vectors), BF16)],
         [kept, *pieces],
-        scratch=[pltpu.VMEM((vectors, part), F32)],
+        out_space=pl.ANY,
+        scratch=[pltpu.VMEM((later, vectors, part), F32), pltpu.VMEM((later, part, vectors), BF16), pltpu.SemaphoreType.DMA((levels,))],
     )
     return out
 

time: 66.3 us -> 64.4 us (0.971)
  waiting for transfers between devices: 33.3 us -> 29.7 us
  Pallas kernels: 6.3 us -> 7.33 us
    ppermute x9, waiting for transfers between devices: 12.2 us -> 10.2 us  [over_rows(): return lax.ppermute(x, 'prow', pairs(rows, step)) if step else x]
    ppermute x6, waiting for transfers between devices: 2.64 us -> 1.03 us  [flip(): return lax.ppermute(x, 'pcol', pairs(columns, 1))]
    pallas_call x7 -> x11, Pallas kernels: 6.3 us -> 7.33 us  [call(): pl.pallas_call(kernel, out_shape=out_shapes, in_specs=[smem] * scalars +...]
  transfers between devices with their start and end apart: 24 -> 24, of which waited for: 17 -> 14; matrix products, arithmetic and copies ran while one was open for 0% -> 0% of each run, Pallas kernels for 3% -> 6%
where the time goes in v2:
time: 64.4 us; the launch traced here: 64.2 us
  waiting for transfers between devices  29.7 us (46%)
  starting transfers between devices  27 us (42%)
  Pallas kernels  7.33 us (11%)
    ppermute x9, starting transfers between devices, over_rows(): return lax.ppermute(x, 'prow', pairs(rows, step)) if step else x  11.4 us
    ppermute x3, waiting for transfers between devices, over_turns(): return lax.ppermute(x, ('prow', 'pcol'), links)  10.7 us
    ppermute x9, waiting for transfers between devices, over_rows(): return lax.ppermute(x, 'prow', pairs(rows, step)) if step else x  10.2 us
    ppermute x6, starting transfers between devices, over_pairs(): return lax.ppermute(x, 'pcol', pairs(columns, 2 * step)) if step else x  8.9 us
    ppermute x6, waiting for transfers between devices, over_pairs(): return lax.ppermute(x, 'pcol', pairs(columns, 2 * step)) if step else x  7.79 us
    pallas_call x11, Pallas kernels, call(): pl.pallas_call(kernel, out_shape=out_shapes, in_specs=[smem] * scalars +...  7.33 us
    ppermute x3, starting transfers between devices, over_turns(): return lax.ppermute(x, ('prow', 'pcol'), links)  6.11 us
  transfers between devices with their start and end apart: 24, of which 14 were waited for; matrix products, arithmetic and copies ran while one was open for 0% of the time, Pallas kernels for 6%

profile of v2, /device:TPU:0, one launch (start us, length us, event | category | flops | bytes accessed | tf_op | source)
XLA Modules:
  0.0 64.2 jit_solution(15386714682162385102)
XLA Ops:
  0.0 1.2 %shard_map.46 = (bf16[128,128]{1,0:T(8,128)(2,1)S(1)}, bf16[512,512]{1,0:T(8,128)(2,1)S(1)}) custom-call(bf16[3,1,128,128]{3,2,1,0:T(8,128)(2,1)} %refs_5_.1, bf16[2,1,1,512,512]{4,3,2,1,0:T(8,128)(2,1)} %refs_6_.1), custom_call_target="tpu_custom_call" | custom-call | bytes 1146880 | tf_op jit(solution)/shard_map/pallas_call | solution.py:25
  1.2 3.0 %collective-permute-start.14 = (bf16[512,512]{1,0:T(8,128)(2,1)S(1)}, bf16[512,512]{1,0:T(8,128)(2,1)S(1)}, u32[]{:S(2)}, u32[]{:S(2)}) collective-permute-start(bf16[512,512]{1,0:T(8,128)(2,1)S(1)} %get-tuple-element.36.refs_9_), channel_id=1, source_target_pairs={{0,8},{1,17},{2,10},{3,19},{4,12},{5,21},{6,14},{7,23},{8,0},{9,25... | collective-permute-start | bytes 1572872 | tf_op jit(solution)/shard_map/ppermute | solution.py:227
  4.2 1.5 %collective-permute-start.15 = (bf16[512,512]{1,0:T(8,128)(2,1)S(1)}, bf16[512,512]{1,0:T(8,128)(2,1)S(1)}, u32[]{:S(2)}, u32[]{:S(2)}) collective-permute-start(bf16[512,512]{1,0:T(8,128)(2,1)S(1)} %get-tuple-element.36.refs_9_), channel_id=1, source_target_pairs={{0,16},{1,9},{2,18},{3,11},{4,20},{5,13},{6,22},{7,15},{8,24},{9,1... | collective-permute-start | bytes 1572872 | tf_op jit(solution)/shard_map/ppermute | solution.py:227
  5.7 10.7 %collective-permute-done.14.refs_10_ = bf16[512,512]{1,0:T(8,128)(2,1)S(1)} collective-permute-done((bf16[512,512]{1,0:T(8,128)(2,1)S(1)}, bf16[512,512]{1,0:T(8,128)(2,1)S(1)}, u32[]{:S(2)}, u32[]{:S(2)}) %collective-permute-start.14) | collective-permute-done | bytes 524320 | tf_op jit(solution)/shard_map/ppermute | solution.py:227
  16.4 1.6 %collective-permute-start.16 = (bf16[512,512]{1,0:T(8,128)(2,1)S(1)}, bf16[512,512]{1,0:T(8,128)(2,1)S(1)}, u32[]{:S(2)}, u32[]{:S(2)}) collective-permute-start(bf16[512,512]{1,0:T(8,128)(2,1)S(1)} %collective-permute-done.14.refs_10_), channel_id=1, source_target_pairs={{0,16},{1,9},{2,18},{3,11},{4,20},{5,13},{6,22},{7,15},{8,24},{9,1... | collective-permute-start | bytes 1572872 | tf_op jit(solution)/shard_map/ppermute | solution.py:227
  18.0 1.6 %collective-permute-start = (bf16[128,128]{1,0:T(8,128)(2,1)S(1)}, bf16[128,128]{1,0:T(8,128)(2,1)S(1)}, u32[]{:S(2)}, u32[]{:S(2)}) collective-permute-start(bf16[128,128]{1,0:T(8,128)(2,1)S(1)} %get-tuple-element.26.refs_0_), channel_id=1, source_target_pairs={{0,8},{8,0},{16,24},{24,16},{1,9},{9,1},{17,25},{25,17},{2,10},{10... | collective-permute-start | bytes 98312 | tf_op jit(solution)/shard_map/ppermute | solution.py:223
  19.6 1.3 %collective-permute-start.1 = (bf16[128,128]{1,0:T(8,128)(2,1)S(1)}, bf16[128,128]{1,0:T(8,128)(2,1)S(1)}, u32[]{:S(2)}, u32[]{:S(2)}) collective-permute-start(bf16[128,128]{1,0:T(8,128)(2,1)S(1)} %get-tuple-element.26.refs_0_), channel_id=1, source_target_pairs={{0,16},{8,24},{16,0},{24,8},{1,17},{9,25},{17,1},{25,9},{2,18},{10... | collective-permute-start | bytes 98312 | tf_op jit(solution)/shard_map/ppermute | solution.py:223
  20.9 0.5 collective-permute-start.2
  21.5 1.0 %shard_map.47.refs_4_ = bf16[512,512]{1,0:T(8,128)(2,1)S(1)} custom-call(bf16[3,1,512,512]{3,2,1,0:T(8,128)(2,1)} %refs_8_.3), custom_call_target="tpu_custom_call" | custom-call | bytes 1572864 | tf_op jit(solution)/shard_map/pallas_call | solution.py:25
  22.5 0.0 copy-start
  22.5 0.0 collective-permute-done.refs_1_
  22.6 4.1 %collective-permute-done.1.refs_2_ = bf16[128,128]{1,0:T(8,128)(2,1)S(1)} collective-permute-done((bf16[128,128]{1,0:T(8,128)(2,1)S(1)}, bf16[128,128]{1,0:T(8,128)(2,1)S(1)}, u32[]{:S(2)}, u32[]{:S(2)}) %collective-permute-start.1) | collective-permute-done | bytes 32800 | tf_op jit(solution)/shard_map/ppermute | solution.py:223
  26.7 0.0 collective-permute-done.2.refs_3_
  26.7 0.0 copy-done.2
  26.7 0.0 copy-done.1
  26.7 0.9 %shard_map.48 = (bf16[128,128]{1,0:T(8,128)(2,1)S(1)}, bf16[32,768]{1,0:T(8,128)(2,1)S(1)}, bf16[32,768]{1,0:T(8,128)(2,1)S(1)}, bf16[32,768]{1,0:T(8,128)(2,1)S(1)}, bf16[32,768]{1,0:T(8,128)(2,1)S(1)}) custom-call(bf16[128,128]{1,0:T(8,128)(2,1)S(1)} %get-tuple-element.26.refs_0_, bf16[128,128]{1,0:T(8,128)(2,1)S(1)} %collective-permute-done.refs_1_, ...), custom_call_target="tpu_custom_call" | custom-call | flops 134217728 | bytes 1802240 | tf_op jit(solution)/shard_map/pallas_call | solution.py:25
  27.5 2.7 %collective-permute-start.5 = (bf16[32,768]{1,0:T(8,128)(2,1)S(1)}, bf16[32,768]{1,0:T(8,128)(2,1)S(1)}, u32[]{:S(2)}, u32[]{:S(2)}) collective-permute-start(bf16[32,768]{1,0:T(8,128)(2,1)S(1)} %get-tuple-element.31), channel_id=1, source_target_pairs={{0,24},{8,16},{16,8},{24,0},{1,25},{9,17},{17,9},{25,1},{2,26},{10... | collective-permute-start | bytes 147464 | tf_op jit(solution)/shard_map/ppermute | solution.py:223
  30.3 0.0 copy-done.3
  30.3 0.0 collective-permute-start.6
  30.3 0.4 collective-permute-start.3
  30.6 0.8 %collective-permute-done.6.far_targets = s32[2,1,4]{2,1,0:T(1,128)S(1)} collective-permute-done((s32[2,1,4]{2,1,0:T(1,128)S(1)}, s32[2,1,4]{2,1,0:T(1,128)S(1)}, u32[]{:S(2)}, u32[]{:S(2)}) %collective-permute-start.6) | collective-permute-done | bytes 64 | tf_op jit(solution)/shard_map/ppermute | solution.py:233
  31.4 1.3 %collective-permute-start.4 = (bf16[32,768]{1,0:T(8,128)(2,1)S(1)}, bf16[32,768]{1,0:T(8,128)(2,1)S(1)}, u32[]{:S(2)}, u32[]{:S(2)}) collective-permute-start(bf16[32,768]{1,0:T(8,128)(2,1)S(1)} %get-tuple-element.30), channel_id=1, source_target_pairs={{0,16},{8,24},{16,0},{24,8},{1,17},{9,25},{17,1},{25,9},{2,18},{10... | collective-permute-start | bytes 147464 | tf_op jit(solution)/shard_map/ppermute | solution.py:223
  32.7 0.0 collective-permute-done.5.refs_3_
  32.7 0.0 collective-permute-start.7
  32.7 1.7 %collective-permute-done.3.refs_1_ = bf16[32,768]{1,0:T(8,128)(2,1)S(1)} collective-permute-done((bf16[32,768]{1,0:T(8,128)(2,1)S(1)}, bf16[32,768]{1,0:T(8,128)(2,1)S(1)}, u32[]{:S(2)}, u32[]{:S(2)}) %collective-permute-start.3) | collective-permute-done | bytes 49184 | tf_op jit(solution)/shard_map/ppermute | solution.py:223
  34.4 0.0 collective-permute-start.10
  34.4 1.1 %collective-permute-done.4.refs_2_ = bf16[32,768]{1,0:T(8,128)(2,1)S(1)} collective-permute-done((bf16[32,768]{1,0:T(8,128)(2,1)S(1)}, bf16[32,768]{1,0:T(8,128)(2,1)S(1)}, u32[]{:S(2)}, u32[]{:S(2)}) %collective-permute-start.4) | collective-permute-done | bytes 49184 | tf_op jit(solution)/shard_map/ppermute | solution.py:223
  35.5 0.0 collective-permute-start.8
  35.5 0.0 collective-permute-done.7.refs_4_
  35.5 0.5 collective-permute-start.9
  36.0 0.6 shard_map.50.weights
  36.7 0.0 collective-permute-done.10.refs_7_
  36.7 0.1 collective-permute-done.8.refs_5_
  36.7 0.2 collective-permute-done.9.refs_6_
  36.9 0.2 shard_map.51
  37.1 1.6 %collective-permute-start.11 = (bf16[32,512]{1,0:T(8,128)(2,1)S(1)}, bf16[32,512]{1,0:T(8,128)(2,1)S(1)}, u32[]{:S(2)}, u32[]{:S(2)}) collective-permute-start(bf16[32,512]{1,0:T(8,128)(2,1)S(1)} %get-tuple-element.33), channel_id=1, source_target_pairs={{0,2},{1,3},{2,0},{3,1},{4,6},{5,7},{6,4},{7,5},{8,10},{9,11},{10,... | collective-permute-start | bytes 98312 | tf_op jit(solution)/shard_map/ppermute | solution.py:230
  38.7 2.6 %collective-permute-start.12 = (bf16[32,512]{1,0:T(8,128)(2,1)S(1)}, bf16[32,512]{1,0:T(8,128)(2,1)S(1)}, u32[]{:S(2)}, u32[]{:S(2)}) collective-permute-start(bf16[32,512]{1,0:T(8,128)(2,1)S(1)} %get-tuple-element.34), channel_id=1, source_target_pairs={{0,4},{1,5},{2,6},{3,7},{4,0},{5,1},{6,2},{7,3},{8,12},{9,13},{10,... | collective-permute-start | bytes 98312 | tf_op jit(solution)/shard_map/ppermute | solution.py:230
  41.3 0.2 collective-permute-start.13
  41.5 0.0 collective-permute-done.11.refs_5_
  41.5 2.6 %collective-permute-done.12.refs_6_ = bf16[32,512]{1,0:T(8,128)(2,1)S(1)} collective-permute-done((bf16[32,512]{1,0:T(8,128)(2,1)S(1)}, bf16[32,512]{1,0:T(8,128)(2,1)S(1)}, u32[]{:S(2)}, u32[]{:S(2)}) %collective-permute-start.12) | collective-permute-done | bytes 32800 | tf_op jit(solution)/shard_map/ppermute | solution.py:230
  44.1 2.9 %collective-permute-done.13.refs_7_ = bf16[32,512]{1,0:T(8,128)(2,1)S(1)} collective-permute-done((bf16[32,512]{1,0:T(8,128)(2,1)S(1)}, bf16[32,512]{1,0:T(8,128)(2,1)S(1)}, u32[]{:S(2)}, u32[]{:S(2)}) %collective-permute-start.13) | collective-permute-done | bytes 32800 | tf_op jit(solution)/shard_map/ppermute | solution.py:230
  47.0 0.0 collective-permute-done.15.refs_11_
  47.0 0.0 collective-permute-done.16.refs_12_
  47.0 0.0 copy-done
  47.0 0.9 %shard_map.52 = (bf16[32,512]{1,0:T(8,128)(2,1)S(1)}, bf16[4,32,512]{2,1,0:T(8,128)(2,1)S(1)}) custom-call(bf16[32,768]{1,0:T(8,128)(2,1)S(1)} %get-tuple-element.28.refs_0_, bf16[32,768]{1,0:T(8,128)(2,1)S(1)} %collective-permute-done.3.refs_1_, bf16[32,768]{1,0:T(8,128)(2,1)S(1)} %collective-permute-done.4.refs_2_, ...), custom_call_target="tpu_custom_call" | custom-call | flops 83886080 | bytes 3997696 | tf_op jit(solution)/shard_map/pallas_call | solution.py:25
  47.9 0.0 collective-permute-start.17
  48.0 0.6 %shard_map.49.weights = f32[8,4,8,128]{3,2,1,0:T(8,128)S(1)} custom-call(s32[2,1,4]{2,1,0:T(1,128)S(1)} %copy-done.3, s32[2,1,4]{2,1,0:T(1,128)S(1)} %collective-permute-done.6.far_targets), custom_call_target="tpu_custom_call" | custom-call | bytes 64 | tf_op jit(solution)/shard_map/pallas_call | solution.py:25
  48.6 0.7 %shard_map.53.refs_8_ = f32[4,32,512]{2,1,0:T(8,128)S(1)} custom-call(s32[2,1,4]{2,1,0:T(1,128)S(1)} %copy-done.3, s32[2,1,4]{2,1,0:T(1,128)S(1)} %collective-permute-done.6.far_targets, bf16[32,768]{1,0:T(8,128)(2,1)S(1)} %get-tuple-element.28.refs_0_, bf16[32,768]{1,0:T(8,128)(2,1)S(1)} %collective-permute-done.3.refs_1_, ...), custom_call_target="tpu_custom_call" | custom-call | bytes 393280 | tf_op jit(solution)/shard_map/pallas_call | solution.py:25
  49.3 0.0 collective-permute-done.17.refs_4_.refs_5_.refs_6_.refs_7_
  49.3 0.2 shard_map.54
  49.5 0.1 collective-permute-start.18
  49.6 1.0 %collective-permute-start.19 = (bf16[32,512]{1,0:T(8,128)(2,1)S(1)}, bf16[32,512]{1,0:T(8,128)(2,1)S(1)}, u32[]{:S(2)}, u32[]{:S(2)}) collective-permute-start(bf16[32,512]{1,0:T(8,128)(2,1)S(1)} %get-tuple-element.40), channel_id=1, source_target_pairs={{0,4},{1,5},{2,6},{3,7},{4,0},{5,1},{6,2},{7,3},{8,12},{9,13},{10,... | collective-permute-start | bytes 98312 | tf_op jit(solution)/shard_map/ppermute | solution.py:230
  50.5 3.4 %collective-permute-start.20 = (bf16[32,512]{1,0:T(8,128)(2,1)S(1)}, bf16[32,512]{1,0:T(8,128)(2,1)S(1)}, u32[]{:S(2)}, u32[]{:S(2)}) collective-permute-start(bf16[32,512]{1,0:T(8,128)(2,1)S(1)} %get-tuple-element.41), channel_id=1, source_target_pairs={{0,6},{1,7},{2,4},{3,5},{4,2},{5,3},{6,0},{7,1},{8,14},{9,15},{10,... | collective-permute-start | bytes 98312 | tf_op jit(solution)/shard_map/ppermute | solution.py:230
  53.9 0.0 collective-permute-done.18.refs_5_
  53.9 0.7 %collective-permute-done.19.refs_6_ = bf16[32,512]{1,0:T(8,128)(2,1)S(1)} collective-permute-done((bf16[32,512]{1,0:T(8,128)(2,1)S(1)}, bf16[32,512]{1,0:T(8,128)(2,1)S(1)}, u32[]{:S(2)}, u32[]{:S(2)}) %collective-permute-start.19) | collective-permute-done | bytes 32800 | tf_op jit(solution)/shard_map/ppermute | solution.py:230
  54.7 1.6 %collective-permute-done.20.refs_7_ = bf16[32,512]{1,0:T(8,128)(2,1)S(1)} collective-permute-done((bf16[32,512]{1,0:T(8,128)(2,1)S(1)}, bf16[32,512]{1,0:T(8,128)(2,1)S(1)}, u32[]{:S(2)}, u32[]{:S(2)}) %collective-permute-start.20) | collective-permute-done | bytes 32800 | tf_op jit(solution)/shard_map/ppermute | solution.py:230
  56.2 0.3 shard_map.55
  56.5 1.1 %collective-permute-start.21 = (bf16[2,32,128]{2,1,0:T(8,128)(2,1)S(1)}, bf16[2,32,128]{2,1,0:T(8,128)(2,1)S(1)}, u32[]{:S(2)}, u32[]{:S(2)}) collective-permute-start(bf16[2,32,128]{2,1,0:T(8,128)(2,1)S(1)} %get-tuple-element.44), channel_id=1, source_target_pairs={{0,8},{8,0},{16,24},{24,16},{1,9},{9,1},{17,25},{25,17},{2,10},{10... | collective-permute-start | bytes 49160 | tf_op jit(solution)/shard_map/ppermute | solution.py:223
  57.7 1.1 %collective-permute-start.22 = (bf16[2,32,128]{2,1,0:T(8,128)(2,1)S(1)}, bf16[2,32,128]{2,1,0:T(8,128)(2,1)S(1)}, u32[]{:S(2)}, u32[]{:S(2)}) collective-permute-start(bf16[2,32,128]{2,1,0:T(8,128)(2,1)S(1)} %get-tuple-element.45), channel_id=1, source_target_pairs={{0,16},{8,24},{16,0},{24,8},{1,17},{9,25},{17,1},{25,9},{2,18},{10... | collective-permute-start | bytes 49160 | tf_op jit(solution)/shard_map/ppermute | solution.py:223
  58.8 1.3 %collective-permute-start.23 = (bf16[2,32,128]{2,1,0:T(8,128)(2,1)S(1)}, bf16[2,32,128]{2,1,0:T(8,128)(2,1)S(1)}, u32[]{:S(2)}, u32[]{:S(2)}) collective-permute-start(bf16[2,32,128]{2,1,0:T(8,128)(2,1)S(1)} %get-tuple-element.46), channel_id=1, source_target_pairs={{0,24},{8,16},{16,8},{24,0},{1,25},{9,17},{17,9},{25,1},{2,26},{10... | collective-permute-start | bytes 49160 | tf_op jit(solution)/shard_map/ppermute | solution.py:223
  60.1 0.3 collective-permute-done.21.refs_2_
  60.4 1.0 %collective-permute-done.22.refs_3_ = bf16[2,32,128]{2,1,0:T(8,128)(2,1)S(1)} collective-permute-done((bf16[2,32,128]{2,1,0:T(8,128)(2,1)S(1)}, bf16[2,32,128]{2,1,0:T(8,128)(2,1)S(1)}, u32[]{:S(2)}, u32[]{:S(2)}) %collective-permute-start.22) | collective-permute-done | bytes 16416 | tf_op jit(solution)/shard_map/ppermute | solution.py:223
  61.4 2.0 %collective-permute-done.23.refs_4_ = bf16[2,32,128]{2,1,0:T(8,128)(2,1)S(1)} collective-permute-done((bf16[2,32,128]{2,1,0:T(8,128)(2,1)S(1)}, bf16[2,32,128]{2,1,0:T(8,128)(2,1)S(1)}, u32[]{:S(2)}, u32[]{:S(2)}) %collective-permute-start.23) | collective-permute-done | bytes 16416 | tf_op jit(solution)/shard_map/ppermute | solution.py:223
  63.4 0.8 %shard_map.56 = bf16[3,1,128,128]{3,2,1,0:T(8,128)(2,1)} custom-call(bf16[128,128]{1,0:T(8,128)(2,1)S(1)} %get-tuple-element.27.refs_0_, bf16[2,32,128]{2,1,0:T(8,128)(2,1)S(1)} %get-tuple-element.43.refs_1_, bf16[2,32,128]{2,1,0:T(8,128)(2,1)S(1)} %collective-permute-done.21.refs_2_, bf16[2,32,128]{2,1,0:T(8,128)(2,1)S(1)} %collective-permute-done.22.refs_3_, ...), custom_call_target="tpu_custom_call" | custom-call | bytes 98304 | tf_op jit(solution)/shard_map/pallas_call | solution.py:25
  (3 shorter events, 0.0 us)
Async XLA Ops:
  0.0 26.7 %copy-start.2 = (bf16[3,1,128,128]{3,2,1,0:T(8,128)(2,1)S(1)}, bf16[3,1,128,128]{3,2,1,0:T(8,128)(2,1)}, u32[]{:S(2)}) copy-start(bf16[3,1,128,128]{3,2,1,0:T(8,128)(2,1)} %refs_5_.1) | copy-start | bytes 294916
  0.0 26.7 %copy-start.1 = (bf16[2,1,1,512,512]{4,3,2,1,0:T(8,128)(2,1)S(1)}, bf16[2,1,1,512,512]{4,3,2,1,0:T(8,128)(2,1)}, u32[]{:S(2)}) copy-start(bf16[2,1,1,512,512]{4,3,2,1,0:T(8,128)(2,1)} %refs_6_.1) | copy-start | bytes 3145732
  1.2 15.2 %collective-permute-start.14 = (bf16[512,512]{1,0:T(8,128)(2,1)S(1)}, bf16[512,512]{1,0:T(8,128)(2,1)S(1)}, u32[]{:S(2)}, u32[]{:S(2)}) collective-permute-start(bf16[512,512]{1,0:T(8,128)(2,1)S(1)} %get-tuple-element.36.refs_9_), channel_id=1, source_target_pairs={{0,8},{1,17},{2,10},{3,19},{4,12},{5,21},{6,14},{7,23},{8,0},{9,25... | collective-permute-start | bytes 1572872 | tf_op jit(solution)/shard_map/ppermute | solution.py:227
  4.2 42.8 %collective-permute-start.15 = (bf16[512,512]{1,0:T(8,128)(2,1)S(1)}, bf16[512,512]{1,0:T(8,128)(2,1)S(1)}, u32[]{:S(2)}, u32[]{:S(2)}) collective-permute-start(bf16[512,512]{1,0:T(8,128)(2,1)S(1)} %get-tuple-element.36.refs_9_), channel_id=1, source_target_pairs={{0,16},{1,9},{2,18},{3,11},{4,20},{5,13},{6,22},{7,15},{8,24},{9,1... | collective-permute-start | bytes 1572872 | tf_op jit(solution)/shard_map/ppermute | solution.py:227
  16.4 30.6 %collective-permute-start.16 = (bf16[512,512]{1,0:T(8,128)(2,1)S(1)}, bf16[512,512]{1,0:T(8,128)(2,1)S(1)}, u32[]{:S(2)}, u32[]{:S(2)}) collective-permute-start(bf16[512,512]{1,0:T(8,128)(2,1)S(1)} %collective-permute-done.14.refs_10_), channel_id=1, source_target_pairs={{0,16},{1,9},{2,18},{3,11},{4,20},{5,13},{6,22},{7,15},{8,24},{9,1... | collective-permute-start | bytes 1572872 | tf_op jit(solution)/shard_map/ppermute | solution.py:227
  18.0 12.3 %copy-start.3 = (s32[2,1,4]{2,1,0:T(1,128)S(1)}, s32[2,1,4]{2,1,0:T(1,128)}, u32[]{:S(2)}) copy-start(s32[2,1,4]{2,1,0:T(1,128)} %own_targets.5) | copy-start | bytes 100
  18.0 4.6 %collective-permute-start = (bf16[128,128]{1,0:T(8,128)(2,1)S(1)}, bf16[128,128]{1,0:T(8,128)(2,1)S(1)}, u32[]{:S(2)}, u32[]{:S(2)}) collective-permute-start(bf16[128,128]{1,0:T(8,128)(2,1)S(1)} %get-tuple-element.26.refs_0_), channel_id=1, source_target_pairs={{0,8},{8,0},{16,24},{24,16},{1,9},{9,1},{17,25},{25,17},{2,10},{10... | collective-permute-start | bytes 98312 | tf_op jit(solution)/shard_map/ppermute | solution.py:223
  19.6 7.0 %collective-permute-start.1 = (bf16[128,128]{1,0:T(8,128)(2,1)S(1)}, bf16[128,128]{1,0:T(8,128)(2,1)S(1)}, u32[]{:S(2)}, u32[]{:S(2)}) collective-permute-start(bf16[128,128]{1,0:T(8,128)(2,1)S(1)} %get-tuple-element.26.refs_0_), channel_id=1, source_target_pairs={{0,16},{8,24},{16,0},{24,8},{1,17},{9,25},{17,1},{25,9},{2,18},{10... | collective-permute-start | bytes 98312 | tf_op jit(solution)/shard_map/ppermute | solution.py:223
  20.9 5.7 %collective-permute-start.2 = (bf16[128,128]{1,0:T(8,128)(2,1)S(1)}, bf16[128,128]{1,0:T(8,128)(2,1)S(1)}, u32[]{:S(2)}, u32[]{:S(2)}) collective-permute-start(bf16[128,128]{1,0:T(8,128)(2,1)S(1)} %get-tuple-element.26.refs_0_), channel_id=1, source_target_pairs={{0,24},{8,16},{16,8},{24,0},{1,25},{9,17},{17,9},{25,1},{2,26},{10... | collective-permute-start | bytes 98312 | tf_op jit(solution)/shard_map/ppermute | solution.py:223
  22.5 24.5 %copy-start = (bf16[3,1,512,512]{3,2,1,0:T(8,128)(2,1)S(1)}, bf16[3,1,512,512]{3,2,1,0:T(8,128)(2,1)}, u32[]{:S(2)}) copy-start(bf16[3,1,512,512]{3,2,1,0:T(8,128)(2,1)} %refs_8_.3) | copy-start | bytes 4718596
  27.5 5.2 %collective-permute-start.5 = (bf16[32,768]{1,0:T(8,128)(2,1)S(1)}, bf16[32,768]{1,0:T(8,128)(2,1)S(1)}, u32[]{:S(2)}, u32[]{:S(2)}) collective-permute-start(bf16[32,768]{1,0:T(8,128)(2,1)S(1)} %get-tuple-element.31), channel_id=1, source_target_pairs={{0,24},{8,16},{16,8},{24,0},{1,25},{9,17},{17,9},{25,1},{2,26},{10... | collective-permute-start | bytes 147464 | tf_op jit(solution)/shard_map/ppermute | solution.py:223
  30.3 1.2 %collective-permute-start.6 = (s32[2,1,4]{2,1,0:T(1,128)S(1)}, s32[2,1,4]{2,1,0:T(1,128)S(1)}, u32[]{:S(2)}, u32[]{:S(2)}) collective-permute-start(s32[2,1,4]{2,1,0:T(1,128)S(1)} %copy-done.3), channel_id=1, source_target_pairs={{0,1},{1,0},{2,3},{3,2},{4,5},{5,4},{6,7},{7,6},{8,9},{9,8},{10,11... | collective-permute-start | bytes 104 | tf_op jit(solution)/shard_map/ppermute | solution.py:233
  30.3 4.2 %collective-permute-start.3 = (bf16[32,768]{1,0:T(8,128)(2,1)S(1)}, bf16[32,768]{1,0:T(8,128)(2,1)S(1)}, u32[]{:S(2)}, u32[]{:S(2)}) collective-permute-start(bf16[32,768]{1,0:T(8,128)(2,1)S(1)} %get-tuple-element.29), channel_id=1, source_target_pairs={{0,8},{8,0},{16,24},{24,16},{1,9},{9,1},{17,25},{25,17},{2,10},{10... | collective-permute-start | bytes 147464 | tf_op jit(solution)/shard_map/ppermute | solution.py:223
  31.4 4.1 %collective-permute-start.4 = (bf16[32,768]{1,0:T(8,128)(2,1)S(1)}, bf16[32,768]{1,0:T(8,128)(2,1)S(1)}, u32[]{:S(2)}, u32[]{:S(2)}) collective-permute-start(bf16[32,768]{1,0:T(8,128)(2,1)S(1)} %get-tuple-element.30), channel_id=1, source_target_pairs={{0,16},{8,24},{16,0},{24,8},{1,17},{9,25},{17,1},{25,9},{2,18},{10... | collective-permute-start | bytes 147464 | tf_op jit(solution)/shard_map/ppermute | solution.py:223
  32.7 2.8 %collective-permute-start.7 = (bf16[32,768]{1,0:T(8,128)(2,1)S(1)}, bf16[32,768]{1,0:T(8,128)(2,1)S(1)}, u32[]{:S(2)}, u32[]{:S(2)}) collective-permute-start(bf16[32,768]{1,0:T(8,128)(2,1)S(1)} %get-tuple-element.28.refs_0_), channel_id=1, source_target_pairs={{0,1},{1,0},{2,3},{3,2},{4,5},{5,4},{6,7},{7,6},{8,9},{9,8},{10,11... | collective-permute-start | bytes 147464 | tf_op jit(solution)/shard_map/ppermute | solution.py:233
  34.4 2.2 %collective-permute-start.10 = (bf16[32,768]{1,0:T(8,128)(2,1)S(1)}, bf16[32,768]{1,0:T(8,128)(2,1)S(1)}, u32[]{:S(2)}, u32[]{:S(2)}) collective-permute-start(bf16[32,768]{1,0:T(8,128)(2,1)S(1)} %collective-permute-done.5.refs_3_), channel_id=1, source_target_pairs={{0,1},{1,0},{2,3},{3,2},{4,5},{5,4},{6,7},{7,6},{8,9},{9,8},{10,11... | collective-permute-start | bytes 147464 | tf_op jit(solution)/shard_map/ppermute | solution.py:233
  35.5 1.2 %collective-permute-start.8 = (bf16[32,768]{1,0:T(8,128)(2,1)S(1)}, bf16[32,768]{1,0:T(8,128)(2,1)S(1)}, u32[]{:S(2)}, u32[]{:S(2)}) collective-permute-start(bf16[32,768]{1,0:T(8,128)(2,1)S(1)} %collective-permute-done.3.refs_1_), channel_id=1, source_target_pairs={{0,1},{1,0},{2,3},{3,2},{4,5},{5,4},{6,7},{7,6},{8,9},{9,8},{10,11... | collective-permute-start | bytes 147464 | tf_op jit(solution)/shard_map/ppermute | solution.py:233
  35.5 1.4 %collective-permute-start.9 = (bf16[32,768]{1,0:T(8,128)(2,1)S(1)}, bf16[32,768]{1,0:T(8,128)(2,1)S(1)}, u32[]{:S(2)}, u32[]{:S(2)}) collective-permute-start(bf16[32,768]{1,0:T(8,128)(2,1)S(1)} %collective-permute-done.4.refs_2_), channel_id=1, source_target_pairs={{0,1},{1,0},{2,3},{3,2},{4,5},{5,4},{6,7},{7,6},{8,9},{9,8},{10,11... | collective-permute-start | bytes 147464 | tf_op jit(solution)/shard_map/ppermute | solution.py:233
  37.1 4.5 %collective-permute-start.11 = (bf16[32,512]{1,0:T(8,128)(2,1)S(1)}, bf16[32,512]{1,0:T(8,128)(2,1)S(1)}, u32[]{:S(2)}, u32[]{:S(2)}) collective-permute-start(bf16[32,512]{1,0:T(8,128)(2,1)S(1)} %get-tuple-element.33), channel_id=1, source_target_pairs={{0,2},{1,3},{2,0},{3,1},{4,6},{5,7},{6,4},{7,5},{8,10},{9,11},{10,... | collective-permute-start | bytes 98312 | tf_op jit(solution)/shard_map/ppermute | solution.py:230
  38.7 5.4 %collective-permute-start.12 = (bf16[32,512]{1,0:T(8,128)(2,1)S(1)}, bf16[32,512]{1,0:T(8,128)(2,1)S(1)}, u32[]{:S(2)}, u32[]{:S(2)}) collective-permute-start(bf16[32,512]{1,0:T(8,128)(2,1)S(1)} %get-tuple-element.34), channel_id=1, source_target_pairs={{0,4},{1,5},{2,6},{3,7},{4,0},{5,1},{6,2},{7,3},{8,12},{9,13},{10,... | collective-permute-start | bytes 98312 | tf_op jit(solution)/shard_map/ppermute | solution.py:230
  41.3 5.7 %collective-permute-start.13 = (bf16[32,512]{1,0:T(8,128)(2,1)S(1)}, bf16[32,512]{1,0:T(8,128)(2,1)S(1)}, u32[]{:S(2)}, u32[]{:S(2)}) collective-permute-start(bf16[32,512]{1,0:T(8,128)(2,1)S(1)} %get-tuple-element.35), channel_id=1, source_target_pairs={{0,6},{1,7},{2,4},{3,5},{4,2},{5,3},{6,0},{7,1},{8,14},{9,15},{10,... | collective-permute-start | bytes 98312 | tf_op jit(solution)/shard_map/ppermute | solution.py:230
  47.9 1.4 %collective-permute-start.17 = (bf16[4,32,512]{2,1,0:T(8,128)(2,1)S(1)}, bf16[4,32,512]{2,1,0:T(8,128)(2,1)S(1)}, u32[]{:S(2)}, u32[]{:S(2)}) collective-permute-start(bf16[4,32,512]{2,1,0:T(8,128)(2,1)S(1)} %get-tuple-element.37.refs_0_.refs_1_.refs_2_.refs_3_), channel_id=1, source_target_pairs={{0,1},{1,0},{2,3},{3,2},{4,5},{5,4},{6,7},{7,6},{8,9},{9,8},{10,11... | collective-permute-start | bytes 393224 | tf_op jit(solution)/shard_map/ppermute | solution.py:233
  49.5 4.5 %collective-permute-start.18 = (bf16[32,512]{1,0:T(8,128)(2,1)S(1)}, bf16[32,512]{1,0:T(8,128)(2,1)S(1)}, u32[]{:S(2)}, u32[]{:S(2)}) collective-permute-start(bf16[32,512]{1,0:T(8,128)(2,1)S(1)} %get-tuple-element.39), channel_id=1, source_target_pairs={{0,2},{1,3},{2,0},{3,1},{4,6},{5,7},{6,4},{7,5},{8,10},{9,11},{10,... | collective-permute-start | bytes 98312 | tf_op jit(solution)/shard_map/ppermute | solution.py:230
  49.6 5.1 %collective-permute-start.19 = (bf16[32,512]{1,0:T(8,128)(2,1)S(1)}, bf16[32,512]{1,0:T(8,128)(2,1)S(1)}, u32[]{:S(2)}, u32[]{:S(2)}) collective-permute-start(bf16[32,512]{1,0:T(8,128)(2,1)S(1)} %get-tuple-element.40), channel_id=1, source_target_pairs={{0,4},{1,5},{2,6},{3,7},{4,0},{5,1},{6,2},{7,3},{8,12},{9,13},{10,... | collective-permute-start | bytes 98312 | tf_op jit(solution)/shard_map/ppermute | solution.py:230
  50.5 5.7 %collective-permute-start.20 = (bf16[32,512]{1,0:T(8,128)(2,1)S(1)}, bf16[32,512]{1,0:T(8,128)(2,1)S(1)}, u32[]{:S(2)}, u32[]{:S(2)}) collective-permute-start(bf16[32,512]{1,0:T(8,128)(2,1)S(1)} %get-tuple-element.41), channel_id=1, source_target_pairs={{0,6},{1,7},{2,4},{3,5},{4,2},{5,3},{6,0},{7,1},{8,14},{9,15},{10,... | collective-permute-start | bytes 98312 | tf_op jit(solution)/shard_map/ppermute | solution.py:230
  56.5 3.8 %collective-permute-start.21 = (bf16[2,32,128]{2,1,0:T(8,128)(2,1)S(1)}, bf16[2,32,128]{2,1,0:T(8,128)(2,1)S(1)}, u32[]{:S(2)}, u32[]{:S(2)}) collective-permute-start(bf16[2,32,128]{2,1,0:T(8,128)(2,1)S(1)} %get-tuple-element.44), channel_id=1, source_target_pairs={{0,8},{8,0},{16,24},{24,16},{1,9},{9,1},{17,25},{25,17},{2,10},{10... | collective-permute-start | bytes 49160 | tf_op jit(solution)/shard_map/ppermute | solution.py:223
  57.7 3.7 %collective-permute-start.22 = (bf16[2,32,128]{2,1,0:T(8,128)(2,1)S(1)}, bf16[2,32,128]{2,1,0:T(8,128)(2,1)S(1)}, u32[]{:S(2)}, u32[]{:S(2)}) collective-permute-start(bf16[2,32,128]{2,1,0:T(8,128)(2,1)S(1)} %get-tuple-element.45), channel_id=1, source_target_pairs={{0,16},{8,24},{16,0},{24,8},{1,17},{9,25},{17,1},{25,9},{2,18},{10... | collective-permute-start | bytes 49160 | tf_op jit(solution)/shard_map/ppermute | solution.py:223
  58.8 4.6 %collective-permute-start.23 = (bf16[2,32,128]{2,1,0:T(8,128)(2,1)S(1)}, bf16[2,32,128]{2,1,0:T(8,128)(2,1)S(1)}, u32[]{:S(2)}, u32[]{:S(2)}) collective-permute-start(bf16[2,32,128]{2,1,0:T(8,128)(2,1)S(1)} %get-tuple-element.46), channel_id=1, source_target_pairs={{0,24},{8,16},{16,8},{24,0},{1,25},{9,17},{17,9},{25,1},{2,26},{10... | collective-permute-start | bytes 49160 | tf_op jit(solution)/shard_map/ppermute | solution.py:223

commit v3 on v2

--- a/solution.py
+++ b/solution.py
@@ -57,7 +57,7 @@
     solved = jnp.dot(inverse[...], whole[...], preferred_element_type=F32).astype(BF16)
     whole[...] = solved
     kept[...] = whole[pl.ds(pl.multiple_of(me * part, part), part), :]
-    product = jnp.dot(off[0, 0, 0], solved, preferred_element_type=F32)
+    product = jnp.dot(off[...], solved, preferred_element_type=F32)
     turned[...] = product.T
     for level in range(later):
         turned_rest[level] = rhs[level + 1, 0].astype(F32).T
@@ -248,13 +248,13 @@
         [shape((part, vectors), BF16)] + [shape((size, size), BF16)] * (later - 1),
         [rhs, off],
     )
-    (top,) = load([(0, (0, 0))], [shape((size, size), BF16)], [inverse])
+    top, side = load([(0, (0, 0)), (1, (0, 0, 0))], [shape((size, size), BF16)] * 2, [inverse, off])
     shares = [over_rows(first, step) for step in range(rows)]
     width = size + later * part
     kept, *sent = call(
         functools.partial(first_kernel, rows, later),
         [shape((part, vectors), BF16)] + [shape((each, width), BF16)] * rows,
-        [*shares, top, rhs, off],
+        [*shares, top, rhs, side],
         scratch=[
             pltpu.VMEM((size, vectors), BF16),
             pltpu.VMEM((vectors, size), F32),
@@ -268,10 +268,10 @@
     blocks, steps = {}, [(0, 0)]
     for level in range(1, later):
         have = [owned[level - 1]]
-        for turn in zip(bits, bits[::-1]):
+        for turn in zip(bits[::-1], bits):
             have += [over_turns(x, turn) for x in have]
         blocks[level] = have
-    for turn in zip(bits, bits[::-1]):
+    for turn in zip(bits[::-1], bits):
         steps += [(even ^ turn[0], odd ^ turn[1]) for even, odd in steps]
 
     own, far = list(messages), list(far_messages)

time: 64.4 us -> 64.5 us (level)
  waiting for transfers between devices: 29.7 us -> 30.9 us
  starting transfers between devices: 27 us -> 25.9 us
    ppermute x9, starting transfers between devices: 11.4 us -> 10.3 us  [over_rows(): return lax.ppermute(x, 'prow', pairs(rows, step)) if step else x]
    ppermute x9, waiting for transfers between devices: 10.2 us -> 11.1 us  [over_rows(): return lax.ppermute(x, 'prow', pairs(rows, step)) if step else x]
  transfers between devices with their start and end apart: 24 -> 24, of which waited for: 14 -> 15; matrix products, arithmetic and copies ran while one was open for 0% -> 0% of each run, Pallas kernels for 6% -> 6%
where the time goes in v3:
time: 64.5 us; the launch traced here: 64.4 us
  waiting for transfers between devices  30.9 us (48%)
  starting transfers between devices  25.9 us (40%)
  Pallas kernels  7.4 us (11%)
    ppermute x9, waiting for transfers between devices, over_rows(): return lax.ppermute(x, 'prow', pairs(rows, step)) if step else x  11.1 us
    ppermute x3, waiting for transfers between devices, over_turns(): return lax.ppermute(x, ('prow', 'pcol'), links)  10.8 us
    ppermute x9, starting transfers between devices, over_rows(): return lax.ppermute(x, 'prow', pairs(rows, step)) if step else x  10.3 us
    ppermute x6, starting transfers between devices, over_pairs(): return lax.ppermute(x, 'pcol', pairs(columns, 2 * step)) if step else x  8.9 us
    ppermute x6, waiting for transfers between devices, over_pairs(): return lax.ppermute(x, 'pcol', pairs(columns, 2 * step)) if step else x  7.86 us
    pallas_call x11, Pallas kernels, call(): pl.pallas_call(kernel, out_shape=out_shapes, in_specs=[smem] * scalars +...  7.4 us
    ppermute x3, starting transfers between devices, over_turns(): return lax.ppermute(x, ('prow', 'pcol'), links)  6.02 us
  transfers between devices with their start and end apart: 24, of which 15 were waited for; matrix products, arithmetic and copies ran while one was open for 0% of the time, Pallas kernels for 6%

profile of v3, /device:TPU:0, one launch (start us, length us, event | category | flops | bytes accessed | tf_op | source)
XLA Modules:
  0.0 64.4 jit_solution(8953827502200200554)
XLA Ops:
  0.0 1.1 %shard_map.46 = (bf16[128,128]{1,0:T(8,128)(2,1)S(1)}, bf16[512,512]{1,0:T(8,128)(2,1)S(1)}) custom-call(bf16[3,1,128,128]{3,2,1,0:T(8,128)(2,1)} %refs_5_.1, bf16[2,1,1,512,512]{4,3,2,1,0:T(8,128)(2,1)} %refs_1_.3), custom_call_target="tpu_custom_call" | custom-call | bytes 1146880 | tf_op jit(solution)/shard_map/pallas_call | solution.py:25
  1.1 0.0 copy-start.1
  1.1 3.1 %collective-permute-start.14 = (bf16[512,512]{1,0:T(8,128)(2,1)S(1)}, bf16[512,512]{1,0:T(8,128)(2,1)S(1)}, u32[]{:S(2)}, u32[]{:S(2)}) collective-permute-start(bf16[512,512]{1,0:T(8,128)(2,1)S(1)} %get-tuple-element.40.refs_9_), channel_id=1, source_target_pairs={{0,16},{1,9},{2,18},{3,11},{4,20},{5,13},{6,22},{7,15},{8,24},{9,1... | collective-permute-start | bytes 1572872 | tf_op jit(solution)/shard_map/ppermute | solution.py:227
  4.2 1.5 %collective-permute-start.15 = (bf16[512,512]{1,0:T(8,128)(2,1)S(1)}, bf16[512,512]{1,0:T(8,128)(2,1)S(1)}, u32[]{:S(2)}, u32[]{:S(2)}) collective-permute-start(bf16[512,512]{1,0:T(8,128)(2,1)S(1)} %get-tuple-element.40.refs_9_), channel_id=1, source_target_pairs={{0,8},{1,17},{2,10},{3,19},{4,12},{5,21},{6,14},{7,23},{8,0},{9,25... | collective-permute-start | bytes 1572872 | tf_op jit(solution)/shard_map/ppermute | solution.py:227
  5.7 10.7 %collective-permute-done.14.refs_10_ = bf16[512,512]{1,0:T(8,128)(2,1)S(1)} collective-permute-done((bf16[512,512]{1,0:T(8,128)(2,1)S(1)}, bf16[512,512]{1,0:T(8,128)(2,1)S(1)}, u32[]{:S(2)}, u32[]{:S(2)}) %collective-permute-start.14) | collective-permute-done | bytes 524320 | tf_op jit(solution)/shard_map/ppermute | solution.py:227
  16.4 1.5 %collective-permute-start.16 = (bf16[512,512]{1,0:T(8,128)(2,1)S(1)}, bf16[512,512]{1,0:T(8,128)(2,1)S(1)}, u32[]{:S(2)}, u32[]{:S(2)}) collective-permute-start(bf16[512,512]{1,0:T(8,128)(2,1)S(1)} %collective-permute-done.14.refs_10_), channel_id=1, source_target_pairs={{0,8},{1,17},{2,10},{3,19},{4,12},{5,21},{6,14},{7,23},{8,0},{9,25... | collective-permute-start | bytes 1572872 | tf_op jit(solution)/shard_map/ppermute | solution.py:227
  17.9 0.6 collective-permute-start
  18.4 2.5 %collective-permute-start.1 = (bf16[128,128]{1,0:T(8,128)(2,1)S(1)}, bf16[128,128]{1,0:T(8,128)(2,1)S(1)}, u32[]{:S(2)}, u32[]{:S(2)}) collective-permute-start(bf16[128,128]{1,0:T(8,128)(2,1)S(1)} %get-tuple-element.28.refs_0_), channel_id=1, source_target_pairs={{0,16},{8,24},{16,0},{24,8},{1,17},{9,25},{17,1},{25,9},{2,18},{10... | collective-permute-start | bytes 98312 | tf_op jit(solution)/shard_map/ppermute | solution.py:223
  20.9 0.5 collective-permute-start.2
  21.4 1.2 %shard_map.47 = (bf16[512,512]{1,0:T(8,128)(2,1)S(1)}, bf16[512,512]{1,0:T(8,128)(2,1)S(1)}) custom-call(bf16[3,1,512,512]{3,2,1,0:T(8,128)(2,1)} %refs_8_.3, bf16[2,1,1,512,512]{4,3,2,1,0:T(8,128)(2,1)} %refs_1_.3), custom_call_target="tpu_custom_call" | custom-call | bytes 2621440 | tf_op jit(solution)/shard_map/pallas_call | solution.py:25
  22.6 0.0 copy-start
  22.6 3.7 %collective-permute-done.refs_1_ = bf16[128,128]{1,0:T(8,128)(2,1)S(1)} collective-permute-done((bf16[128,128]{1,0:T(8,128)(2,1)S(1)}, bf16[128,128]{1,0:T(8,128)(2,1)S(1)}, u32[]{:S(2)}, u32[]{:S(2)}) %collective-permute-start) | collective-permute-done | bytes 32800 | tf_op jit(solution)/shard_map/ppermute | solution.py:223
  26.3 0.0 collective-permute-done.1.refs_2_
  26.3 1.9 %collective-permute-done.2.refs_3_ = bf16[128,128]{1,0:T(8,128)(2,1)S(1)} collective-permute-done((bf16[128,128]{1,0:T(8,128)(2,1)S(1)}, bf16[128,128]{1,0:T(8,128)(2,1)S(1)}, u32[]{:S(2)}, u32[]{:S(2)}) %collective-permute-start.2) | collective-permute-done | bytes 32800 | tf_op jit(solution)/shard_map/ppermute | solution.py:223
  28.2 0.0 copy-done.1
  28.2 0.8 %shard_map.48 = (bf16[128,128]{1,0:T(8,128)(2,1)S(1)}, bf16[32,768]{1,0:T(8,128)(2,1)S(1)}, bf16[32,768]{1,0:T(8,128)(2,1)S(1)}, bf16[32,768]{1,0:T(8,128)(2,1)S(1)}, bf16[32,768]{1,0:T(8,128)(2,1)S(1)}) custom-call(bf16[128,128]{1,0:T(8,128)(2,1)S(1)} %get-tuple-element.28.refs_0_, bf16[128,128]{1,0:T(8,128)(2,1)S(1)} %collective-permute-done.refs_1_, ...), custom_call_target="tpu_custom_call" | custom-call | flops 134217728 | bytes 1277952 | tf_op jit(solution)/shard_map/pallas_call | solution.py:25
  29.1 0.9 %collective-permute-start.5 = (bf16[32,768]{1,0:T(8,128)(2,1)S(1)}, bf16[32,768]{1,0:T(8,128)(2,1)S(1)}, u32[]{:S(2)}, u32[]{:S(2)}) collective-permute-start(bf16[32,768]{1,0:T(8,128)(2,1)S(1)} %get-tuple-element.35), channel_id=1, source_target_pairs={{0,24},{8,16},{16,8},{24,0},{1,25},{9,17},{17,9},{25,1},{2,26},{10... | collective-permute-start | bytes 147464 | tf_op jit(solution)/shard_map/ppermute | solution.py:223
  29.9 0.0 copy-done.2
  29.9 0.0 collective-permute-start.6
  30.0 0.9 %collective-permute-start.3 = (bf16[32,768]{1,0:T(8,128)(2,1)S(1)}, bf16[32,768]{1,0:T(8,128)(2,1)S(1)}, u32[]{:S(2)}, u32[]{:S(2)}) collective-permute-start(bf16[32,768]{1,0:T(8,128)(2,1)S(1)} %get-tuple-element.33), channel_id=1, source_target_pairs={{0,8},{8,0},{16,24},{24,16},{1,9},{9,1},{17,25},{25,17},{2,10},{10... | collective-permute-start | bytes 147464 | tf_op jit(solution)/shard_map/ppermute | solution.py:223
  30.8 0.3 collective-permute-done.6.far_targets
  31.1 1.5 %collective-permute-start.4 = (bf16[32,768]{1,0:T(8,128)(2,1)S(1)}, bf16[32,768]{1,0:T(8,128)(2,1)S(1)}, u32[]{:S(2)}, u32[]{:S(2)}) collective-permute-start(bf16[32,768]{1,0:T(8,128)(2,1)S(1)} %get-tuple-element.34), channel_id=1, source_target_pairs={{0,16},{8,24},{16,0},{24,8},{1,17},{9,25},{17,1},{25,9},{2,18},{10... | collective-permute-start | bytes 147464 | tf_op jit(solution)/shard_map/ppermute | solution.py:223
  32.6 1.8 %collective-permute-done.5.refs_3_ = bf16[32,768]{1,0:T(8,128)(2,1)S(1)} collective-permute-done((bf16[32,768]{1,0:T(8,128)(2,1)S(1)}, bf16[32,768]{1,0:T(8,128)(2,1)S(1)}, u32[]{:S(2)}, u32[]{:S(2)}) %collective-permute-start.5) | collective-permute-done | bytes 49184 | tf_op jit(solution)/shard_map/ppermute | solution.py:223
  34.4 0.0 collective-permute-start.7
  34.4 0.0 collective-permute-done.3.refs_1_
  34.4 0.5 collective-permute-start.10
  34.9 0.3 collective-permute-done.4.refs_2_
  35.2 0.0 collective-permute-start.8
  35.2 0.4 collective-permute-done.7.refs_4_
  35.6 0.2 collective-permute-start.9
  35.8 0.6 shard_map.50.weights
  36.4 0.0 collective-permute-done.10.refs_7_
  36.4 0.0 collective-permute-done.8.refs_5_
  36.5 0.4 collective-permute-done.9.refs_6_
  36.9 0.2 shard_map.51
  37.0 1.7 %collective-permute-start.11 = (bf16[32,512]{1,0:T(8,128)(2,1)S(1)}, bf16[32,512]{1,0:T(8,128)(2,1)S(1)}, u32[]{:S(2)}, u32[]{:S(2)}) collective-permute-start(bf16[32,512]{1,0:T(8,128)(2,1)S(1)} %get-tuple-element.37), channel_id=1, source_target_pairs={{0,2},{1,3},{2,0},{3,1},{4,6},{5,7},{6,4},{7,5},{8,10},{9,11},{10,... | collective-permute-start | bytes 98312 | tf_op jit(solution)/shard_map/ppermute | solution.py:230
  38.7 2.6 %collective-permute-start.12 = (bf16[32,512]{1,0:T(8,128)(2,1)S(1)}, bf16[32,512]{1,0:T(8,128)(2,1)S(1)}, u32[]{:S(2)}, u32[]{:S(2)}) collective-permute-start(bf16[32,512]{1,0:T(8,128)(2,1)S(1)} %get-tuple-element.38), channel_id=1, source_target_pairs={{0,4},{1,5},{2,6},{3,7},{4,0},{5,1},{6,2},{7,3},{8,12},{9,13},{10,... | collective-permute-start | bytes 98312 | tf_op jit(solution)/shard_map/ppermute | solution.py:230
  41.3 0.1 collective-permute-start.13
  41.5 0.0 collective-permute-done.11.refs_5_
  41.5 2.7 %collective-permute-done.12.refs_6_ = bf16[32,512]{1,0:T(8,128)(2,1)S(1)} collective-permute-done((bf16[32,512]{1,0:T(8,128)(2,1)S(1)}, bf16[32,512]{1,0:T(8,128)(2,1)S(1)}, u32[]{:S(2)}, u32[]{:S(2)}) %collective-permute-start.12) | collective-permute-done | bytes 32800 | tf_op jit(solution)/shard_map/ppermute | solution.py:230
  44.2 2.9 %collective-permute-done.13.refs_7_ = bf16[32,512]{1,0:T(8,128)(2,1)S(1)} collective-permute-done((bf16[32,512]{1,0:T(8,128)(2,1)S(1)}, bf16[32,512]{1,0:T(8,128)(2,1)S(1)}, u32[]{:S(2)}, u32[]{:S(2)}) %collective-permute-start.13) | collective-permute-done | bytes 32800 | tf_op jit(solution)/shard_map/ppermute | solution.py:230
  47.0 0.0 collective-permute-done.15.refs_11_
  47.0 0.0 collective-permute-done.16.refs_12_
  47.1 0.0 copy-done
  47.1 0.9 %shard_map.52 = (bf16[32,512]{1,0:T(8,128)(2,1)S(1)}, bf16[4,32,512]{2,1,0:T(8,128)(2,1)S(1)}) custom-call(bf16[32,768]{1,0:T(8,128)(2,1)S(1)} %get-tuple-element.32.refs_0_, bf16[32,768]{1,0:T(8,128)(2,1)S(1)} %collective-permute-done.3.refs_1_, bf16[32,768]{1,0:T(8,128)(2,1)S(1)} %collective-permute-done.4.refs_2_, ...), custom_call_target="tpu_custom_call" | custom-call | flops 83886080 | bytes 3997696 | tf_op jit(solution)/shard_map/pallas_call | solution.py:25
  48.0 0.0 collective-permute-start.17
  48.0 0.6 %shard_map.49.weights = f32[8,4,8,128]{3,2,1,0:T(8,128)S(1)} custom-call(s32[2,1,4]{2,1,0:T(1,128)S(1)} %copy-done.2, s32[2,1,4]{2,1,0:T(1,128)S(1)} %collective-permute-done.6.far_targets), custom_call_target="tpu_custom_call" | custom-call | bytes 64 | tf_op jit(solution)/shard_map/pallas_call | solution.py:25
  48.7 0.7 %shard_map.53.refs_8_ = f32[4,32,512]{2,1,0:T(8,128)S(1)} custom-call(s32[2,1,4]{2,1,0:T(1,128)S(1)} %copy-done.2, s32[2,1,4]{2,1,0:T(1,128)S(1)} %collective-permute-done.6.far_targets, bf16[32,768]{1,0:T(8,128)(2,1)S(1)} %get-tuple-element.32.refs_0_, bf16[32,768]{1,0:T(8,128)(2,1)S(1)} %collective-permute-done.3.refs_1_, ...), custom_call_target="tpu_custom_call" | custom-call | bytes 393280 | tf_op jit(solution)/shard_map/pallas_call | solution.py:25
  49.3 0.0 collective-permute-done.17.refs_4_.refs_5_.refs_6_.refs_7_
  49.4 0.2 shard_map.54
  49.5 0.1 collective-permute-start.18
  49.6 1.0 %collective-permute-start.19 = (bf16[32,512]{1,0:T(8,128)(2,1)S(1)}, bf16[32,512]{1,0:T(8,128)(2,1)S(1)}, u32[]{:S(2)}, u32[]{:S(2)}) collective-permute-start(bf16[32,512]{1,0:T(8,128)(2,1)S(1)} %get-tuple-element.44), channel_id=1, source_target_pairs={{0,4},{1,5},{2,6},{3,7},{4,0},{5,1},{6,2},{7,3},{8,12},{9,13},{10,... | collective-permute-start | bytes 98312 | tf_op jit(solution)/shard_map/ppermute | solution.py:230
  50.6 3.4 %collective-permute-start.20 = (bf16[32,512]{1,0:T(8,128)(2,1)S(1)}, bf16[32,512]{1,0:T(8,128)(2,1)S(1)}, u32[]{:S(2)}, u32[]{:S(2)}) collective-permute-start(bf16[32,512]{1,0:T(8,128)(2,1)S(1)} %get-tuple-element.45), channel_id=1, source_target_pairs={{0,6},{1,7},{2,4},{3,5},{4,2},{5,3},{6,0},{7,1},{8,14},{9,15},{10,... | collective-permute-start | bytes 98312 | tf_op jit(solution)/shard_map/ppermute | solution.py:230
  54.0 0.0 collective-permute-done.18.refs_5_
  54.0 0.7 %collective-permute-done.19.refs_6_ = bf16[32,512]{1,0:T(8,128)(2,1)S(1)} collective-permute-done((bf16[32,512]{1,0:T(8,128)(2,1)S(1)}, bf16[32,512]{1,0:T(8,128)(2,1)S(1)}, u32[]{:S(2)}, u32[]{:S(2)}) %collective-permute-start.19) | collective-permute-done | bytes 32800 | tf_op jit(solution)/shard_map/ppermute | solution.py:230
  54.7 1.6 %collective-permute-done.20.refs_7_ = bf16[32,512]{1,0:T(8,128)(2,1)S(1)} collective-permute-done((bf16[32,512]{1,0:T(8,128)(2,1)S(1)}, bf16[32,512]{1,0:T(8,128)(2,1)S(1)}, u32[]{:S(2)}, u32[]{:S(2)}) %collective-permute-start.20) | collective-permute-done | bytes 32800 | tf_op jit(solution)/shard_map/ppermute | solution.py:230
  56.3 0.3 shard_map.55
  56.6 1.2 %collective-permute-start.21 = (bf16[2,32,128]{2,1,0:T(8,128)(2,1)S(1)}, bf16[2,32,128]{2,1,0:T(8,128)(2,1)S(1)}, u32[]{:S(2)}, u32[]{:S(2)}) collective-permute-start(bf16[2,32,128]{2,1,0:T(8,128)(2,1)S(1)} %get-tuple-element.48), channel_id=1, source_target_pairs={{0,8},{8,0},{16,24},{24,16},{1,9},{9,1},{17,25},{25,17},{2,10},{10... | collective-permute-start | bytes 49160 | tf_op jit(solution)/shard_map/ppermute | solution.py:223
  57.8 1.2 %collective-permute-start.22 = (bf16[2,32,128]{2,1,0:T(8,128)(2,1)S(1)}, bf16[2,32,128]{2,1,0:T(8,128)(2,1)S(1)}, u32[]{:S(2)}, u32[]{:S(2)}) collective-permute-start(bf16[2,32,128]{2,1,0:T(8,128)(2,1)S(1)} %get-tuple-element.49), channel_id=1, source_target_pairs={{0,16},{8,24},{16,0},{24,8},{1,17},{9,25},{17,1},{25,9},{2,18},{10... | collective-permute-start | bytes 49160 | tf_op jit(solution)/shard_map/ppermute | solution.py:223
  59.0 1.2 %collective-permute-start.23 = (bf16[2,32,128]{2,1,0:T(8,128)(2,1)S(1)}, bf16[2,32,128]{2,1,0:T(8,128)(2,1)S(1)}, u32[]{:S(2)}, u32[]{:S(2)}) collective-permute-start(bf16[2,32,128]{2,1,0:T(8,128)(2,1)S(1)} %get-tuple-element.50), channel_id=1, source_target_pairs={{0,24},{8,16},{16,8},{24,0},{1,25},{9,17},{17,9},{25,1},{2,26},{10... | collective-permute-start | bytes 49160 | tf_op jit(solution)/shard_map/ppermute | solution.py:223
  60.1 0.2 collective-permute-done.21.refs_2_
  60.4 1.2 %collective-permute-done.22.refs_3_ = bf16[2,32,128]{2,1,0:T(8,128)(2,1)S(1)} collective-permute-done((bf16[2,32,128]{2,1,0:T(8,128)(2,1)S(1)}, bf16[2,32,128]{2,1,0:T(8,128)(2,1)S(1)}, u32[]{:S(2)}, u32[]{:S(2)}) %collective-permute-start.22) | collective-permute-done | bytes 16416 | tf_op jit(solution)/shard_map/ppermute | solution.py:223
  61.5 2.1 %collective-permute-done.23.refs_4_ = bf16[2,32,128]{2,1,0:T(8,128)(2,1)S(1)} collective-permute-done((bf16[2,32,128]{2,1,0:T(8,128)(2,1)S(1)}, bf16[2,32,128]{2,1,0:T(8,128)(2,1)S(1)}, u32[]{:S(2)}, u32[]{:S(2)}) %collective-permute-start.23) | collective-permute-done | bytes 16416 | tf_op jit(solution)/shard_map/ppermute | solution.py:223
  63.6 0.8 %shard_map.56 = bf16[3,1,128,128]{3,2,1,0:T(8,128)(2,1)} custom-call(bf16[128,128]{1,0:T(8,128)(2,1)S(1)} %get-tuple-element.31.refs_0_, bf16[2,32,128]{2,1,0:T(8,128)(2,1)S(1)} %get-tuple-element.47.refs_1_, bf16[2,32,128]{2,1,0:T(8,128)(2,1)S(1)} %collective-permute-done.21.refs_2_, bf16[2,32,128]{2,1,0:T(8,128)(2,1)S(1)} %collective-permute-done.22.refs_3_, ...), custom_call_target="tpu_custom_call" | custom-call | bytes 98304 | tf_op jit(solution)/shard_map/pallas_call | solution.py:25
  (1 shorter events, 0.0 us)
Async XLA Ops:
  1.1 27.1 %copy-start.1 = (bf16[3,1,128,128]{3,2,1,0:T(8,128)(2,1)S(1)}, bf16[3,1,128,128]{3,2,1,0:T(8,128)(2,1)}, u32[]{:S(2)}) copy-start(bf16[3,1,128,128]{3,2,1,0:T(8,128)(2,1)} %refs_5_.1) | copy-start | bytes 294916
  1.1 15.3 %collective-permute-start.14 = (bf16[512,512]{1,0:T(8,128)(2,1)S(1)}, bf16[512,512]{1,0:T(8,128)(2,1)S(1)}, u32[]{:S(2)}, u32[]{:S(2)}) collective-permute-start(bf16[512,512]{1,0:T(8,128)(2,1)S(1)} %get-tuple-element.40.refs_9_), channel_id=1, source_target_pairs={{0,16},{1,9},{2,18},{3,11},{4,20},{5,13},{6,22},{7,15},{8,24},{9,1... | collective-permute-start | bytes 1572872 | tf_op jit(solution)/shard_map/ppermute | solution.py:227
  4.2 42.9 %collective-permute-start.15 = (bf16[512,512]{1,0:T(8,128)(2,1)S(1)}, bf16[512,512]{1,0:T(8,128)(2,1)S(1)}, u32[]{:S(2)}, u32[]{:S(2)}) collective-permute-start(bf16[512,512]{1,0:T(8,128)(2,1)S(1)} %get-tuple-element.40.refs_9_), channel_id=1, source_target_pairs={{0,8},{1,17},{2,10},{3,19},{4,12},{5,21},{6,14},{7,23},{8,0},{9,25... | collective-permute-start | bytes 1572872 | tf_op jit(solution)/shard_map/ppermute | solution.py:227
  16.4 30.7 %collective-permute-start.16 = (bf16[512,512]{1,0:T(8,128)(2,1)S(1)}, bf16[512,512]{1,0:T(8,128)(2,1)S(1)}, u32[]{:S(2)}, u32[]{:S(2)}) collective-permute-start(bf16[512,512]{1,0:T(8,128)(2,1)S(1)} %collective-permute-done.14.refs_10_), channel_id=1, source_target_pairs={{0,8},{1,17},{2,10},{3,19},{4,12},{5,21},{6,14},{7,23},{8,0},{9,25... | collective-permute-start | bytes 1572872 | tf_op jit(solution)/shard_map/ppermute | solution.py:227
  17.9 12.1 %copy-start.2 = (s32[2,1,4]{2,1,0:T(1,128)S(1)}, s32[2,1,4]{2,1,0:T(1,128)}, u32[]{:S(2)}) copy-start(s32[2,1,4]{2,1,0:T(1,128)} %own_targets.5) | copy-start | bytes 100
  17.9 8.4 %collective-permute-start = (bf16[128,128]{1,0:T(8,128)(2,1)S(1)}, bf16[128,128]{1,0:T(8,128)(2,1)S(1)}, u32[]{:S(2)}, u32[]{:S(2)}) collective-permute-start(bf16[128,128]{1,0:T(8,128)(2,1)S(1)} %get-tuple-element.28.refs_0_), channel_id=1, source_target_pairs={{0,8},{8,0},{16,24},{24,16},{1,9},{9,1},{17,25},{25,17},{2,10},{10... | collective-permute-start | bytes 98312 | tf_op jit(solution)/shard_map/ppermute | solution.py:223
  18.4 7.9 %collective-permute-start.1 = (bf16[128,128]{1,0:T(8,128)(2,1)S(1)}, bf16[128,128]{1,0:T(8,128)(2,1)S(1)}, u32[]{:S(2)}, u32[]{:S(2)}) collective-permute-start(bf16[128,128]{1,0:T(8,128)(2,1)S(1)} %get-tuple-element.28.refs_0_), channel_id=1, source_target_pairs={{0,16},{8,24},{16,0},{24,8},{1,17},{9,25},{17,1},{25,9},{2,18},{10... | collective-permute-start | bytes 98312 | tf_op jit(solution)/shard_map/ppermute | solution.py:223
  20.9 7.3 %collective-permute-start.2 = (bf16[128,128]{1,0:T(8,128)(2,1)S(1)}, bf16[128,128]{1,0:T(8,128)(2,1)S(1)}, u32[]{:S(2)}, u32[]{:S(2)}) collective-permute-start(bf16[128,128]{1,0:T(8,128)(2,1)S(1)} %get-tuple-element.28.refs_0_), channel_id=1, source_target_pairs={{0,24},{8,16},{16,8},{24,0},{1,25},{9,17},{17,9},{25,1},{2,26},{10... | collective-permute-start | bytes 98312 | tf_op jit(solution)/shard_map/ppermute | solution.py:223
  22.6 24.5 %copy-start = (bf16[3,1,512,512]{3,2,1,0:T(8,128)(2,1)S(1)}, bf16[3,1,512,512]{3,2,1,0:T(8,128)(2,1)}, u32[]{:S(2)}) copy-start(bf16[3,1,512,512]{3,2,1,0:T(8,128)(2,1)} %refs_8_.3) | copy-start | bytes 4718596
  29.1 5.3 %collective-permute-start.5 = (bf16[32,768]{1,0:T(8,128)(2,1)S(1)}, bf16[32,768]{1,0:T(8,128)(2,1)S(1)}, u32[]{:S(2)}, u32[]{:S(2)}) collective-permute-start(bf16[32,768]{1,0:T(8,128)(2,1)S(1)} %get-tuple-element.35), channel_id=1, source_target_pairs={{0,24},{8,16},{16,8},{24,0},{1,25},{9,17},{17,9},{25,1},{2,26},{10... | collective-permute-start | bytes 147464 | tf_op jit(solution)/shard_map/ppermute | solution.py:223
  29.9 1.2 %collective-permute-start.6 = (s32[2,1,4]{2,1,0:T(1,128)S(1)}, s32[2,1,4]{2,1,0:T(1,128)S(1)}, u32[]{:S(2)}, u32[]{:S(2)}) collective-permute-start(s32[2,1,4]{2,1,0:T(1,128)S(1)} %copy-done.2), channel_id=1, source_target_pairs={{0,1},{1,0},{2,3},{3,2},{4,5},{5,4},{6,7},{7,6},{8,9},{9,8},{10,11... | collective-permute-start | bytes 104 | tf_op jit(solution)/shard_map/ppermute | solution.py:233
  30.0 4.5 %collective-permute-start.3 = (bf16[32,768]{1,0:T(8,128)(2,1)S(1)}, bf16[32,768]{1,0:T(8,128)(2,1)S(1)}, u32[]{:S(2)}, u32[]{:S(2)}) collective-permute-start(bf16[32,768]{1,0:T(8,128)(2,1)S(1)} %get-tuple-element.33), channel_id=1, source_target_pairs={{0,8},{8,0},{16,24},{24,16},{1,9},{9,1},{17,25},{25,17},{2,10},{10... | collective-permute-start | bytes 147464 | tf_op jit(solution)/shard_map/ppermute | solution.py:223
  31.1 4.1 %collective-permute-start.4 = (bf16[32,768]{1,0:T(8,128)(2,1)S(1)}, bf16[32,768]{1,0:T(8,128)(2,1)S(1)}, u32[]{:S(2)}, u32[]{:S(2)}) collective-permute-start(bf16[32,768]{1,0:T(8,128)(2,1)S(1)} %get-tuple-element.34), channel_id=1, source_target_pairs={{0,16},{8,24},{16,0},{24,8},{1,17},{9,25},{17,1},{25,9},{2,18},{10... | collective-permute-start | bytes 147464 | tf_op jit(solution)/shard_map/ppermute | solution.py:223
  34.4 1.2 %collective-permute-start.7 = (bf16[32,768]{1,0:T(8,128)(2,1)S(1)}, bf16[32,768]{1,0:T(8,128)(2,1)S(1)}, u32[]{:S(2)}, u32[]{:S(2)}) collective-permute-start(bf16[32,768]{1,0:T(8,128)(2,1)S(1)} %get-tuple-element.32.refs_0_), channel_id=1, source_target_pairs={{0,1},{1,0},{2,3},{3,2},{4,5},{5,4},{6,7},{7,6},{8,9},{9,8},{10,11... | collective-permute-start | bytes 147464 | tf_op jit(solution)/shard_map/ppermute | solution.py:233
  34.4 2.0 %collective-permute-start.10 = (bf16[32,768]{1,0:T(8,128)(2,1)S(1)}, bf16[32,768]{1,0:T(8,128)(2,1)S(1)}, u32[]{:S(2)}, u32[]{:S(2)}) collective-permute-start(bf16[32,768]{1,0:T(8,128)(2,1)S(1)} %collective-permute-done.5.refs_3_), channel_id=1, source_target_pairs={{0,1},{1,0},{2,3},{3,2},{4,5},{5,4},{6,7},{7,6},{8,9},{9,8},{10,11... | collective-permute-start | bytes 147464 | tf_op jit(solution)/shard_map/ppermute | solution.py:233
  35.2 1.2 %collective-permute-start.8 = (bf16[32,768]{1,0:T(8,128)(2,1)S(1)}, bf16[32,768]{1,0:T(8,128)(2,1)S(1)}, u32[]{:S(2)}, u32[]{:S(2)}) collective-permute-start(bf16[32,768]{1,0:T(8,128)(2,1)S(1)} %collective-permute-done.3.refs_1_), channel_id=1, source_target_pairs={{0,1},{1,0},{2,3},{3,2},{4,5},{5,4},{6,7},{7,6},{8,9},{9,8},{10,11... | collective-permute-start | bytes 147464 | tf_op jit(solution)/shard_map/ppermute | solution.py:233
  35.6 1.2 %collective-permute-start.9 = (bf16[32,768]{1,0:T(8,128)(2,1)S(1)}, bf16[32,768]{1,0:T(8,128)(2,1)S(1)}, u32[]{:S(2)}, u32[]{:S(2)}) collective-permute-start(bf16[32,768]{1,0:T(8,128)(2,1)S(1)} %collective-permute-done.4.refs_2_), channel_id=1, source_target_pairs={{0,1},{1,0},{2,3},{3,2},{4,5},{5,4},{6,7},{7,6},{8,9},{9,8},{10,11... | collective-permute-start | bytes 147464 | tf_op jit(solution)/shard_map/ppermute | solution.py:233
  37.0 4.5 %collective-permute-start.11 = (bf16[32,512]{1,0:T(8,128)(2,1)S(1)}, bf16[32,512]{1,0:T(8,128)(2,1)S(1)}, u32[]{:S(2)}, u32[]{:S(2)}) collective-permute-start(bf16[32,512]{1,0:T(8,128)(2,1)S(1)} %get-tuple-element.37), channel_id=1, source_target_pairs={{0,2},{1,3},{2,0},{3,1},{4,6},{5,7},{6,4},{7,5},{8,10},{9,11},{10,... | collective-permute-start | bytes 98312 | tf_op jit(solution)/shard_map/ppermute | solution.py:230
  38.7 5.4 %collective-permute-start.12 = (bf16[32,512]{1,0:T(8,128)(2,1)S(1)}, bf16[32,512]{1,0:T(8,128)(2,1)S(1)}, u32[]{:S(2)}, u32[]{:S(2)}) collective-permute-start(bf16[32,512]{1,0:T(8,128)(2,1)S(1)} %get-tuple-element.38), channel_id=1, source_target_pairs={{0,4},{1,5},{2,6},{3,7},{4,0},{5,1},{6,2},{7,3},{8,12},{9,13},{10,... | collective-permute-start | bytes 98312 | tf_op jit(solution)/shard_map/ppermute | solution.py:230
  41.3 5.7 %collective-permute-start.13 = (bf16[32,512]{1,0:T(8,128)(2,1)S(1)}, bf16[32,512]{1,0:T(8,128)(2,1)S(1)}, u32[]{:S(2)}, u32[]{:S(2)}) collective-permute-start(bf16[32,512]{1,0:T(8,128)(2,1)S(1)} %get-tuple-element.39), channel_id=1, source_target_pairs={{0,6},{1,7},{2,4},{3,5},{4,2},{5,3},{6,0},{7,1},{8,14},{9,15},{10,... | collective-permute-start | bytes 98312 | tf_op jit(solution)/shard_map/ppermute | solution.py:230
  48.0 1.4 %collective-permute-start.17 = (bf16[4,32,512]{2,1,0:T(8,128)(2,1)S(1)}, bf16[4,32,512]{2,1,0:T(8,128)(2,1)S(1)}, u32[]{:S(2)}, u32[]{:S(2)}) collective-permute-start(bf16[4,32,512]{2,1,0:T(8,128)(2,1)S(1)} %get-tuple-element.41.refs_0_.refs_1_.refs_2_.refs_3_), channel_id=1, source_target_pairs={{0,1},{1,0},{2,3},{3,2},{4,5},{5,4},{6,7},{7,6},{8,9},{9,8},{10,11... | collective-permute-start | bytes 393224 | tf_op jit(solution)/shard_map/ppermute | solution.py:233
  49.5 4.5 %collective-permute-start.18 = (bf16[32,512]{1,0:T(8,128)(2,1)S(1)}, bf16[32,512]{1,0:T(8,128)(2,1)S(1)}, u32[]{:S(2)}, u32[]{:S(2)}) collective-permute-start(bf16[32,512]{1,0:T(8,128)(2,1)S(1)} %get-tuple-element.43), channel_id=1, source_target_pairs={{0,2},{1,3},{2,0},{3,1},{4,6},{5,7},{6,4},{7,5},{8,10},{9,11},{10,... | collective-permute-start | bytes 98312 | tf_op jit(solution)/shard_map/ppermute | solution.py:230
  49.6 5.1 %collective-permute-start.19 = (bf16[32,512]{1,0:T(8,128)(2,1)S(1)}, bf16[32,512]{1,0:T(8,128)(2,1)S(1)}, u32[]{:S(2)}, u32[]{:S(2)}) collective-permute-start(bf16[32,512]{1,0:T(8,128)(2,1)S(1)} %get-tuple-element.44), channel_id=1, source_target_pairs={{0,4},{1,5},{2,6},{3,7},{4,0},{5,1},{6,2},{7,3},{8,12},{9,13},{10,... | collective-permute-start | bytes 98312 | tf_op jit(solution)/shard_map/ppermute | solution.py:230
  50.6 5.7 %collective-permute-start.20 = (bf16[32,512]{1,0:T(8,128)(2,1)S(1)}, bf16[32,512]{1,0:T(8,128)(2,1)S(1)}, u32[]{:S(2)}, u32[]{:S(2)}) collective-permute-start(bf16[32,512]{1,0:T(8,128)(2,1)S(1)} %get-tuple-element.45), channel_id=1, source_target_pairs={{0,6},{1,7},{2,4},{3,5},{4,2},{5,3},{6,0},{7,1},{8,14},{9,15},{10,... | collective-permute-start | bytes 98312 | tf_op jit(solution)/shard_map/ppermute | solution.py:230
  56.6 3.8 %collective-permute-start.21 = (bf16[2,32,128]{2,1,0:T(8,128)(2,1)S(1)}, bf16[2,32,128]{2,1,0:T(8,128)(2,1)S(1)}, u32[]{:S(2)}, u32[]{:S(2)}) collective-permute-start(bf16[2,32,128]{2,1,0:T(8,128)(2,1)S(1)} %get-tuple-element.48), channel_id=1, source_target_pairs={{0,8},{8,0},{16,24},{24,16},{1,9},{9,1},{17,25},{25,17},{2,10},{10... | collective-permute-start | bytes 49160 | tf_op jit(solution)/shard_map/ppermute | solution.py:223
  57.8 3.7 %collective-permute-start.22 = (bf16[2,32,128]{2,1,0:T(8,128)(2,1)S(1)}, bf16[2,32,128]{2,1,0:T(8,128)(2,1)S(1)}, u32[]{:S(2)}, u32[]{:S(2)}) collective-permute-start(bf16[2,32,128]{2,1,0:T(8,128)(2,1)S(1)} %get-tuple-element.49), channel_id=1, source_target_pairs={{0,16},{8,24},{16,0},{24,8},{1,17},{9,25},{17,1},{25,9},{2,18},{10... | collective-permute-start | bytes 49160 | tf_op jit(solution)/shard_map/ppermute | solution.py:223
  59.0 4.6 %collective-permute-start.23 = (bf16[2,32,128]{2,1,0:T(8,128)(2,1)S(1)}, bf16[2,32,128]{2,1,0:T(8,128)(2,1)S(1)}, u32[]{:S(2)}, u32[]{:S(2)}) collective-permute-start(bf16[2,32,128]{2,1,0:T(8,128)(2,1)S(1)} %get-tuple-element.50), channel_id=1, source_target_pairs={{0,24},{8,16},{16,8},{24,0},{1,25},{9,17},{17,9},{25,1},{2,26},{10... | collective-permute-start | bytes 49160 | tf_op jit(solution)/shard_map/ppermute | solution.py:223

commit v4 on v3

--- a/solution.py
+++ b/solution.py
@@ -73,8 +73,9 @@
     me_col = lax.axis_index("pcol")
     turn = turns[0] if turns[0] == turns[1] else jnp.where(odd == 1, turns[1], turns[0])
     column = targets[source, 0, lax.axis_index("prow") ^ turn] - level * 2 * half
-    wanted = (column >= 0) & (column < 2 * half) & ((column & 1) == (me_col & 1))
-    return wanted, (column >> 1) ^ (me_col >> 1)
+    slot = (column >> 1) ^ (me_col >> 1)
+    wanted = (column >= 0) & (column < 2 * half) & (((column ^ me_col) & 1) == jnp.where(slot == 0, 0, 1))
+    return wanted, slot
 
 
 def weights_kernel(half, level, turns, own_targets, far_targets, out):
@@ -153,17 +154,23 @@
     return (wide[:each] + wide[each:]).astype(BF16)
 
 
-def middle_kernel(rows, half, level, *refs):
+def middle_kernel(rows, half, level, count, *refs):
     messages = refs[:rows]
     arrived = refs[rows : rows + half]
     inverse = refs[rows + half]
-    blocks = refs[rows + half + 1 : 2 * rows + half + 1]
-    solved, products, scratch = refs[2 * rows + half + 1 :]
+    blocks = refs[rows + half + 1 : rows + half + 1 + count]
+    solved, products, scratch = refs[rows + half + 1 + count :]
     given = residual(rows, level - 1, messages, arrived, scratch)
     value = solve(inverse, level, given)
     solved[...] = value
     for at, block in enumerate(blocks):
         products[at] = lax.dot_general(value, block[...], NT, preferred_element_type=F32).astype(BF16)
+
+
+def relayed_kernel(solved, *refs):
+    products = refs[-1]
+    for at, block in enumerate(refs[:-1]):
+        products[at] = lax.dot_general(solved[...], block[...], NT, preferred_element_type=F32).astype(BF16)
 
 
 def last_kernel(rows, half, level, before, *refs):
@@ -227,7 +234,11 @@
         return lax.ppermute(x, ("prow", "pcol"), links)
 
     def over_pairs(x, step):
-        return lax.ppermute(x, "pcol", pairs(columns, 2 * step)) if step else x
+        return lax.ppermute(x, "pcol", pairs(columns, 2 * step + 1)) if step else x
+
+    def to_partners(x, step):
+        links = [(r * columns + c, (r ^ step) * columns + (c ^ 1)) for r in range(rows) for c in range(columns)]
+        return lax.ppermute(x, ("prow", "pcol"), links)
 
     def flip(x):
         return lax.ppermute(x, "pcol", pairs(columns, 1))
@@ -262,16 +273,16 @@
         ],
         flops=4 * size * size * vectors,
     )
-    messages = [over_rows(x, step) for step, x in enumerate(sent)]
-    far_messages = [flip(x) for x in messages]
+    far_messages = [flip(sent[0])] + [to_partners(x, step) for step, x in enumerate(sent) if step]
+    messages = [sent[0]] + [flip(x) for x in far_messages[1:]]
     bits = [1 << b for b in range(rows.bit_length() - 1)]
     blocks, steps = {}, [(0, 0)]
     for level in range(1, later):
         have = [owned[level - 1]]
-        for turn in zip(bits[::-1], bits):
+        for turn in zip(bits, bits[::-1]):
             have += [over_turns(x, turn) for x in have]
         blocks[level] = have
-    for turn in zip(bits[::-1], bits):
+    for turn in zip(bits, bits[::-1]):
         steps += [(even ^ turn[0], odd ^ turn[1]) for even, odd in steps]
 
     own, far = list(messages), list(far_messages)
@@ -301,17 +312,25 @@
         )
         arrived = [over_pairs(x, step) for step, x in enumerate(out)]
         if level < later:
+            count = rows // 2 + 1
             value, products = call(
-                functools.partial(middle_kernel, rows, half, level),
-                [shape((each, size), BF16), shape((rows, each, size), BF16)],
-                [*messages, *arrived, inverse, *blocks[level]],
+                functools.partial(middle_kernel, rows, half, level, count),
+                [shape((each, size), BF16), shape((count, each, size), BF16)],
+                [*messages, *arrived, inverse, *blocks[level][:count]],
                 scratch=[pltpu.VMEM((each, size), F32)],
-                flops=2 * each * size * size * (rows + 1),
+                flops=2 * each * size * size * (count + 1),
+            )
+            (relayed,) = call(
+                relayed_kernel,
+                [shape((rows - count, each, size), BF16)],
+                [value, *blocks[level][count:]],
+                flops=2 * each * size * size * (rows - count),
             )
             solved.append(value)
-            far_products = flip(products)
             past += list(zip([(level - 1, turn, at) for turn, at in zip(turns, places)], own, far))
-            own, far, turns, places = [products] * rows, [far_products] * rows, steps, [*range(rows)] * 2
+            own = [products] * count + [relayed] * (rows - count)
+            far = [flip(products)] * count + [flip(relayed)] * (rows - count)
+            turns, places = steps, [*range(count), *range(rows - count)] * 2
     pieces = call(
         functools.partial(last_kernel, rows, half, later, len(solved)),
         [shape((later, each, part), BF16)] * rows,

time: 64.5 us -> 63.3 us (0.981)
  waiting for transfers between devices: 30.9 us -> 29.2 us
    ppermute x9 -> x6, waiting for transfers between devices: 11.1 us -> 6.62 us  [over_rows(): return lax.ppermute(x, 'prow', pairs(rows, step)) if step else x]
    ppermute x6 -> x7, starting transfers between devices: 0.71 us -> 4.23 us  [flip(): return lax.ppermute(x, 'pcol', pairs(columns, 1))]
    ppermute x9 -> x6, starting transfers between devices: 10.3 us -> 7.04 us  [over_rows(): return lax.ppermute(x, 'prow', pairs(rows, step)) if step else x]
    ppermute x6 -> x9, waiting for transfers between devices: 7.86 us -> 11 us  [the longest x6 7.67 us: over_pairs(): return lax.ppermute(x, 'pcol', pairs(columns, 2 * step + 1)) if step else x]
    pallas_call x11 -> x12, Pallas kernels: 7.4 us -> 7.51 us  [call(): pl.pallas_call(kernel, out_shape=out_shapes, in_specs=[smem] * scalars +...]
    ppermute x6 -> x9, starting transfers between devices: 8.9 us -> 8.81 us  [the longest x6 7.9 us: over_pairs(): return lax.ppermute(x, 'pcol', pairs(columns, 2 * step + 1)) if step else x]
  transfers between devices with their start and end apart: 24 -> 25, of which waited for: 15 -> 14; matrix products, arithmetic and copies ran while one was open for 0% -> 0% of each run, Pallas kernels for 6% -> 8%
where the time goes in v4:
time: 63.3 us; the launch traced here: 63.1 us
  waiting for transfers between devices  29.2 us (46%)
  starting transfers between devices  26.2 us (41%)
  Pallas kernels  7.51 us (12%)
    ppermute x3, waiting for transfers between devices, over_turns(): return lax.ppermute(x, ('prow', 'pcol'), links)  10.7 us
    ppermute x6, starting transfers between devices, over_pairs(): return lax.ppermute(x, 'pcol', pairs(columns, 2 * step + 1)) if step else x  7.9 us
    ppermute x6, waiting for transfers between devices, over_pairs(): return lax.ppermute(x, 'pcol', pairs(columns, 2 * step + 1)) if step else x  7.67 us
    pallas_call x12, Pallas kernels, call(): pl.pallas_call(kernel, out_shape=out_shapes, in_specs=[smem] * scalars +...  7.51 us
    ppermute x6, starting transfers between devices, over_rows(): return lax.ppermute(x, 'prow', pairs(rows, step)) if step else x  7.04 us
    ppermute x6, waiting for transfers between devices, over_rows(): return lax.ppermute(x, 'prow', pairs(rows, step)) if step else x  6.62 us
    ppermute x3, starting transfers between devices, over_turns(): return lax.ppermute(x, ('prow', 'pcol'), links)  6.11 us
    ppermute x7, starting transfers between devices, flip(): return lax.ppermute(x, 'pcol', pairs(columns, 1))  4.23 us
  transfers between devices with their start and end apart: 25, of which 14 were waited for; matrix products, arithmetic and copies ran while one was open for 0% of the time, Pallas kernels for 8%

profile of v4, /device:TPU:0, one launch (start us, length us, event | category | flops | bytes accessed | tf_op | source)
XLA Modules:
  0.0 63.1 jit_solution(13725722461629116088)
XLA Ops:
  0.0 1.1 %shard_map.46 = (bf16[128,128]{1,0:T(8,128)(2,1)S(1)}, bf16[512,512]{1,0:T(8,128)(2,1)S(1)}) custom-call(bf16[3,1,128,128]{3,2,1,0:T(8,128)(2,1)} %refs_5_.1, bf16[2,1,1,512,512]{4,3,2,1,0:T(8,128)(2,1)} %refs_1_.3), custom_call_target="tpu_custom_call" | custom-call | bytes 1146880 | tf_op jit(solution)/shard_map/pallas_call | solution.py:25
  1.1 0.0 copy-start.1
  1.1 3.0 %collective-permute-start.14 = (bf16[512,512]{1,0:T(8,128)(2,1)S(1)}, bf16[512,512]{1,0:T(8,128)(2,1)S(1)}, u32[]{:S(2)}, u32[]{:S(2)}) collective-permute-start(bf16[512,512]{1,0:T(8,128)(2,1)S(1)} %get-tuple-element.40.refs_9_), channel_id=1, source_target_pairs={{0,8},{1,17},{2,10},{3,19},{4,12},{5,21},{6,14},{7,23},{8,0},{9,25... | collective-permute-start | bytes 1572872 | tf_op jit(solution)/shard_map/ppermute | solution.py:234
  4.1 1.5 %collective-permute-start.15 = (bf16[512,512]{1,0:T(8,128)(2,1)S(1)}, bf16[512,512]{1,0:T(8,128)(2,1)S(1)}, u32[]{:S(2)}, u32[]{:S(2)}) collective-permute-start(bf16[512,512]{1,0:T(8,128)(2,1)S(1)} %get-tuple-element.40.refs_9_), channel_id=1, source_target_pairs={{0,16},{1,9},{2,18},{3,11},{4,20},{5,13},{6,22},{7,15},{8,24},{9,1... | collective-permute-start | bytes 1572872 | tf_op jit(solution)/shard_map/ppermute | solution.py:234
  5.7 10.7 %collective-permute-done.14.refs_10_ = bf16[512,512]{1,0:T(8,128)(2,1)S(1)} collective-permute-done((bf16[512,512]{1,0:T(8,128)(2,1)S(1)}, bf16[512,512]{1,0:T(8,128)(2,1)S(1)}, u32[]{:S(2)}, u32[]{:S(2)}) %collective-permute-start.14) | collective-permute-done | bytes 524320 | tf_op jit(solution)/shard_map/ppermute | solution.py:234
  16.3 1.6 %collective-permute-start.16 = (bf16[512,512]{1,0:T(8,128)(2,1)S(1)}, bf16[512,512]{1,0:T(8,128)(2,1)S(1)}, u32[]{:S(2)}, u32[]{:S(2)}) collective-permute-start(bf16[512,512]{1,0:T(8,128)(2,1)S(1)} %collective-permute-done.14.refs_10_), channel_id=1, source_target_pairs={{0,16},{1,9},{2,18},{3,11},{4,20},{5,13},{6,22},{7,15},{8,24},{9,1... | collective-permute-start | bytes 1572872 | tf_op jit(solution)/shard_map/ppermute | solution.py:234
  17.9 1.6 %collective-permute-start = (bf16[128,128]{1,0:T(8,128)(2,1)S(1)}, bf16[128,128]{1,0:T(8,128)(2,1)S(1)}, u32[]{:S(2)}, u32[]{:S(2)}) collective-permute-start(bf16[128,128]{1,0:T(8,128)(2,1)S(1)} %get-tuple-element.28.refs_0_), channel_id=1, source_target_pairs={{0,8},{8,0},{16,24},{24,16},{1,9},{9,1},{17,25},{25,17},{2,10},{10... | collective-permute-start | bytes 98312 | tf_op jit(solution)/shard_map/ppermute | solution.py:230
  19.5 1.3 %collective-permute-start.1 = (bf16[128,128]{1,0:T(8,128)(2,1)S(1)}, bf16[128,128]{1,0:T(8,128)(2,1)S(1)}, u32[]{:S(2)}, u32[]{:S(2)}) collective-permute-start(bf16[128,128]{1,0:T(8,128)(2,1)S(1)} %get-tuple-element.28.refs_0_), channel_id=1, source_target_pairs={{0,16},{8,24},{16,0},{24,8},{1,17},{9,25},{17,1},{25,9},{2,18},{10... | collective-permute-start | bytes 98312 | tf_op jit(solution)/shard_map/ppermute | solution.py:230
  20.8 0.5 collective-permute-start.2
  21.4 1.2 %shard_map.47 = (bf16[512,512]{1,0:T(8,128)(2,1)S(1)}, bf16[512,512]{1,0:T(8,128)(2,1)S(1)}) custom-call(bf16[3,1,512,512]{3,2,1,0:T(8,128)(2,1)} %refs_8_.3, bf16[2,1,1,512,512]{4,3,2,1,0:T(8,128)(2,1)} %refs_1_.3), custom_call_target="tpu_custom_call" | custom-call | bytes 2621440 | tf_op jit(solution)/shard_map/pallas_call | solution.py:25
  22.6 0.0 copy-start
  22.6 0.0 collective-permute-done.refs_1_
  22.6 3.9 %collective-permute-done.1.refs_2_ = bf16[128,128]{1,0:T(8,128)(2,1)S(1)} collective-permute-done((bf16[128,128]{1,0:T(8,128)(2,1)S(1)}, bf16[128,128]{1,0:T(8,128)(2,1)S(1)}, u32[]{:S(2)}, u32[]{:S(2)}) %collective-permute-start.1) | collective-permute-done | bytes 32800 | tf_op jit(solution)/shard_map/ppermute | solution.py:230
  26.6 0.0 collective-permute-done.2.refs_3_
  26.6 0.8 %shard_map.48 = (bf16[128,128]{1,0:T(8,128)(2,1)S(1)}, bf16[32,768]{1,0:T(8,128)(2,1)S(1)}, bf16[32,768]{1,0:T(8,128)(2,1)S(1)}, bf16[32,768]{1,0:T(8,128)(2,1)S(1)}, bf16[32,768]{1,0:T(8,128)(2,1)S(1)}) custom-call(bf16[128,128]{1,0:T(8,128)(2,1)S(1)} %get-tuple-element.28.refs_0_, bf16[128,128]{1,0:T(8,128)(2,1)S(1)} %collective-permute-done.refs_1_, ...), custom_call_target="tpu_custom_call" | custom-call | flops 134217728 | bytes 1277952 | tf_op jit(solution)/shard_map/pallas_call | solution.py:25
  27.4 0.1 collective-permute-start.3
  27.5 2.6 %collective-permute-start.9 = (s32[2,1,4]{2,1,0:T(1,128)S(1)}, s32[2,1,4]{2,1,0:T(1,128)S(1)}, u32[]{:S(2)}, u32[]{:S(2)}) collective-permute-start(s32[2,1,4]{2,1,0:T(1,128)S(1)} %copy-done.2), channel_id=1, source_target_pairs={{0,1},{1,0},{2,3},{3,2},{4,5},{5,4},{6,7},{7,6},{8,9},{9,8},{10,11... | collective-permute-start | bytes 104 | tf_op jit(solution)/shard_map/ppermute | solution.py:244
  30.1 0.3 collective-permute-start.5
  30.4 0.5 collective-permute-done.9.far_targets
  30.9 0.5 collective-permute-start.7
  31.4 0.0 collective-permute-done.3.refs_5_
  31.4 0.5 collective-permute-start.10
  31.9 2.1 %collective-permute-done.5.refs_6_ = bf16[32,768]{1,0:T(8,128)(2,1)S(1)} collective-permute-done((bf16[32,768]{1,0:T(8,128)(2,1)S(1)}, bf16[32,768]{1,0:T(8,128)(2,1)S(1)}, u32[]{:S(2)}, u32[]{:S(2)}) %collective-permute-start.5) | collective-permute-done | bytes 49184 | tf_op jit(solution)/shard_map/ppermute | solution.py:241
  34.0 0.1 collective-permute-start.4
  34.1 1.3 %collective-permute-done.7.refs_7_ = bf16[32,768]{1,0:T(8,128)(2,1)S(1)} collective-permute-done((bf16[32,768]{1,0:T(8,128)(2,1)S(1)}, bf16[32,768]{1,0:T(8,128)(2,1)S(1)}, u32[]{:S(2)}, u32[]{:S(2)}) %collective-permute-start.7) | collective-permute-done | bytes 49184 | tf_op jit(solution)/shard_map/ppermute | solution.py:241
  35.3 0.3 collective-permute-start.6
  35.7 0.0 collective-permute-done.10.refs_4_
  35.7 0.2 collective-permute-start.8
  35.8 0.6 %shard_map.50.weights = f32[8,4,8,128]{3,2,1,0:T(8,128)S(1)} custom-call(s32[2,1,4]{2,1,0:T(1,128)S(1)} %copy-done.2, s32[2,1,4]{2,1,0:T(1,128)S(1)} %collective-permute-done.9.far_targets), custom_call_target="tpu_custom_call" | custom-call | bytes 64 | tf_op jit(solution)/shard_map/pallas_call | solution.py:25
  36.5 0.0 collective-permute-done.4.refs_1_
  36.5 0.1 collective-permute-done.6.refs_2_
  36.6 0.4 collective-permute-done.8.refs_3_
  36.9 0.2 shard_map.51
  37.1 1.4 %collective-permute-start.11 = (bf16[32,512]{1,0:T(8,128)(2,1)S(1)}, bf16[32,512]{1,0:T(8,128)(2,1)S(1)}, u32[]{:S(2)}, u32[]{:S(2)}) collective-permute-start(bf16[32,512]{1,0:T(8,128)(2,1)S(1)} %get-tuple-element.37), channel_id=1, source_target_pairs={{0,3},{1,2},{2,1},{3,0},{4,7},{5,6},{6,5},{7,4},{8,11},{9,10},{10,... | collective-permute-start | bytes 98312 | tf_op jit(solution)/shard_map/ppermute | solution.py:237
  38.5 2.5 %collective-permute-start.12 = (bf16[32,512]{1,0:T(8,128)(2,1)S(1)}, bf16[32,512]{1,0:T(8,128)(2,1)S(1)}, u32[]{:S(2)}, u32[]{:S(2)}) collective-permute-start(bf16[32,512]{1,0:T(8,128)(2,1)S(1)} %get-tuple-element.38), channel_id=1, source_target_pairs={{0,5},{1,4},{2,7},{3,6},{4,1},{5,0},{6,3},{7,2},{8,13},{9,12},{10,... | collective-permute-start | bytes 98312 | tf_op jit(solution)/shard_map/ppermute | solution.py:237
  41.0 0.0 collective-permute-start.13
  41.0 0.0 collective-permute-done.11.refs_5_
  41.0 1.9 %collective-permute-done.12.refs_6_ = bf16[32,512]{1,0:T(8,128)(2,1)S(1)} collective-permute-done((bf16[32,512]{1,0:T(8,128)(2,1)S(1)}, bf16[32,512]{1,0:T(8,128)(2,1)S(1)}, u32[]{:S(2)}, u32[]{:S(2)}) %collective-permute-start.12) | collective-permute-done | bytes 32800 | tf_op jit(solution)/shard_map/ppermute | solution.py:237
  43.0 3.2 %collective-permute-done.13.refs_7_ = bf16[32,512]{1,0:T(8,128)(2,1)S(1)} collective-permute-done((bf16[32,512]{1,0:T(8,128)(2,1)S(1)}, bf16[32,512]{1,0:T(8,128)(2,1)S(1)}, u32[]{:S(2)}, u32[]{:S(2)}) %collective-permute-start.13) | collective-permute-done | bytes 32800 | tf_op jit(solution)/shard_map/ppermute | solution.py:237
  46.2 0.0 collective-permute-done.15.refs_11_
  46.2 0.8 %shard_map.52 = (bf16[32,512]{1,0:T(8,128)(2,1)S(1)}, bf16[3,32,512]{2,1,0:T(8,128)(2,1)S(1)}) custom-call(bf16[32,768]{1,0:T(8,128)(2,1)S(1)} %get-tuple-element.32.refs_0_, bf16[32,768]{1,0:T(8,128)(2,1)S(1)} %collective-permute-done.4.refs_1_, bf16[32,768]{1,0:T(8,128)(2,1)S(1)} %collective-permute-done.6.refs_2_, ...), custom_call_target="tpu_custom_call" | custom-call | flops 67108864 | bytes 3473408 | tf_op jit(solution)/shard_map/pallas_call | solution.py:25
  46.9 0.2 collective-permute-start.17
  47.1 0.0 collective-permute-done.16.refs_0_
  47.1 0.2 shard_map.53.refs_3_
  47.4 0.4 collective-permute-start.18
  47.7 0.7 %shard_map.49.weights = f32[8,4,8,128]{3,2,1,0:T(8,128)S(1)} custom-call(s32[2,1,4]{2,1,0:T(1,128)S(1)} %copy-done.2, s32[2,1,4]{2,1,0:T(1,128)S(1)} %collective-permute-done.9.far_targets), custom_call_target="tpu_custom_call" | custom-call | bytes 64 | tf_op jit(solution)/shard_map/pallas_call | solution.py:25
  48.4 0.7 %shard_map.54.refs_8_ = f32[4,32,512]{2,1,0:T(8,128)S(1)} custom-call(s32[2,1,4]{2,1,0:T(1,128)S(1)} %copy-done.2, s32[2,1,4]{2,1,0:T(1,128)S(1)} %collective-permute-done.9.far_targets, bf16[32,768]{1,0:T(8,128)(2,1)S(1)} %get-tuple-element.32.refs_0_, bf16[32,768]{1,0:T(8,128)(2,1)S(1)} %collective-permute-done.4.refs_1_, ...), custom_call_target="tpu_custom_call" | custom-call | bytes 393280 | tf_op jit(solution)/shard_map/pallas_call | solution.py:25
  49.1 0.0 collective-permute-done.17.refs_4_.refs_5_.refs_6_
  49.1 0.0 collective-permute-done.18.refs_7_
  49.1 0.2 shard_map.55
  49.3 0.1 collective-permute-start.19
  49.4 0.9 %collective-permute-start.20 = (bf16[32,512]{1,0:T(8,128)(2,1)S(1)}, bf16[32,512]{1,0:T(8,128)(2,1)S(1)}, u32[]{:S(2)}, u32[]{:S(2)}) collective-permute-start(bf16[32,512]{1,0:T(8,128)(2,1)S(1)} %get-tuple-element.45), channel_id=1, source_target_pairs={{0,5},{1,4},{2,7},{3,6},{4,1},{5,0},{6,3},{7,2},{8,13},{9,12},{10,... | collective-permute-start | bytes 98312 | tf_op jit(solution)/shard_map/ppermute | solution.py:237
  50.3 2.9 %collective-permute-start.21 = (bf16[32,512]{1,0:T(8,128)(2,1)S(1)}, bf16[32,512]{1,0:T(8,128)(2,1)S(1)}, u32[]{:S(2)}, u32[]{:S(2)}) collective-permute-start(bf16[32,512]{1,0:T(8,128)(2,1)S(1)} %get-tuple-element.46), channel_id=1, source_target_pairs={{0,7},{1,6},{2,5},{3,4},{4,3},{5,2},{6,1},{7,0},{8,15},{9,14},{10,... | collective-permute-start | bytes 98312 | tf_op jit(solution)/shard_map/ppermute | solution.py:237
  53.2 0.0 collective-permute-done.19.refs_5_
  53.3 0.4 collective-permute-done.20.refs_6_
  53.7 2.1 %collective-permute-done.21.refs_7_ = bf16[32,512]{1,0:T(8,128)(2,1)S(1)} collective-permute-done((bf16[32,512]{1,0:T(8,128)(2,1)S(1)}, bf16[32,512]{1,0:T(8,128)(2,1)S(1)}, u32[]{:S(2)}, u32[]{:S(2)}) %collective-permute-start.21) | collective-permute-done | bytes 32800 | tf_op jit(solution)/shard_map/ppermute | solution.py:237
  55.8 0.3 shard_map.56
  56.1 0.6 collective-permute-start.22
  56.7 1.0 %collective-permute-start.23 = (bf16[2,32,128]{2,1,0:T(8,128)(2,1)S(1)}, bf16[2,32,128]{2,1,0:T(8,128)(2,1)S(1)}, u32[]{:S(2)}, u32[]{:S(2)}) collective-permute-start(bf16[2,32,128]{2,1,0:T(8,128)(2,1)S(1)} %get-tuple-element.49), channel_id=1, source_target_pairs={{0,16},{8,24},{16,0},{24,8},{1,17},{9,25},{17,1},{25,9},{2,18},{10... | collective-permute-start | bytes 49160 | tf_op jit(solution)/shard_map/ppermute | solution.py:230
  57.7 2.0 %collective-permute-start.24 = (bf16[2,32,128]{2,1,0:T(8,128)(2,1)S(1)}, bf16[2,32,128]{2,1,0:T(8,128)(2,1)S(1)}, u32[]{:S(2)}, u32[]{:S(2)}) collective-permute-start(bf16[2,32,128]{2,1,0:T(8,128)(2,1)S(1)} %get-tuple-element.50), channel_id=1, source_target_pairs={{0,24},{8,16},{16,8},{24,0},{1,25},{9,17},{17,9},{25,1},{2,26},{10... | collective-permute-start | bytes 49160 | tf_op jit(solution)/shard_map/ppermute | solution.py:230
  59.6 0.2 collective-permute-done.22.refs_2_
  59.9 0.5 collective-permute-done.23.refs_3_
  60.4 1.9 %collective-permute-done.24.refs_4_ = bf16[2,32,128]{2,1,0:T(8,128)(2,1)S(1)} collective-permute-done((bf16[2,32,128]{2,1,0:T(8,128)(2,1)S(1)}, bf16[2,32,128]{2,1,0:T(8,128)(2,1)S(1)}, u32[]{:S(2)}, u32[]{:S(2)}) %collective-permute-start.24) | collective-permute-done | bytes 16416 | tf_op jit(solution)/shard_map/ppermute | solution.py:230
  62.3 0.8 %shard_map.57 = bf16[3,1,128,128]{3,2,1,0:T(8,128)(2,1)} custom-call(bf16[128,128]{1,0:T(8,128)(2,1)S(1)} %get-tuple-element.31.refs_0_, bf16[2,32,128]{2,1,0:T(8,128)(2,1)S(1)} %get-tuple-element.47.refs_1_, bf16[2,32,128]{2,1,0:T(8,128)(2,1)S(1)} %collective-permute-done.22.refs_2_, bf16[2,32,128]{2,1,0:T(8,128)(2,1)S(1)} %collective-permute-done.23.refs_3_, ...), custom_call_target="tpu_custom_call" | custom-call | bytes 98304 | tf_op jit(solution)/shard_map/pallas_call | solution.py:25
  (4 shorter events, 0.0 us)
Async XLA Ops:
  1.1 25.5 %copy-start.1 = (bf16[3,1,128,128]{3,2,1,0:T(8,128)(2,1)S(1)}, bf16[3,1,128,128]{3,2,1,0:T(8,128)(2,1)}, u32[]{:S(2)}) copy-start(bf16[3,1,128,128]{3,2,1,0:T(8,128)(2,1)} %refs_5_.1) | copy-start | bytes 294916
  1.1 15.2 %collective-permute-start.14 = (bf16[512,512]{1,0:T(8,128)(2,1)S(1)}, bf16[512,512]{1,0:T(8,128)(2,1)S(1)}, u32[]{:S(2)}, u32[]{:S(2)}) collective-permute-start(bf16[512,512]{1,0:T(8,128)(2,1)S(1)} %get-tuple-element.40.refs_9_), channel_id=1, source_target_pairs={{0,8},{1,17},{2,10},{3,19},{4,12},{5,21},{6,14},{7,23},{8,0},{9,25... | collective-permute-start | bytes 1572872 | tf_op jit(solution)/shard_map/ppermute | solution.py:234
  4.1 42.0 %collective-permute-start.15 = (bf16[512,512]{1,0:T(8,128)(2,1)S(1)}, bf16[512,512]{1,0:T(8,128)(2,1)S(1)}, u32[]{:S(2)}, u32[]{:S(2)}) collective-permute-start(bf16[512,512]{1,0:T(8,128)(2,1)S(1)} %get-tuple-element.40.refs_9_), channel_id=1, source_target_pairs={{0,16},{1,9},{2,18},{3,11},{4,20},{5,13},{6,22},{7,15},{8,24},{9,1... | collective-permute-start | bytes 1572872 | tf_op jit(solution)/shard_map/ppermute | solution.py:234
  16.3 30.8 %collective-permute-start.16 = (bf16[512,512]{1,0:T(8,128)(2,1)S(1)}, bf16[512,512]{1,0:T(8,128)(2,1)S(1)}, u32[]{:S(2)}, u32[]{:S(2)}) collective-permute-start(bf16[512,512]{1,0:T(8,128)(2,1)S(1)} %collective-permute-done.14.refs_10_), channel_id=1, source_target_pairs={{0,16},{1,9},{2,18},{3,11},{4,20},{5,13},{6,22},{7,15},{8,24},{9,1... | collective-permute-start | bytes 1572872 | tf_op jit(solution)/shard_map/ppermute | solution.py:234
  17.9 9.6 %copy-start.2 = (s32[2,1,4]{2,1,0:T(1,128)S(1)}, s32[2,1,4]{2,1,0:T(1,128)}, u32[]{:S(2)}) copy-start(s32[2,1,4]{2,1,0:T(1,128)} %own_targets.5) | copy-start | bytes 100
  17.9 4.7 %collective-permute-start = (bf16[128,128]{1,0:T(8,128)(2,1)S(1)}, bf16[128,128]{1,0:T(8,128)(2,1)S(1)}, u32[]{:S(2)}, u32[]{:S(2)}) collective-permute-start(bf16[128,128]{1,0:T(8,128)(2,1)S(1)} %get-tuple-element.28.refs_0_), channel_id=1, source_target_pairs={{0,8},{8,0},{16,24},{24,16},{1,9},{9,1},{17,25},{25,17},{2,10},{10... | collective-permute-start | bytes 98312 | tf_op jit(solution)/shard_map/ppermute | solution.py:230
  19.5 7.0 %collective-permute-start.1 = (bf16[128,128]{1,0:T(8,128)(2,1)S(1)}, bf16[128,128]{1,0:T(8,128)(2,1)S(1)}, u32[]{:S(2)}, u32[]{:S(2)}) collective-permute-start(bf16[128,128]{1,0:T(8,128)(2,1)S(1)} %get-tuple-element.28.refs_0_), channel_id=1, source_target_pairs={{0,16},{8,24},{16,0},{24,8},{1,17},{9,25},{17,1},{25,9},{2,18},{10... | collective-permute-start | bytes 98312 | tf_op jit(solution)/shard_map/ppermute | solution.py:230
  20.8 5.7 %collective-permute-start.2 = (bf16[128,128]{1,0:T(8,128)(2,1)S(1)}, bf16[128,128]{1,0:T(8,128)(2,1)S(1)}, u32[]{:S(2)}, u32[]{:S(2)}) collective-permute-start(bf16[128,128]{1,0:T(8,128)(2,1)S(1)} %get-tuple-element.28.refs_0_), channel_id=1, source_target_pairs={{0,24},{8,16},{16,8},{24,0},{1,25},{9,17},{17,9},{25,1},{2,26},{10... | collective-permute-start | bytes 98312 | tf_op jit(solution)/shard_map/ppermute | solution.py:230
  22.6 23.6 %copy-start = (bf16[3,1,512,512]{3,2,1,0:T(8,128)(2,1)S(1)}, bf16[3,1,512,512]{3,2,1,0:T(8,128)(2,1)}, u32[]{:S(2)}) copy-start(bf16[3,1,512,512]{3,2,1,0:T(8,128)(2,1)} %refs_8_.3) | copy-start | bytes 4718596
  27.4 4.0 %collective-permute-start.3 = (bf16[32,768]{1,0:T(8,128)(2,1)S(1)}, bf16[32,768]{1,0:T(8,128)(2,1)S(1)}, u32[]{:S(2)}, u32[]{:S(2)}) collective-permute-start(bf16[32,768]{1,0:T(8,128)(2,1)S(1)} %get-tuple-element.33), channel_id=1, source_target_pairs={{0,9},{1,8},{2,11},{3,10},{4,13},{5,12},{6,15},{7,14},{8,1},{9,0},... | collective-permute-start | bytes 147464 | tf_op jit(solution)/shard_map/ppermute | solution.py:241
  27.5 3.4 %collective-permute-start.9 = (s32[2,1,4]{2,1,0:T(1,128)S(1)}, s32[2,1,4]{2,1,0:T(1,128)S(1)}, u32[]{:S(2)}, u32[]{:S(2)}) collective-permute-start(s32[2,1,4]{2,1,0:T(1,128)S(1)} %copy-done.2), channel_id=1, source_target_pairs={{0,1},{1,0},{2,3},{3,2},{4,5},{5,4},{6,7},{7,6},{8,9},{9,8},{10,11... | collective-permute-start | bytes 104 | tf_op jit(solution)/shard_map/ppermute | solution.py:244
  30.1 3.9 %collective-permute-start.5 = (bf16[32,768]{1,0:T(8,128)(2,1)S(1)}, bf16[32,768]{1,0:T(8,128)(2,1)S(1)}, u32[]{:S(2)}, u32[]{:S(2)}) collective-permute-start(bf16[32,768]{1,0:T(8,128)(2,1)S(1)} %get-tuple-element.34), channel_id=1, source_target_pairs={{0,17},{1,16},{2,19},{3,18},{4,21},{5,20},{6,23},{7,22},{8,25},{9,... | collective-permute-start | bytes 147464 | tf_op jit(solution)/shard_map/ppermute | solution.py:241
  30.9 4.4 %collective-permute-start.7 = (bf16[32,768]{1,0:T(8,128)(2,1)S(1)}, bf16[32,768]{1,0:T(8,128)(2,1)S(1)}, u32[]{:S(2)}, u32[]{:S(2)}) collective-permute-start(bf16[32,768]{1,0:T(8,128)(2,1)S(1)} %get-tuple-element.35), channel_id=1, source_target_pairs={{0,25},{1,24},{2,27},{3,26},{4,29},{5,28},{6,31},{7,30},{8,17},{9,... | collective-permute-start | bytes 147464 | tf_op jit(solution)/shard_map/ppermute | solution.py:241
  31.4 4.3 %collective-permute-start.10 = (bf16[32,768]{1,0:T(8,128)(2,1)S(1)}, bf16[32,768]{1,0:T(8,128)(2,1)S(1)}, u32[]{:S(2)}, u32[]{:S(2)}) collective-permute-start(bf16[32,768]{1,0:T(8,128)(2,1)S(1)} %get-tuple-element.32.refs_0_), channel_id=1, source_target_pairs={{0,1},{1,0},{2,3},{3,2},{4,5},{5,4},{6,7},{7,6},{8,9},{9,8},{10,11... | collective-permute-start | bytes 147464 | tf_op jit(solution)/shard_map/ppermute | solution.py:244
  34.0 2.5 %collective-permute-start.4 = (bf16[32,768]{1,0:T(8,128)(2,1)S(1)}, bf16[32,768]{1,0:T(8,128)(2,1)S(1)}, u32[]{:S(2)}, u32[]{:S(2)}) collective-permute-start(bf16[32,768]{1,0:T(8,128)(2,1)S(1)} %collective-permute-done.3.refs_5_), channel_id=1, source_target_pairs={{0,1},{1,0},{2,3},{3,2},{4,5},{5,4},{6,7},{7,6},{8,9},{9,8},{10,11... | collective-permute-start | bytes 147464 | tf_op jit(solution)/shard_map/ppermute | solution.py:244
  35.3 1.2 %collective-permute-start.6 = (bf16[32,768]{1,0:T(8,128)(2,1)S(1)}, bf16[32,768]{1,0:T(8,128)(2,1)S(1)}, u32[]{:S(2)}, u32[]{:S(2)}) collective-permute-start(bf16[32,768]{1,0:T(8,128)(2,1)S(1)} %collective-permute-done.5.refs_6_), channel_id=1, source_target_pairs={{0,1},{1,0},{2,3},{3,2},{4,5},{5,4},{6,7},{7,6},{8,9},{9,8},{10,11... | collective-permute-start | bytes 147464 | tf_op jit(solution)/shard_map/ppermute | solution.py:244
  35.7 1.2 %collective-permute-start.8 = (bf16[32,768]{1,0:T(8,128)(2,1)S(1)}, bf16[32,768]{1,0:T(8,128)(2,1)S(1)}, u32[]{:S(2)}, u32[]{:S(2)}) collective-permute-start(bf16[32,768]{1,0:T(8,128)(2,1)S(1)} %collective-permute-done.7.refs_7_), channel_id=1, source_target_pairs={{0,1},{1,0},{2,3},{3,2},{4,5},{5,4},{6,7},{7,6},{8,9},{9,8},{10,11... | collective-permute-start | bytes 147464 | tf_op jit(solution)/shard_map/ppermute | solution.py:244
  37.1 4.0 %collective-permute-start.11 = (bf16[32,512]{1,0:T(8,128)(2,1)S(1)}, bf16[32,512]{1,0:T(8,128)(2,1)S(1)}, u32[]{:S(2)}, u32[]{:S(2)}) collective-permute-start(bf16[32,512]{1,0:T(8,128)(2,1)S(1)} %get-tuple-element.37), channel_id=1, source_target_pairs={{0,3},{1,2},{2,1},{3,0},{4,7},{5,6},{6,5},{7,4},{8,11},{9,10},{10,... | collective-permute-start | bytes 98312 | tf_op jit(solution)/shard_map/ppermute | solution.py:237
  38.5 4.5 %collective-permute-start.12 = (bf16[32,512]{1,0:T(8,128)(2,1)S(1)}, bf16[32,512]{1,0:T(8,128)(2,1)S(1)}, u32[]{:S(2)}, u32[]{:S(2)}) collective-permute-start(bf16[32,512]{1,0:T(8,128)(2,1)S(1)} %get-tuple-element.38), channel_id=1, source_target_pairs={{0,5},{1,4},{2,7},{3,6},{4,1},{5,0},{6,3},{7,2},{8,13},{9,12},{10,... | collective-permute-start | bytes 98312 | tf_op jit(solution)/shard_map/ppermute | solution.py:237
  41.0 5.1 %collective-permute-start.13 = (bf16[32,512]{1,0:T(8,128)(2,1)S(1)}, bf16[32,512]{1,0:T(8,128)(2,1)S(1)}, u32[]{:S(2)}, u32[]{:S(2)}) collective-permute-start(bf16[32,512]{1,0:T(8,128)(2,1)S(1)} %get-tuple-element.39), channel_id=1, source_target_pairs={{0,7},{1,6},{2,5},{3,4},{4,3},{5,2},{6,1},{7,0},{8,15},{9,14},{10,... | collective-permute-start | bytes 98312 | tf_op jit(solution)/shard_map/ppermute | solution.py:237
  46.9 2.2 %collective-permute-start.17 = (bf16[3,32,512]{2,1,0:T(8,128)(2,1)S(1)}, bf16[3,32,512]{2,1,0:T(8,128)(2,1)S(1)}, u32[]{:S(2)}, u32[]{:S(2)}) collective-permute-start(bf16[3,32,512]{2,1,0:T(8,128)(2,1)S(1)} %get-tuple-element.41.refs_0_.refs_1_.refs_2_), channel_id=1, source_target_pairs={{0,1},{1,0},{2,3},{3,2},{4,5},{5,4},{6,7},{7,6},{8,9},{9,8},{10,11... | collective-permute-start | bytes 294920 | tf_op jit(solution)/shard_map/ppermute | solution.py:244
  47.4 1.7 %collective-permute-start.18 = (bf16[1,32,512]{2,1,0:T(8,128)(2,1)S(1)}, bf16[1,32,512]{2,1,0:T(8,128)(2,1)S(1)}, u32[]{:S(2)}, u32[]{:S(2)}) collective-permute-start(bf16[1,32,512]{2,1,0:T(8,128)(2,1)S(1)} %shard_map.53.refs_3_), channel_id=1, source_target_pairs={{0,1},{1,0},{2,3},{3,2},{4,5},{5,4},{6,7},{7,6},{8,9},{9,8},{10,11... | collective-permute-start | bytes 98312 | tf_op jit(solution)/shard_map/ppermute | solution.py:244
  49.3 4.0 %collective-permute-start.19 = (bf16[32,512]{1,0:T(8,128)(2,1)S(1)}, bf16[32,512]{1,0:T(8,128)(2,1)S(1)}, u32[]{:S(2)}, u32[]{:S(2)}) collective-permute-start(bf16[32,512]{1,0:T(8,128)(2,1)S(1)} %get-tuple-element.44), channel_id=1, source_target_pairs={{0,3},{1,2},{2,1},{3,0},{4,7},{5,6},{6,5},{7,4},{8,11},{9,10},{10,... | collective-permute-start | bytes 98312 | tf_op jit(solution)/shard_map/ppermute | solution.py:237
  49.4 4.3 %collective-permute-start.20 = (bf16[32,512]{1,0:T(8,128)(2,1)S(1)}, bf16[32,512]{1,0:T(8,128)(2,1)S(1)}, u32[]{:S(2)}, u32[]{:S(2)}) collective-permute-start(bf16[32,512]{1,0:T(8,128)(2,1)S(1)} %get-tuple-element.45), channel_id=1, source_target_pairs={{0,5},{1,4},{2,7},{3,6},{4,1},{5,0},{6,3},{7,2},{8,13},{9,12},{10,... | collective-permute-start | bytes 98312 | tf_op jit(solution)/shard_map/ppermute | solution.py:237
  50.3 5.5 %collective-permute-start.21 = (bf16[32,512]{1,0:T(8,128)(2,1)S(1)}, bf16[32,512]{1,0:T(8,128)(2,1)S(1)}, u32[]{:S(2)}, u32[]{:S(2)}) collective-permute-start(bf16[32,512]{1,0:T(8,128)(2,1)S(1)} %get-tuple-element.46), channel_id=1, source_target_pairs={{0,7},{1,6},{2,5},{3,4},{4,3},{5,2},{6,1},{7,0},{8,15},{9,14},{10,... | collective-permute-start | bytes 98312 | tf_op jit(solution)/shard_map/ppermute | solution.py:237
  56.1 3.8 %collective-permute-start.22 = (bf16[2,32,128]{2,1,0:T(8,128)(2,1)S(1)}, bf16[2,32,128]{2,1,0:T(8,128)(2,1)S(1)}, u32[]{:S(2)}, u32[]{:S(2)}) collective-permute-start(bf16[2,32,128]{2,1,0:T(8,128)(2,1)S(1)} %get-tuple-element.48), channel_id=1, source_target_pairs={{0,8},{8,0},{16,24},{24,16},{1,9},{9,1},{17,25},{25,17},{2,10},{10... | collective-permute-start | bytes 49160 | tf_op jit(solution)/shard_map/ppermute | solution.py:230
  56.7 3.7 %collective-permute-start.23 = (bf16[2,32,128]{2,1,0:T(8,128)(2,1)S(1)}, bf16[2,32,128]{2,1,0:T(8,128)(2,1)S(1)}, u32[]{:S(2)}, u32[]{:S(2)}) collective-permute-start(bf16[2,32,128]{2,1,0:T(8,128)(2,1)S(1)} %get-tuple-element.49), channel_id=1, source_target_pairs={{0,16},{8,24},{16,0},{24,8},{1,17},{9,25},{17,1},{25,9},{2,18},{10... | collective-permute-start | bytes 49160 | tf_op jit(solution)/shard_map/ppermute | solution.py:230
  57.7 4.6 %collective-permute-start.24 = (bf16[2,32,128]{2,1,0:T(8,128)(2,1)S(1)}, bf16[2,32,128]{2,1,0:T(8,128)(2,1)S(1)}, u32[]{:S(2)}, u32[]{:S(2)}) collective-permute-start(bf16[2,32,128]{2,1,0:T(8,128)(2,1)S(1)} %get-tuple-element.50), channel_id=1, source_target_pairs={{0,24},{8,16},{16,8},{24,0},{1,25},{9,17},{17,9},{25,1},{2,26},{10... | collective-permute-start | bytes 49160 | tf_op jit(solution)/shard_map/ppermute | solution.py:230

commit v5 on v4

--- a/solution.py
+++ b/solution.py
@@ -69,26 +69,26 @@
             messages[step][:, low : low + part] = turned_rest[level, at, :].astype(BF16)
 
 
-def slot_of(targets, source, turns, odd, half, level):
+def slot_of(targets, source, turns, odd, half, level, away):
     me_col = lax.axis_index("pcol")
     turn = turns[0] if turns[0] == turns[1] else jnp.where(odd == 1, turns[1], turns[0])
     column = targets[source, 0, lax.axis_index("prow") ^ turn] - level * 2 * half
     slot = (column >> 1) ^ (me_col >> 1)
-    wanted = (column >= 0) & (column < 2 * half) & (((column ^ me_col) & 1) == jnp.where(slot == 0, 0, 1))
+    wanted = (column >= 0) & (column < 2 * half) & (((column ^ me_col) & 1) == jnp.where(slot == 0, away, 1 - away))
     return wanted, slot
 
 
-def weights_kernel(half, level, turns, own_targets, far_targets, out):
+def weights_kernel(half, level, turns, away, own_targets, far_targets, out):
     parity = lax.axis_index("pcol") & 1
     for group, (targets, odd) in enumerate(((own_targets, parity), (far_targets, 1 - parity))):
         for at, turn in enumerate(turns):
-            wanted, slot = slot_of(targets, level, turn, odd, half, level)
+            wanted, slot = slot_of(targets, level, turn, odd, half, level, away)
             for step in range(half):
                 value = jnp.where(wanted & (slot == step), 1.0, 0.0).astype(F32)
                 out[group * len(turns) + at, step] = jnp.full(out.shape[2:], value, F32)
 
 
-def earlier_kernel(half, level, sources, own_targets, far_targets, *refs):
+def earlier_kernel(half, level, sources, away, own_targets, far_targets, *refs):
     own = refs[: len(sources)]
     far = refs[len(sources) : 2 * len(sources)]
     total = refs[-1]
@@ -104,7 +104,7 @@
 
     for targets, group, odd in ((own_targets, own, parity), (far_targets, far, 1 - parity)):
         for (source, turns, at), ref in zip(sources, group):
-            add(*slot_of(targets, source, turns, odd, half, level), at, ref)
+            add(*slot_of(targets, source, turns, odd, half, level, away), at, ref)
 
 
 def slots_kernel(half, places, weights, *refs):
@@ -244,6 +244,7 @@
         return lax.ppermute(x, "pcol", pairs(columns, 1))
 
     far_targets = flip(targets)
+    far_inverse = flip(inverse)
 
     def load(places, out_shapes, operands):
         return call(
@@ -292,7 +293,7 @@
     solved = []
     for level in range(1, levels):
         (weights,) = call(
-            functools.partial(weights_kernel, half, level - 1, tuple(turns)),
+            functools.partial(weights_kernel, half, level - 1, tuple(turns), int(level == later)),
             [shape((2 * rows, half, 8, 128), F32)],
             [targets, far_targets],
             scalars=2,
@@ -300,7 +301,7 @@
         before = []
         if past:
             before = call(
-                functools.partial(earlier_kernel, half, level - 1, tuple(x[0] for x in past)),
+                functools.partial(earlier_kernel, half, level - 1, tuple(x[0] for x in past), int(level == later)),
                 [shape((half, each, size), F32)],
                 [targets, far_targets, *(x[1] for x in past), *(x[2] for x in past)],
                 scalars=2,
@@ -326,7 +327,7 @@
                 [value, *blocks[level][count:]],
                 flops=2 * each * size * size * (rows - count),
             )
-            solved.append(value)
+            solved.append(flip(value))
             past += list(zip([(level - 1, turn, at) for turn, at in zip(turns, places)], own, far))
             own = [products] * count + [relayed] * (rows - count)
             far = [flip(products)] * count + [flip(relayed)] * (rows - count)
@@ -334,11 +335,11 @@
     pieces = call(
         functools.partial(last_kernel, rows, half, later, len(solved)),
         [shape((later, each, part), BF16)] * rows,
-        [*messages, *arrived, inverse, *solved],
+        [*far_messages, *arrived, far_inverse, *solved],
         scratch=[pltpu.VMEM((each, size), F32)],
         flops=2 * each * size * size,
     )
-    pieces = [over_rows(x, step) for step, x in enumerate(pieces)]
+    pieces = [to_partners(x, step) if step else flip(x) for step, x in enumerate(pieces)]
     (out,) = call(
         functools.partial(output_kernel, rows, later),
         [shape((levels, 1, part, vectors), BF16)],

time: 63.3 us -> 70.2 us (1.11)
  starting transfers between devices: 26.2 us -> 31.9 us
  waiting for transfers between devices: 29.2 us -> 30.4 us
    ppermute x3 -> x6, starting transfers between devices: 0.91 us -> 7.73 us  [to_partners(): return lax.ppermute(x, ('prow', 'pcol'), links)]
    ppermute x6 -> x3, starting transfers between devices: 7.04 us -> 2.72 us  [over_rows(): return lax.ppermute(x, 'prow', pairs(rows, step)) if step else x]
    ppermute x3 -> x6, waiting for transfers between devices: 3.35 us -> 7.21 us  [to_partners(): return lax.ppermute(x, ('prow', 'pcol'), links)]
    ppermute x6, starting transfers between devices: 7.9 us -> 10.5 us  [over_pairs(): return lax.ppermute(x, 'pcol', pairs(columns, 2 * step + 1)) if step else x]
    ppermute x6 -> x3, waiting for transfers between devices: 6.62 us -> 5.12 us  [over_rows(): return lax.ppermute(x, 'prow', pairs(rows, step)) if step else x]
    ppermute x6, waiting for transfers between devices: 7.67 us -> 6.73 us  [over_pairs(): return lax.ppermute(x, 'pcol', pairs(columns, 2 * step + 1)) if step else x]
    ppermute x3, starting transfers between devices: 6.11 us -> 6.97 us  [over_turns(): return lax.ppermute(x, ('prow', 'pcol'), links)]
    ppermute x7 -> x10, starting transfers between devices: 4.23 us -> 4.04 us  [flip(): return lax.ppermute(x, 'pcol', pairs(columns, 1))]
  transfers between devices with their start and end apart: 25 -> 28, of which waited for: 14 -> 14; matrix products, arithmetic and copies ran while one was open for 0% -> 0% of each run, Pallas kernels for 8% -> 9%
where the time goes in v5:
time: 70.2 us; the launch traced here: 70 us
  starting transfers between devices  31.9 us (45%)
  waiting for transfers between devices  30.4 us (43%)
  Pallas kernels  7.51 us (11%)
    ppermute x6, starting transfers between devices, over_pairs(): return lax.ppermute(x, 'pcol', pairs(columns, 2 * step + 1)) if step else x  10.5 us
    ppermute x3, waiting for transfers between devices, over_turns(): return lax.ppermute(x, ('prow', 'pcol'), links)  10 us
    ppermute x6, starting transfers between devices, to_partners(): return lax.ppermute(x, ('prow', 'pcol'), links)  7.73 us
    pallas_call x12, Pallas kernels, call(): pl.pallas_call(kernel, out_shape=out_shapes, in_specs=[smem] * scalars +...  7.51 us
    ppermute x6, waiting for transfers between devices, to_partners(): return lax.ppermute(x, ('prow', 'pcol'), links)  7.21 us
    ppermute x3, starting transfers between devices, over_turns(): return lax.ppermute(x, ('prow', 'pcol'), links)  6.97 us
    ppermute x6, waiting for transfers between devices, over_pairs(): return lax.ppermute(x, 'pcol', pairs(columns, 2 * step + 1)) if step else x  6.73 us
    ppermute x3, waiting for transfers between devices, over_rows(): return lax.ppermute(x, 'prow', pairs(rows, step)) if step else x  5.12 us
  transfers between devices with their start and end apart: 28, of which 14 were waited for; matrix products, arithmetic and copies ran while one was open for 0% of the time, Pallas kernels for 9%

profile of v5, /device:TPU:0, one launch (start us, length us, event | category | flops | bytes accessed | tf_op | source)
XLA Modules:
  0.0 70.0 jit_solution(2068474178315834418)
XLA Ops:
  0.0 0.5 collective-permute-start.22
  0.5 1.1 %shard_map.46 = (bf16[128,128]{1,0:T(8,128)(2,1)S(1)}, bf16[512,512]{1,0:T(8,128)(2,1)S(1)}) custom-call(bf16[3,1,128,128]{3,2,1,0:T(8,128)(2,1)} %refs_5_.1, bf16[2,1,1,512,512]{4,3,2,1,0:T(8,128)(2,1)} %refs_1_.3), custom_call_target="tpu_custom_call" | custom-call | bytes 1146880 | tf_op jit(solution)/shard_map/pallas_call | solution.py:25
  1.6 0.0 copy-start.1
  1.6 2.5 %collective-permute-start.14 = (bf16[512,512]{1,0:T(8,128)(2,1)S(1)}, bf16[512,512]{1,0:T(8,128)(2,1)S(1)}, u32[]{:S(2)}, u32[]{:S(2)}) collective-permute-start(bf16[512,512]{1,0:T(8,128)(2,1)S(1)} %get-tuple-element.40.refs_9_), channel_id=1, source_target_pairs={{0,8},{1,17},{2,10},{3,19},{4,12},{5,21},{6,14},{7,23},{8,0},{9,25... | collective-permute-start | bytes 1572872 | tf_op jit(solution)/shard_map/ppermute | solution.py:234
  4.1 1.5 %collective-permute-start.15 = (bf16[512,512]{1,0:T(8,128)(2,1)S(1)}, bf16[512,512]{1,0:T(8,128)(2,1)S(1)}, u32[]{:S(2)}, u32[]{:S(2)}) collective-permute-start(bf16[512,512]{1,0:T(8,128)(2,1)S(1)} %get-tuple-element.40.refs_9_), channel_id=1, source_target_pairs={{0,16},{1,9},{2,18},{3,11},{4,20},{5,13},{6,22},{7,15},{8,24},{9,1... | collective-permute-start | bytes 1572872 | tf_op jit(solution)/shard_map/ppermute | solution.py:234
  5.7 10.0 %collective-permute-done.14.refs_10_ = bf16[512,512]{1,0:T(8,128)(2,1)S(1)} collective-permute-done((bf16[512,512]{1,0:T(8,128)(2,1)S(1)}, bf16[512,512]{1,0:T(8,128)(2,1)S(1)}, u32[]{:S(2)}, u32[]{:S(2)}) %collective-permute-start.14) | collective-permute-done | bytes 524320 | tf_op jit(solution)/shard_map/ppermute | solution.py:234
  15.7 2.9 %collective-permute-start.16 = (bf16[512,512]{1,0:T(8,128)(2,1)S(1)}, bf16[512,512]{1,0:T(8,128)(2,1)S(1)}, u32[]{:S(2)}, u32[]{:S(2)}) collective-permute-start(bf16[512,512]{1,0:T(8,128)(2,1)S(1)} %collective-permute-done.14.refs_10_), channel_id=1, source_target_pairs={{0,16},{1,9},{2,18},{3,11},{4,20},{5,13},{6,22},{7,15},{8,24},{9,1... | collective-permute-start | bytes 1572872 | tf_op jit(solution)/shard_map/ppermute | solution.py:234
  18.6 1.6 %collective-permute-start = (bf16[128,128]{1,0:T(8,128)(2,1)S(1)}, bf16[128,128]{1,0:T(8,128)(2,1)S(1)}, u32[]{:S(2)}, u32[]{:S(2)}) collective-permute-start(bf16[128,128]{1,0:T(8,128)(2,1)S(1)} %get-tuple-element.28.refs_0_), channel_id=1, source_target_pairs={{0,8},{8,0},{16,24},{24,16},{1,9},{9,1},{17,25},{25,17},{2,10},{10... | collective-permute-start | bytes 98312 | tf_op jit(solution)/shard_map/ppermute | solution.py:230
  20.2 0.0 collective-permute-start.1
  20.2 2.6 %collective-permute-done.refs_1_ = bf16[128,128]{1,0:T(8,128)(2,1)S(1)} collective-permute-done((bf16[128,128]{1,0:T(8,128)(2,1)S(1)}, bf16[128,128]{1,0:T(8,128)(2,1)S(1)}, u32[]{:S(2)}, u32[]{:S(2)}) %collective-permute-start) | collective-permute-done | bytes 32800 | tf_op jit(solution)/shard_map/ppermute | solution.py:230
  22.8 1.1 %collective-permute-start.2 = (bf16[128,128]{1,0:T(8,128)(2,1)S(1)}, bf16[128,128]{1,0:T(8,128)(2,1)S(1)}, u32[]{:S(2)}, u32[]{:S(2)}) collective-permute-start(bf16[128,128]{1,0:T(8,128)(2,1)S(1)} %get-tuple-element.28.refs_0_), channel_id=1, source_target_pairs={{0,24},{8,16},{16,8},{24,0},{1,25},{9,17},{17,9},{25,1},{2,26},{10... | collective-permute-start | bytes 98312 | tf_op jit(solution)/shard_map/ppermute | solution.py:230
  23.9 1.2 %shard_map.47 = (bf16[512,512]{1,0:T(8,128)(2,1)S(1)}, bf16[512,512]{1,0:T(8,128)(2,1)S(1)}) custom-call(bf16[3,1,512,512]{3,2,1,0:T(8,128)(2,1)} %refs_8_.1, bf16[2,1,1,512,512]{4,3,2,1,0:T(8,128)(2,1)} %refs_1_.3), custom_call_target="tpu_custom_call" | custom-call | bytes 2621440 | tf_op jit(solution)/shard_map/pallas_call | solution.py:25
  25.1 0.0 copy-start
  25.2 1.3 %collective-permute-done.1.refs_2_ = bf16[128,128]{1,0:T(8,128)(2,1)S(1)} collective-permute-done((bf16[128,128]{1,0:T(8,128)(2,1)S(1)}, bf16[128,128]{1,0:T(8,128)(2,1)S(1)}, u32[]{:S(2)}, u32[]{:S(2)}) %collective-permute-start.1) | collective-permute-done | bytes 32800 | tf_op jit(solution)/shard_map/ppermute | solution.py:230
  26.4 1.2 %collective-permute-done.2.refs_3_ = bf16[128,128]{1,0:T(8,128)(2,1)S(1)} collective-permute-done((bf16[128,128]{1,0:T(8,128)(2,1)S(1)}, bf16[128,128]{1,0:T(8,128)(2,1)S(1)}, u32[]{:S(2)}, u32[]{:S(2)}) %collective-permute-start.2) | collective-permute-done | bytes 32800 | tf_op jit(solution)/shard_map/ppermute | solution.py:230
  27.7 0.8 %shard_map.48 = (bf16[128,128]{1,0:T(8,128)(2,1)S(1)}, bf16[32,768]{1,0:T(8,128)(2,1)S(1)}, bf16[32,768]{1,0:T(8,128)(2,1)S(1)}, bf16[32,768]{1,0:T(8,128)(2,1)S(1)}, bf16[32,768]{1,0:T(8,128)(2,1)S(1)}) custom-call(bf16[128,128]{1,0:T(8,128)(2,1)S(1)} %get-tuple-element.28.refs_0_, bf16[128,128]{1,0:T(8,128)(2,1)S(1)} %collective-permute-done.refs_1_, ...), custom_call_target="tpu_custom_call" | custom-call | flops 134217728 | bytes 1277952 | tf_op jit(solution)/shard_map/pallas_call | solution.py:25
  28.5 1.4 %collective-permute-start.3 = (bf16[32,768]{1,0:T(8,128)(2,1)S(1)}, bf16[32,768]{1,0:T(8,128)(2,1)S(1)}, u32[]{:S(2)}, u32[]{:S(2)}) collective-permute-start(bf16[32,768]{1,0:T(8,128)(2,1)S(1)} %get-tuple-element.32.refs_0_), channel_id=1, source_target_pairs={{0,1},{1,0},{2,3},{3,2},{4,5},{5,4},{6,7},{7,6},{8,9},{9,8},{10,11... | collective-permute-start | bytes 147464 | tf_op jit(solution)/shard_map/ppermute | solution.py:244
  29.9 0.1 collective-permute-start.7
  30.0 1.1 %collective-permute-done.7.far_targets = s32[2,1,4]{2,1,0:T(1,128)S(1)} collective-permute-done((s32[2,1,4]{2,1,0:T(1,128)S(1)}, s32[2,1,4]{2,1,0:T(1,128)S(1)}, u32[]{:S(2)}, u32[]{:S(2)}) %collective-permute-start.7) | collective-permute-done | bytes 64 | tf_op jit(solution)/shard_map/ppermute | solution.py:244
  31.1 1.5 %collective-permute-start.4 = (bf16[32,768]{1,0:T(8,128)(2,1)S(1)}, bf16[32,768]{1,0:T(8,128)(2,1)S(1)}, u32[]{:S(2)}, u32[]{:S(2)}) collective-permute-start(bf16[32,768]{1,0:T(8,128)(2,1)S(1)} %get-tuple-element.33), channel_id=1, source_target_pairs={{0,9},{1,8},{2,11},{3,10},{4,13},{5,12},{6,15},{7,14},{8,1},{9,0},... | collective-permute-start | bytes 147464 | tf_op jit(solution)/shard_map/ppermute | solution.py:241
  32.6 0.0 collective-permute-done.3.refs_4_.refs_0_
  32.6 1.0 %collective-permute-start.5 = (bf16[32,768]{1,0:T(8,128)(2,1)S(1)}, bf16[32,768]{1,0:T(8,128)(2,1)S(1)}, u32[]{:S(2)}, u32[]{:S(2)}) collective-permute-start(bf16[32,768]{1,0:T(8,128)(2,1)S(1)} %get-tuple-element.34), channel_id=1, source_target_pairs={{0,17},{1,16},{2,19},{3,18},{4,21},{5,20},{6,23},{7,22},{8,25},{9,... | collective-permute-start | bytes 147464 | tf_op jit(solution)/shard_map/ppermute | solution.py:241
  33.6 1.1 %collective-permute-done.4.refs_5_.refs_1_ = bf16[32,768]{1,0:T(8,128)(2,1)S(1)} collective-permute-done((bf16[32,768]{1,0:T(8,128)(2,1)S(1)}, bf16[32,768]{1,0:T(8,128)(2,1)S(1)}, u32[]{:S(2)}, u32[]{:S(2)}) %collective-permute-start.4) | collective-permute-done | bytes 49184 | tf_op jit(solution)/shard_map/ppermute | solution.py:241
  34.8 2.0 %collective-permute-start.6 = (bf16[32,768]{1,0:T(8,128)(2,1)S(1)}, bf16[32,768]{1,0:T(8,128)(2,1)S(1)}, u32[]{:S(2)}, u32[]{:S(2)}) collective-permute-start(bf16[32,768]{1,0:T(8,128)(2,1)S(1)} %get-tuple-element.35), channel_id=1, source_target_pairs={{0,25},{1,24},{2,27},{3,26},{4,29},{5,28},{6,31},{7,30},{8,17},{9,... | collective-permute-start | bytes 147464 | tf_op jit(solution)/shard_map/ppermute | solution.py:241
  36.8 0.3 collective-permute-start.8
  37.2 2.2 %collective-permute-done.6.refs_7_.refs_3_ = bf16[32,768]{1,0:T(8,128)(2,1)S(1)} collective-permute-done((bf16[32,768]{1,0:T(8,128)(2,1)S(1)}, bf16[32,768]{1,0:T(8,128)(2,1)S(1)}, u32[]{:S(2)}, u32[]{:S(2)}) %collective-permute-start.6) | collective-permute-done | bytes 49184 | tf_op jit(solution)/shard_map/ppermute | solution.py:241
  39.4 0.2 collective-permute-start.9
  39.5 0.0 collective-permute-done.8.refs_1_
  39.5 0.3 collective-permute-start.10
  39.9 0.6 shard_map.50.weights
  40.5 0.1 collective-permute-done.9.refs_2_
  40.6 0.2 collective-permute-done.10.refs_3_
  40.8 0.2 shard_map.51
  40.9 1.2 %collective-permute-start.11 = (bf16[32,512]{1,0:T(8,128)(2,1)S(1)}, bf16[32,512]{1,0:T(8,128)(2,1)S(1)}, u32[]{:S(2)}, u32[]{:S(2)}) collective-permute-start(bf16[32,512]{1,0:T(8,128)(2,1)S(1)} %get-tuple-element.37), channel_id=1, source_target_pairs={{0,3},{1,2},{2,1},{3,0},{4,7},{5,6},{6,5},{7,4},{8,11},{9,10},{10,... | collective-permute-start | bytes 98312 | tf_op jit(solution)/shard_map/ppermute | solution.py:237
  42.1 2.4 %collective-permute-start.12 = (bf16[32,512]{1,0:T(8,128)(2,1)S(1)}, bf16[32,512]{1,0:T(8,128)(2,1)S(1)}, u32[]{:S(2)}, u32[]{:S(2)}) collective-permute-start(bf16[32,512]{1,0:T(8,128)(2,1)S(1)} %get-tuple-element.38), channel_id=1, source_target_pairs={{0,5},{1,4},{2,7},{3,6},{4,1},{5,0},{6,3},{7,2},{8,13},{9,12},{10,... | collective-permute-start | bytes 98312 | tf_op jit(solution)/shard_map/ppermute | solution.py:237
  44.5 3.0 %collective-permute-start.13 = (bf16[32,512]{1,0:T(8,128)(2,1)S(1)}, bf16[32,512]{1,0:T(8,128)(2,1)S(1)}, u32[]{:S(2)}, u32[]{:S(2)}) collective-permute-start(bf16[32,512]{1,0:T(8,128)(2,1)S(1)} %get-tuple-element.39), channel_id=1, source_target_pairs={{0,7},{1,6},{2,5},{3,4},{4,3},{5,2},{6,1},{7,0},{8,15},{9,14},{10,... | collective-permute-start | bytes 98312 | tf_op jit(solution)/shard_map/ppermute | solution.py:237
  47.5 2.1 %collective-permute-done.13.refs_7_ = bf16[32,512]{1,0:T(8,128)(2,1)S(1)} collective-permute-done((bf16[32,512]{1,0:T(8,128)(2,1)S(1)}, bf16[32,512]{1,0:T(8,128)(2,1)S(1)}, u32[]{:S(2)}, u32[]{:S(2)}) %collective-permute-start.13) | collective-permute-done | bytes 32800 | tf_op jit(solution)/shard_map/ppermute | solution.py:237
  49.6 0.0 collective-permute-done.15.refs_11_
  49.6 0.8 %shard_map.52 = (bf16[32,512]{1,0:T(8,128)(2,1)S(1)}, bf16[3,32,512]{2,1,0:T(8,128)(2,1)S(1)}) custom-call(bf16[32,768]{1,0:T(8,128)(2,1)S(1)} %get-tuple-element.32.refs_0_, bf16[32,768]{1,0:T(8,128)(2,1)S(1)} %collective-permute-done.8.refs_1_, bf16[32,768]{1,0:T(8,128)(2,1)S(1)} %collective-permute-done.9.refs_2_, ...), custom_call_target="tpu_custom_call" | custom-call | flops 67108864 | bytes 3473408 | tf_op jit(solution)/shard_map/pallas_call | solution.py:25
  50.4 0.4 collective-permute-start.17
  50.8 0.2 shard_map.53.refs_3_
  51.0 0.2 collective-permute-start.18
  51.2 0.7 shard_map.49.weights
  51.9 0.7 shard_map.54.refs_8_
  52.5 0.4 collective-permute-start.23
  53.0 0.0 collective-permute-done.17.refs_4_.refs_5_.refs_6_
  53.0 0.0 collective-permute-done.18.refs_7_
  53.0 0.2 shard_map.55
  53.1 0.1 collective-permute-start.19
  53.2 3.3 %collective-permute-start.20 = (bf16[32,512]{1,0:T(8,128)(2,1)S(1)}, bf16[32,512]{1,0:T(8,128)(2,1)S(1)}, u32[]{:S(2)}, u32[]{:S(2)}) collective-permute-start(bf16[32,512]{1,0:T(8,128)(2,1)S(1)} %get-tuple-element.45), channel_id=1, source_target_pairs={{0,5},{1,4},{2,7},{3,6},{4,1},{5,0},{6,3},{7,2},{8,13},{9,12},{10,... | collective-permute-start | bytes 98312 | tf_op jit(solution)/shard_map/ppermute | solution.py:237
  56.5 0.5 collective-permute-start.21
  57.1 0.0 collective-permute-done.23.refs_9_
  57.1 0.0 collective-permute-done.19.refs_5_
  57.1 1.0 %collective-permute-done.20.refs_6_ = bf16[32,512]{1,0:T(8,128)(2,1)S(1)} collective-permute-done((bf16[32,512]{1,0:T(8,128)(2,1)S(1)}, bf16[32,512]{1,0:T(8,128)(2,1)S(1)}, u32[]{:S(2)}, u32[]{:S(2)}) %collective-permute-start.20) | collective-permute-done | bytes 32800 | tf_op jit(solution)/shard_map/ppermute | solution.py:237
  58.1 3.5 %collective-permute-done.21.refs_7_ = bf16[32,512]{1,0:T(8,128)(2,1)S(1)} collective-permute-done((bf16[32,512]{1,0:T(8,128)(2,1)S(1)}, bf16[32,512]{1,0:T(8,128)(2,1)S(1)}, u32[]{:S(2)}, u32[]{:S(2)}) %collective-permute-start.21) | collective-permute-done | bytes 32800 | tf_op jit(solution)/shard_map/ppermute | solution.py:237
  61.7 0.3 shard_map.56
  62.0 0.2 collective-permute-start.24
  62.2 1.6 %collective-permute-start.25 = (bf16[2,32,128]{2,1,0:T(8,128)(2,1)S(1)}, bf16[2,32,128]{2,1,0:T(8,128)(2,1)S(1)}, u32[]{:S(2)}, u32[]{:S(2)}) collective-permute-start(bf16[2,32,128]{2,1,0:T(8,128)(2,1)S(1)} %get-tuple-element.48), channel_id=1, source_target_pairs={{0,9},{1,8},{2,11},{3,10},{4,13},{5,12},{6,15},{7,14},{8,1},{9,0},... | collective-permute-start | bytes 49160 | tf_op jit(solution)/shard_map/ppermute | solution.py:241
  63.9 1.3 %collective-permute-start.26 = (bf16[2,32,128]{2,1,0:T(8,128)(2,1)S(1)}, bf16[2,32,128]{2,1,0:T(8,128)(2,1)S(1)}, u32[]{:S(2)}, u32[]{:S(2)}) collective-permute-start(bf16[2,32,128]{2,1,0:T(8,128)(2,1)S(1)} %get-tuple-element.49), channel_id=1, source_target_pairs={{0,17},{1,16},{2,19},{3,18},{4,21},{5,20},{6,23},{7,22},{8,25},{9,... | collective-permute-start | bytes 49160 | tf_op jit(solution)/shard_map/ppermute | solution.py:241
  65.2 0.2 collective-permute-start.27
  65.4 0.0 collective-permute-done.25.refs_2_
  65.4 1.6 %collective-permute-done.26.refs_3_ = bf16[2,32,128]{2,1,0:T(8,128)(2,1)S(1)} collective-permute-done((bf16[2,32,128]{2,1,0:T(8,128)(2,1)S(1)}, bf16[2,32,128]{2,1,0:T(8,128)(2,1)S(1)}, u32[]{:S(2)}, u32[]{:S(2)}) %collective-permute-start.26) | collective-permute-done | bytes 16416 | tf_op jit(solution)/shard_map/ppermute | solution.py:241
  67.0 2.2 %collective-permute-done.27.refs_4_ = bf16[2,32,128]{2,1,0:T(8,128)(2,1)S(1)} collective-permute-done((bf16[2,32,128]{2,1,0:T(8,128)(2,1)S(1)}, bf16[2,32,128]{2,1,0:T(8,128)(2,1)S(1)}, u32[]{:S(2)}, u32[]{:S(2)}) %collective-permute-start.27) | collective-permute-done | bytes 16416 | tf_op jit(solution)/shard_map/ppermute | solution.py:241
  69.2 0.8 %shard_map.57 = bf16[3,1,128,128]{3,2,1,0:T(8,128)(2,1)} custom-call(bf16[128,128]{1,0:T(8,128)(2,1)S(1)} %get-tuple-element.31.refs_0_, bf16[2,32,128]{2,1,0:T(8,128)(2,1)S(1)} %collective-permute-done.24.refs_1_, bf16[2,32,128]{2,1,0:T(8,128)(2,1)S(1)} %collective-permute-done.25.refs_2_, bf16[2,32,128]{2,1,0:T(8,128)(2,1)S(1)} %collective-permute-done.26.refs_3_, ...), custom_call_target="tpu_custom_call" | custom-call | bytes 98304 | tf_op jit(solution)/shard_map/pallas_call | solution.py:25
  (10 shorter events, 0.0 us)
Async XLA Ops:
  0.0 61.7 %collective-permute-start.22 = (bf16[3,1,512,512]{3,2,1,0:T(8,128)(2,1)}, bf16[3,1,512,512]{3,2,1,0:T(8,128)(2,1)S(1)}, u32[]{:S(2)}, u32[]{:S(2)}) collective-permute-start(bf16[3,1,512,512]{3,2,1,0:T(8,128)(2,1)} %refs_8_.1), channel_id=1, source_target_pairs={{0,1},{1,0},{2,3},{3,2},{4,5},{5,4},{6,7},{7,6},{8,9},{9,8},{10,11... | collective-permute-start | bytes 4718600 | tf_op jit(solution)/shard_map/ppermute | solution.py:244
  1.6 26.1 %copy-start.1 = (bf16[3,1,128,128]{3,2,1,0:T(8,128)(2,1)S(1)}, bf16[3,1,128,128]{3,2,1,0:T(8,128)(2,1)}, u32[]{:S(2)}) copy-start(bf16[3,1,128,128]{3,2,1,0:T(8,128)(2,1)} %refs_5_.1) | copy-start | bytes 294916
  1.6 14.1 %collective-permute-start.14 = (bf16[512,512]{1,0:T(8,128)(2,1)S(1)}, bf16[512,512]{1,0:T(8,128)(2,1)S(1)}, u32[]{:S(2)}, u32[]{:S(2)}) collective-permute-start(bf16[512,512]{1,0:T(8,128)(2,1)S(1)} %get-tuple-element.40.refs_9_), channel_id=1, source_target_pairs={{0,8},{1,17},{2,10},{3,19},{4,12},{5,21},{6,14},{7,23},{8,0},{9,25... | collective-permute-start | bytes 1572872 | tf_op jit(solution)/shard_map/ppermute | solution.py:234
  4.1 45.5 %collective-permute-start.15 = (bf16[512,512]{1,0:T(8,128)(2,1)S(1)}, bf16[512,512]{1,0:T(8,128)(2,1)S(1)}, u32[]{:S(2)}, u32[]{:S(2)}) collective-permute-start(bf16[512,512]{1,0:T(8,128)(2,1)S(1)} %get-tuple-element.40.refs_9_), channel_id=1, source_target_pairs={{0,16},{1,9},{2,18},{3,11},{4,20},{5,13},{6,22},{7,15},{8,24},{9,1... | collective-permute-start | bytes 1572872 | tf_op jit(solution)/shard_map/ppermute | solution.py:234
  15.7 35.1 %collective-permute-start.16 = (bf16[512,512]{1,0:T(8,128)(2,1)S(1)}, bf16[512,512]{1,0:T(8,128)(2,1)S(1)}, u32[]{:S(2)}, u32[]{:S(2)}) collective-permute-start(bf16[512,512]{1,0:T(8,128)(2,1)S(1)} %collective-permute-done.14.refs_10_), channel_id=1, source_target_pairs={{0,16},{1,9},{2,18},{3,11},{4,20},{5,13},{6,22},{7,15},{8,24},{9,1... | collective-permute-start | bytes 1572872 | tf_op jit(solution)/shard_map/ppermute | solution.py:234
  18.6 11.3 %copy-start.2 = (s32[2,1,4]{2,1,0:T(1,128)S(1)}, s32[2,1,4]{2,1,0:T(1,128)}, u32[]{:S(2)}) copy-start(s32[2,1,4]{2,1,0:T(1,128)} %own_targets.5) | copy-start | bytes 100
  18.6 4.3 %collective-permute-start = (bf16[128,128]{1,0:T(8,128)(2,1)S(1)}, bf16[128,128]{1,0:T(8,128)(2,1)S(1)}, u32[]{:S(2)}, u32[]{:S(2)}) collective-permute-start(bf16[128,128]{1,0:T(8,128)(2,1)S(1)} %get-tuple-element.28.refs_0_), channel_id=1, source_target_pairs={{0,8},{8,0},{16,24},{24,16},{1,9},{9,1},{17,25},{25,17},{2,10},{10... | collective-permute-start | bytes 98312 | tf_op jit(solution)/shard_map/ppermute | solution.py:230
  20.2 6.2 %collective-permute-start.1 = (bf16[128,128]{1,0:T(8,128)(2,1)S(1)}, bf16[128,128]{1,0:T(8,128)(2,1)S(1)}, u32[]{:S(2)}, u32[]{:S(2)}) collective-permute-start(bf16[128,128]{1,0:T(8,128)(2,1)S(1)} %get-tuple-element.28.refs_0_), channel_id=1, source_target_pairs={{0,16},{8,24},{16,0},{24,8},{1,17},{9,25},{17,1},{25,9},{2,18},{10... | collective-permute-start | bytes 98312 | tf_op jit(solution)/shard_map/ppermute | solution.py:230
  22.8 4.8 %collective-permute-start.2 = (bf16[128,128]{1,0:T(8,128)(2,1)S(1)}, bf16[128,128]{1,0:T(8,128)(2,1)S(1)}, u32[]{:S(2)}, u32[]{:S(2)}) collective-permute-start(bf16[128,128]{1,0:T(8,128)(2,1)S(1)} %get-tuple-element.28.refs_0_), channel_id=1, source_target_pairs={{0,24},{8,16},{16,8},{24,0},{1,25},{9,17},{17,9},{25,1},{2,26},{10... | collective-permute-start | bytes 98312 | tf_op jit(solution)/shard_map/ppermute | solution.py:230
  25.1 24.5 %copy-start = (bf16[3,1,512,512]{3,2,1,0:T(8,128)(2,1)S(1)}, bf16[3,1,512,512]{3,2,1,0:T(8,128)(2,1)}, u32[]{:S(2)}) copy-start(bf16[3,1,512,512]{3,2,1,0:T(8,128)(2,1)} %refs_8_.1) | copy-start | bytes 4718596
  28.5 4.1 %collective-permute-start.3 = (bf16[32,768]{1,0:T(8,128)(2,1)S(1)}, bf16[32,768]{1,0:T(8,128)(2,1)S(1)}, u32[]{:S(2)}, u32[]{:S(2)}) collective-permute-start(bf16[32,768]{1,0:T(8,128)(2,1)S(1)} %get-tuple-element.32.refs_0_), channel_id=1, source_target_pairs={{0,1},{1,0},{2,3},{3,2},{4,5},{5,4},{6,7},{7,6},{8,9},{9,8},{10,11... | collective-permute-start | bytes 147464 | tf_op jit(solution)/shard_map/ppermute | solution.py:244
  29.9 1.2 %collective-permute-start.7 = (s32[2,1,4]{2,1,0:T(1,128)S(1)}, s32[2,1,4]{2,1,0:T(1,128)S(1)}, u32[]{:S(2)}, u32[]{:S(2)}) collective-permute-start(s32[2,1,4]{2,1,0:T(1,128)S(1)} %copy-done.2), channel_id=1, source_target_pairs={{0,1},{1,0},{2,3},{3,2},{4,5},{5,4},{6,7},{7,6},{8,9},{9,8},{10,11... | collective-permute-start | bytes 104 | tf_op jit(solution)/shard_map/ppermute | solution.py:244
  31.1 3.7 %collective-permute-start.4 = (bf16[32,768]{1,0:T(8,128)(2,1)S(1)}, bf16[32,768]{1,0:T(8,128)(2,1)S(1)}, u32[]{:S(2)}, u32[]{:S(2)}) collective-permute-start(bf16[32,768]{1,0:T(8,128)(2,1)S(1)} %get-tuple-element.33), channel_id=1, source_target_pairs={{0,9},{1,8},{2,11},{3,10},{4,13},{5,12},{6,15},{7,14},{8,1},{9,0},... | collective-permute-start | bytes 147464 | tf_op jit(solution)/shard_map/ppermute | solution.py:241
  32.6 4.2 %collective-permute-start.5 = (bf16[32,768]{1,0:T(8,128)(2,1)S(1)}, bf16[32,768]{1,0:T(8,128)(2,1)S(1)}, u32[]{:S(2)}, u32[]{:S(2)}) collective-permute-start(bf16[32,768]{1,0:T(8,128)(2,1)S(1)} %get-tuple-element.34), channel_id=1, source_target_pairs={{0,17},{1,16},{2,19},{3,18},{4,21},{5,20},{6,23},{7,22},{8,25},{9,... | collective-permute-start | bytes 147464 | tf_op jit(solution)/shard_map/ppermute | solution.py:241
  34.8 4.6 %collective-permute-start.6 = (bf16[32,768]{1,0:T(8,128)(2,1)S(1)}, bf16[32,768]{1,0:T(8,128)(2,1)S(1)}, u32[]{:S(2)}, u32[]{:S(2)}) collective-permute-start(bf16[32,768]{1,0:T(8,128)(2,1)S(1)} %get-tuple-element.35), channel_id=1, source_target_pairs={{0,25},{1,24},{2,27},{3,26},{4,29},{5,28},{6,31},{7,30},{8,17},{9,... | collective-permute-start | bytes 147464 | tf_op jit(solution)/shard_map/ppermute | solution.py:241
  36.8 2.7 %collective-permute-start.8 = (bf16[32,768]{1,0:T(8,128)(2,1)S(1)}, bf16[32,768]{1,0:T(8,128)(2,1)S(1)}, u32[]{:S(2)}, u32[]{:S(2)}) collective-permute-start(bf16[32,768]{1,0:T(8,128)(2,1)S(1)} %collective-permute-done.4.refs_5_.refs_1_), channel_id=1, source_target_pairs={{0,1},{1,0},{2,3},{3,2},{4,5},{5,4},{6,7},{7,6},{8,9},{9,8},{10,11... | collective-permute-start | bytes 147464 | tf_op jit(solution)/shard_map/ppermute | solution.py:244
  39.4 1.2 %collective-permute-start.9 = (bf16[32,768]{1,0:T(8,128)(2,1)S(1)}, bf16[32,768]{1,0:T(8,128)(2,1)S(1)}, u32[]{:S(2)}, u32[]{:S(2)}) collective-permute-start(bf16[32,768]{1,0:T(8,128)(2,1)S(1)} %collective-permute-done.5.refs_6_.refs_2_), channel_id=1, source_target_pairs={{0,1},{1,0},{2,3},{3,2},{4,5},{5,4},{6,7},{7,6},{8,9},{9,8},{10,11... | collective-permute-start | bytes 147464 | tf_op jit(solution)/shard_map/ppermute | solution.py:244
  39.5 1.2 %collective-permute-start.10 = (bf16[32,768]{1,0:T(8,128)(2,1)S(1)}, bf16[32,768]{1,0:T(8,128)(2,1)S(1)}, u32[]{:S(2)}, u32[]{:S(2)}) collective-permute-start(bf16[32,768]{1,0:T(8,128)(2,1)S(1)} %collective-permute-done.6.refs_7_.refs_3_), channel_id=1, source_target_pairs={{0,1},{1,0},{2,3},{3,2},{4,5},{5,4},{6,7},{7,6},{8,9},{9,8},{10,11... | collective-permute-start | bytes 147464 | tf_op jit(solution)/shard_map/ppermute | solution.py:244
  40.9 3.6 %collective-permute-start.11 = (bf16[32,512]{1,0:T(8,128)(2,1)S(1)}, bf16[32,512]{1,0:T(8,128)(2,1)S(1)}, u32[]{:S(2)}, u32[]{:S(2)}) collective-permute-start(bf16[32,512]{1,0:T(8,128)(2,1)S(1)} %get-tuple-element.37), channel_id=1, source_target_pairs={{0,3},{1,2},{2,1},{3,0},{4,7},{5,6},{6,5},{7,4},{8,11},{9,10},{10,... | collective-permute-start | bytes 98312 | tf_op jit(solution)/shard_map/ppermute | solution.py:237
  42.1 5.4 %collective-permute-start.12 = (bf16[32,512]{1,0:T(8,128)(2,1)S(1)}, bf16[32,512]{1,0:T(8,128)(2,1)S(1)}, u32[]{:S(2)}, u32[]{:S(2)}) collective-permute-start(bf16[32,512]{1,0:T(8,128)(2,1)S(1)} %get-tuple-element.38), channel_id=1, source_target_pairs={{0,5},{1,4},{2,7},{3,6},{4,1},{5,0},{6,3},{7,2},{8,13},{9,12},{10,... | collective-permute-start | bytes 98312 | tf_op jit(solution)/shard_map/ppermute | solution.py:237
  44.5 5.1 %collective-permute-start.13 = (bf16[32,512]{1,0:T(8,128)(2,1)S(1)}, bf16[32,512]{1,0:T(8,128)(2,1)S(1)}, u32[]{:S(2)}, u32[]{:S(2)}) collective-permute-start(bf16[32,512]{1,0:T(8,128)(2,1)S(1)} %get-tuple-element.39), channel_id=1, source_target_pairs={{0,7},{1,6},{2,5},{3,4},{4,3},{5,2},{6,1},{7,0},{8,15},{9,14},{10,... | collective-permute-start | bytes 98312 | tf_op jit(solution)/shard_map/ppermute | solution.py:237
  50.4 2.6 %collective-permute-start.17 = (bf16[3,32,512]{2,1,0:T(8,128)(2,1)S(1)}, bf16[3,32,512]{2,1,0:T(8,128)(2,1)S(1)}, u32[]{:S(2)}, u32[]{:S(2)}) collective-permute-start(bf16[3,32,512]{2,1,0:T(8,128)(2,1)S(1)} %get-tuple-element.41.refs_0_.refs_1_.refs_2_), channel_id=1, source_target_pairs={{0,1},{1,0},{2,3},{3,2},{4,5},{5,4},{6,7},{7,6},{8,9},{9,8},{10,11... | collective-permute-start | bytes 294920 | tf_op jit(solution)/shard_map/ppermute | solution.py:244
  51.0 2.0 %collective-permute-start.18 = (bf16[1,32,512]{2,1,0:T(8,128)(2,1)S(1)}, bf16[1,32,512]{2,1,0:T(8,128)(2,1)S(1)}, u32[]{:S(2)}, u32[]{:S(2)}) collective-permute-start(bf16[1,32,512]{2,1,0:T(8,128)(2,1)S(1)} %shard_map.53.refs_3_), channel_id=1, source_target_pairs={{0,1},{1,0},{2,3},{3,2},{4,5},{5,4},{6,7},{7,6},{8,9},{9,8},{10,11... | collective-permute-start | bytes 98312 | tf_op jit(solution)/shard_map/ppermute | solution.py:244
  52.5 4.5 %collective-permute-start.23 = (bf16[32,512]{1,0:T(8,128)(2,1)S(1)}, bf16[32,512]{1,0:T(8,128)(2,1)S(1)}, u32[]{:S(2)}, u32[]{:S(2)}) collective-permute-start(bf16[32,512]{1,0:T(8,128)(2,1)S(1)} %get-tuple-element.42.solved), channel_id=1, source_target_pairs={{0,1},{1,0},{2,3},{3,2},{4,5},{5,4},{6,7},{7,6},{8,9},{9,8},{10,11... | collective-permute-start | bytes 98312 | tf_op jit(solution)/shard_map/ppermute | solution.py:244
  53.1 4.0 %collective-permute-start.19 = (bf16[32,512]{1,0:T(8,128)(2,1)S(1)}, bf16[32,512]{1,0:T(8,128)(2,1)S(1)}, u32[]{:S(2)}, u32[]{:S(2)}) collective-permute-start(bf16[32,512]{1,0:T(8,128)(2,1)S(1)} %get-tuple-element.44), channel_id=1, source_target_pairs={{0,3},{1,2},{2,1},{3,0},{4,7},{5,6},{6,5},{7,4},{8,11},{9,10},{10,... | collective-permute-start | bytes 98312 | tf_op jit(solution)/shard_map/ppermute | solution.py:237
  53.2 4.9 %collective-permute-start.20 = (bf16[32,512]{1,0:T(8,128)(2,1)S(1)}, bf16[32,512]{1,0:T(8,128)(2,1)S(1)}, u32[]{:S(2)}, u32[]{:S(2)}) collective-permute-start(bf16[32,512]{1,0:T(8,128)(2,1)S(1)} %get-tuple-element.45), channel_id=1, source_target_pairs={{0,5},{1,4},{2,7},{3,6},{4,1},{5,0},{6,3},{7,2},{8,13},{9,12},{10,... | collective-permute-start | bytes 98312 | tf_op jit(solution)/shard_map/ppermute | solution.py:237
  56.5 5.1 %collective-permute-start.21 = (bf16[32,512]{1,0:T(8,128)(2,1)S(1)}, bf16[32,512]{1,0:T(8,128)(2,1)S(1)}, u32[]{:S(2)}, u32[]{:S(2)}) collective-permute-start(bf16[32,512]{1,0:T(8,128)(2,1)S(1)} %get-tuple-element.46), channel_id=1, source_target_pairs={{0,7},{1,6},{2,5},{3,4},{4,3},{5,2},{6,1},{7,0},{8,15},{9,14},{10,... | collective-permute-start | bytes 98312 | tf_op jit(solution)/shard_map/ppermute | solution.py:237
  62.0 3.4 %collective-permute-start.24 = (bf16[2,32,128]{2,1,0:T(8,128)(2,1)S(1)}, bf16[2,32,128]{2,1,0:T(8,128)(2,1)S(1)}, u32[]{:S(2)}, u32[]{:S(2)}) collective-permute-start(bf16[2,32,128]{2,1,0:T(8,128)(2,1)S(1)} %get-tuple-element.47), channel_id=1, source_target_pairs={{0,1},{1,0},{2,3},{3,2},{4,5},{5,4},{6,7},{7,6},{8,9},{9,8},{10,11... | collective-permute-start | bytes 49160 | tf_op jit(solution)/shard_map/ppermute | solution.py:244
  62.2 3.2 %collective-permute-start.25 = (bf16[2,32,128]{2,1,0:T(8,128)(2,1)S(1)}, bf16[2,32,128]{2,1,0:T(8,128)(2,1)S(1)}, u32[]{:S(2)}, u32[]{:S(2)}) collective-permute-start(bf16[2,32,128]{2,1,0:T(8,128)(2,1)S(1)} %get-tuple-element.48), channel_id=1, source_target_pairs={{0,9},{1,8},{2,11},{3,10},{4,13},{5,12},{6,15},{7,14},{8,1},{9,0},... | collective-permute-start | bytes 49160 | tf_op jit(solution)/shard_map/ppermute | solution.py:241
  63.9 3.2 %collective-permute-start.26 = (bf16[2,32,128]{2,1,0:T(8,128)(2,1)S(1)}, bf16[2,32,128]{2,1,0:T(8,128)(2,1)S(1)}, u32[]{:S(2)}, u32[]{:S(2)}) collective-permute-start(bf16[2,32,128]{2,1,0:T(8,128)(2,1)S(1)} %get-tuple-element.49), channel_id=1, source_target_pairs={{0,17},{1,16},{2,19},{3,18},{4,21},{5,20},{6,23},{7,22},{8,25},{9,... | collective-permute-start | bytes 49160 | tf_op jit(solution)/shard_map/ppermute | solution.py:241
  65.2 4.1 %collective-permute-start.27 = (bf16[2,32,128]{2,1,0:T(8,128)(2,1)S(1)}, bf16[2,32,128]{2,1,0:T(8,128)(2,1)S(1)}, u32[]{:S(2)}, u32[]{:S(2)}) collective-permute-start(bf16[2,32,128]{2,1,0:T(8,128)(2,1)S(1)} %get-tuple-element.50), channel_id=1, source_target_pairs={{0,25},{1,24},{2,27},{3,26},{4,29},{5,28},{6,31},{7,30},{8,17},{9,... | collective-permute-start | bytes 49160 | tf_op jit(solution)/shard_map/ppermute | solution.py:241
